TPU v7x, 32 devices: a whole 2x2x4 slice. The times are simulated.
32 devices in a mesh: dp: 8 (over z, x), tensor: 4 (over y, core).
Axes of the slice: x: 2, y: 2, z: 4, core: 2. Of those that a mesh axis runs over, the one named last changes fastest.
Arguments:
- segments: bfloat16 [32, 704, 512], P('dp'), may hold values from -6 to 6
- seg_start: int32 [32, 704], P('dp'), may hold values from 0 to 2048, as said below
- seg_count: int32 [32], P('dp'), may hold values from 300 to 704, as said below
- norm_gain: bfloat16 [512], P('dp'), may hold values from 0.25 to 1.75
- norm_shift: bfloat16 [512], P('dp'), may hold values from -3 to 3
- qkv_weight: bfloat16 [512, 3, 512], P('dp', None, 'tensor'), may hold values from -0.25 to 0.25
- out_weight: bfloat16 [512, 512], P(('tensor', 'dp')), may hold values from -1 to 1
- ffn_gain: bfloat16 [512], P('dp'), may hold values from 0.25 to 1.75
- ffn_shift: bfloat16 [512], P('dp'), may hold values from -3 to 3
- up_weight: bfloat16 [512, 2048], P('dp', 'tensor'), may hold values from -0.25 to 0.25
- up_bias: bfloat16 [2048], P(('tensor', 'dp')), may hold values from -3 to 3
- down_weight: bfloat16 [2048, 512], P(('tensor', 'dp')), may hold values from -0.125 to 0.125
- cotangent: bfloat16 [32, 704, 512], P('dp'), may hold values from -6 to 6
Outputs:
- block_out: bfloat16 [32, 704, 512], P('dp')
- segments_grad: float32 [32, 704, 512], P('dp')
- norm_gain_grad: float32 [512], P('dp')
- norm_shift_grad: float32 [512], P('dp')
- qkv_weight_grad: float32 [512, 3, 512], P('dp', None, 'tensor')
- out_weight_grad: float32 [512, 512], P(('tensor', 'dp'))
- ffn_gain_grad: float32 [512], P('dp')
- ffn_shift_grad: float32 [512], P('dp')
- up_weight_grad: float32 [512, 2048], P('dp', 'tensor')
- up_bias_grad: float32 [2048], P(('tensor', 'dp'))
- down_weight_grad: float32 [2048, 512], P(('tensor', 'dp'))
Inputs may be any that keep to these rules, and one draw needn't show every extreme that they name: One sequence has exactly 704 live segments and one exactly 300; slots at and after seg_count are padding. `seg_start`: 0 in the first slot, strictly rising over a sequence's live segments and below 2048 there; 2048 in every padded slot.
All inputs are finite; a program needn't handle non-finite values.
Results may differ from a plain program's by a relative error of at most 0.014.
Values may be sent and summed in bfloat16 or wider, within the bound.
No kernel may reach another device: no remote copies, remote signals or barrier semaphores. Data moves between devices by JAX's collectives and lax.ppermute only.
A program may use at most 128 MiB of HBM per device.

v0:
```python
import math

import jax
import jax.numpy as jnp
from jax import lax
from jax.sharding import PartitionSpec as P

HEAD = 64


EPSILON = 1e-05
MASKED = -1e30


def split_up(array, dim, devices):
    dims = array.shape
    pieces = array.reshape(*dims[:dim], devices, dims[dim] // devices, *dims[dim + 1 :])
    return jnp.moveaxis(pieces, dim, 0)


def summed_on_arrival(array, axis, dim):
    pieces = split_up(array, dim, lax.axis_size(axis))
    arrived = lax.all_to_all(pieces, axis, split_axis=0, concat_axis=0, tiled=True)
    return arrived.astype(jnp.float32).sum(axis=0)


def sent_together(arrays, axis, dim, along):
    widths = [math.prod(a.shape[along:]) for a in arrays]
    both = jnp.concatenate(
        [a.reshape(*a.shape[:along], w) for a, w in zip(arrays, widths)], axis=along
    )
    filled = summed_on_arrival(both, axis, dim)
    pieces = jnp.split(filled, [sum(widths[:k]) for k in range(1, len(widths))], axis=along)
    return tuple(
        (b.reshape(*filled.shape[:along], *a.shape[along:]) for a, b in zip(arrays, pieces))
    )


def normalize(values, scale_vec, offset_vec):
    centre = jnp.mean(values, axis=-1, keepdims=True)
    centred = values - centre
    spread = jnp.mean(centred * centred, axis=-1, keepdims=True)
    return centred * lax.rsqrt(spread + EPSILON) * scale_vec + offset_vec


def rotate(values, cosine, sine_term):
    half_size = values.shape[-1] // 2
    turned = jnp.concatenate([-values[..., half_size:], values[..., :half_size]], axis=-1)
    return values * cosine + turned * sine_term


def rotary_tables(starts, head_size):
    half_size = head_size // 2
    freq_index = jnp.arange(half_size).astype(jnp.float32)
    inverse = jnp.exp(freq_index * (-math.log(10000.0) / half_size))
    angles = starts.astype(jnp.float32)[..., None] * inverse
    angles = jnp.concatenate([angles, angles], axis=-1)
    return (jnp.cos(angles), jnp.sin(angles))


def allowed_keys(length, live_count):
    places = jnp.arange(length)
    return (places[None, :] <= places[:, None]) & (places[None, :] < live_count)


def exact_gelu(values):
    return jax.nn.gelu(values, approximate=False)


def masked_scores(queries, key_rows, live_count):
    scores = jnp.einsum("qhd,khd->hqk", queries, key_rows, preferred_element_type=jnp.float32)
    allowed = allowed_keys(queries.shape[0], live_count)
    return jnp.where(allowed[None], scores, MASKED)


def attend_forward(packed):
    queries, key_rows, value_rows, live_count = packed
    scores = masked_scores(queries, key_rows, live_count)
    row_max = jnp.max(scores, axis=-1, keepdims=True)
    weights = jnp.exp(scores - row_max)
    row_total = jnp.sum(weights, axis=-1, keepdims=True)
    attention_probs = weights / row_total
    mixed_rows = jnp.einsum(
        "hqk,khd->qhd",
        attention_probs.astype(jnp.bfloat16),
        value_rows,
        preferred_element_type=jnp.float32,
    )
    return (mixed_rows.astype(jnp.bfloat16), row_max[..., 0] + jnp.log(row_total[..., 0]))


def attend_backward(packed):
    queries, key_rows, value_rows, live_count, log_total, out_grad = packed
    scores = masked_scores(queries, key_rows, live_count)
    attention_probs = jnp.exp(scores - log_total[..., None])
    prob_grad = jnp.einsum("qhd,khd->hqk", out_grad, value_rows, preferred_element_type=jnp.float32)
    inner_sum = jnp.sum(prob_grad * attention_probs, axis=-1, keepdims=True)
    score_grad = (attention_probs * (prob_grad - inner_sum)).astype(jnp.bfloat16)
    query_grad = jnp.einsum(
        "hqk,khd->qhd", score_grad, key_rows, preferred_element_type=jnp.float32
    )
    key_grad = jnp.einsum("hqk,qhd->khd", score_grad, queries, preferred_element_type=jnp.float32)
    value_grad = jnp.einsum(
        "hqk,qhd->khd",
        attention_probs.astype(jnp.bfloat16),
        out_grad,
        preferred_element_type=jnp.float32,
    )
    return (query_grad, key_grad, value_grad)


def run_layer(segments, seg_start, seg_count, cotangent, weights):
    seq_local, seg_len, model_width = segments.shape
    token_rows = seq_local * seg_len
    gain_one = weights[0].astype(jnp.float32)
    shift_one = weights[1].astype(jnp.float32)
    gain_two = weights[2].astype(jnp.float32)
    shift_two = weights[3].astype(jnp.float32)
    w_qkv, w_out, w_up = (weights[4], weights[5], weights[6])
    b_up = weights[7].astype(jnp.float32)
    w_down = weights[8]
    local_width = w_qkv.shape[2]
    local_heads = local_width // HEAD
    head_shape = (token_rows, local_heads, HEAD)
    seq_shape = (seq_local, seg_len, local_heads, HEAD)
    inputs = segments.reshape(token_rows, model_width).astype(jnp.float32)
    normed_one, norm_one_pull = jax.vjp(normalize, inputs, gain_one, shift_one)
    attn_in = normed_one.astype(jnp.bfloat16)
    projected = jnp.einsum("nd,dct->nct", attn_in, w_qkv, preferred_element_type=jnp.float32)
    cosine, sine_term = rotary_tables(seg_start.reshape(token_rows), HEAD)
    cosine = cosine[:, None, :]
    sine_term = sine_term[:, None, :]

    def place_rotary(raw_query, raw_key):
        return (
            rotate(raw_query, cosine, sine_term) * HEAD ** (-0.5),
            rotate(raw_key, cosine, sine_term),
        )

    rotated, rotary_pull = jax.vjp(
        place_rotary, projected[:, 0].reshape(head_shape), projected[:, 1].reshape(head_shape)
    )
    queries = rotated[0].astype(jnp.bfloat16).reshape(seq_shape)
    key_rows = rotated[1].astype(jnp.bfloat16).reshape(seq_shape)
    value_rows = projected[:, 2].astype(jnp.bfloat16).reshape(seq_shape)
    mixed_rows, log_total = lax.map(attend_forward, (queries, key_rows, value_rows, seg_count))
    mixed_flat = mixed_rows.reshape(token_rows, local_width)
    attn_part = jnp.dot(mixed_flat, w_out, preferred_element_type=jnp.float32)
    attn_full = lax.psum(attn_part, "tensor")
    residual = inputs + attn_full
    normed_two, norm_two_pull = jax.vjp(normalize, residual, gain_two, shift_two)
    ffn_in = normed_two.astype(jnp.bfloat16)
    pre_act = jnp.dot(ffn_in, w_up, preferred_element_type=jnp.float32) + b_up
    activated, gelu_pull = jax.vjp(exact_gelu, pre_act)
    act_low = activated.astype(jnp.bfloat16)
    ffn_part = jnp.dot(act_low, w_down, preferred_element_type=jnp.float32)
    ffn_full = lax.psum(ffn_part.astype(jnp.bfloat16), "tensor").astype(jnp.float32)
    block_out = (residual + ffn_full).astype(jnp.bfloat16).reshape(segments.shape)
    out_rows = cotangent.reshape(token_rows, model_width)
    down_grad = jnp.einsum("nf,nd->fd", act_low, out_rows, preferred_element_type=jnp.float32)
    act_grad = jnp.einsum("nd,fd->nf", out_rows, w_down, preferred_element_type=jnp.float32)
    pre_grad = gelu_pull(act_grad)[0].astype(jnp.bfloat16)
    bias_grad = jnp.sum(pre_grad, axis=0, dtype=jnp.float32)
    up_grad = jnp.einsum("nd,nf->df", ffn_in, pre_grad, preferred_element_type=jnp.float32)
    ffn_in_part = jnp.einsum("nf,df->nd", pre_grad, w_up, preferred_element_type=jnp.float32)
    ffn_in_grad = lax.psum(ffn_in_part, "tensor")
    resid_ln_grad, gain_two_grad, shift_two_grad = norm_two_pull(ffn_in_grad)
    residual_grad = out_rows.astype(jnp.float32) + resid_ln_grad
    attn_grad_low = residual_grad.astype(jnp.bfloat16)
    out_w_grad = jnp.einsum(
        "nt,nd->td", mixed_flat, attn_grad_low, preferred_element_type=jnp.float32
    )
    mixed_grad = jnp.einsum(
        "nd,td->nt", attn_grad_low, w_out, preferred_element_type=jnp.float32
    ).astype(jnp.bfloat16)
    ffn_shares = None
    query_grad, key_grad, value_grad = lax.map(
        attend_backward,
        (queries, key_rows, value_rows, seg_count, log_total, mixed_grad.reshape(seq_shape)),
    )
    raw_query_grad, raw_key_grad = rotary_pull(
        (query_grad.reshape(head_shape), key_grad.reshape(head_shape))
    )
    proj_grad = jnp.stack(
        [
            raw_query_grad.reshape(token_rows, local_width),
            raw_key_grad.reshape(token_rows, local_width),
            value_grad.reshape(token_rows, local_width),
        ],
        axis=1,
    ).astype(jnp.bfloat16)
    qkv_grad = jnp.einsum("nd,nct->dct", attn_in, proj_grad, preferred_element_type=jnp.float32)
    attn_in_part = jnp.einsum("nct,dct->nd", proj_grad, w_qkv, preferred_element_type=jnp.float32)
    attn_in_grad = lax.psum(attn_in_part.astype(jnp.bfloat16), "tensor").astype(jnp.float32)
    input_ln_grad, gain_one_grad, shift_one_grad = norm_one_pull(attn_in_grad)
    input_grad = (residual_grad + input_ln_grad).reshape(segments.shape)
    grads = (
        gain_one_grad,
        shift_one_grad,
        qkv_grad,
        out_w_grad,
        gain_two_grad,
        shift_two_grad,
        up_grad,
        bias_grad,
        down_grad,
    )
    return (block_out, input_grad, grads, ffn_shares)


def local(
    segments,
    seg_start,
    seg_count,
    norm_gain,
    norm_shift,
    qkv_weight,
    out_weight,
    ffn_gain,
    ffn_shift,
    up_weight,
    up_bias,
    down_weight,
    cotangent,
):
    gathered = (
        lax.all_gather(norm_gain, "dp", axis=0, tiled=True),
        lax.all_gather(norm_shift, "dp", axis=0, tiled=True),
        lax.all_gather(ffn_gain, "dp", axis=0, tiled=True),
        lax.all_gather(ffn_shift, "dp", axis=0, tiled=True),
        lax.all_gather(qkv_weight, "dp", axis=0, tiled=True),
        lax.all_gather(out_weight, "dp", axis=0, tiled=True),
        lax.all_gather(up_weight, "dp", axis=0, tiled=True),
        lax.all_gather(up_bias, "dp", axis=0, tiled=True),
        lax.all_gather(down_weight, "dp", axis=0, tiled=True),
    )
    block_out, input_grad, grads, ffn_shares = run_layer(
        segments, seg_start, seg_count, cotangent, gathered
    )
    (
        gain_one_grad,
        shift_one_grad,
        qkv_grad,
        out_w_grad,
        gain_two_grad,
        shift_two_grad,
        up_grad,
        bias_grad,
        down_grad,
    ) = grads
    shares = (
        summed_on_arrival(gain_one_grad.astype(jnp.bfloat16), "dp", 0),
        *sent_together(
            (shift_one_grad.astype(jnp.bfloat16), qkv_grad.astype(jnp.bfloat16)), "dp", 0, 1
        ),
        summed_on_arrival(out_w_grad.astype(jnp.bfloat16), "dp", 0),
        summed_on_arrival(gain_two_grad.astype(jnp.bfloat16), "dp", 0),
        *sent_together(
            (
                shift_two_grad.astype(jnp.bfloat16),
                up_grad.astype(jnp.bfloat16),
                bias_grad.astype(jnp.bfloat16),
                down_grad.astype(jnp.bfloat16),
            ),
            "dp",
            0,
            1,
        ),
    )
    gain_one_s, shift_one_s, qkv_s, out_s, gain_two_s, shift_two_s, up_s, bias_s, down_s = shares
    return (
        block_out,
        input_grad,
        gain_one_s,
        shift_one_s,
        qkv_s,
        out_s,
        gain_two_s,
        shift_two_s,
        up_s,
        bias_s,
        down_s,
    )


def solution(mesh):
    placed = (
        P("dp", None, None),
        P("dp", None),
        P("dp"),
        P("dp"),
        P("dp"),
        P("dp", None, "tensor"),
        P(("tensor", "dp"), None),
        P("dp"),
        P("dp"),
        P("dp", "tensor"),
        P(("tensor", "dp")),
        P(("tensor", "dp"), None),
        P("dp", None, None),
    )
    return jax.shard_map(
        local,
        mesh=mesh,
        in_specs=placed,
        out_specs=(
            P("dp", None, None),
            P("dp", None, None),
            P("dp"),
            P("dp"),
            P("dp", None, "tensor"),
            P(("tensor", "dp"), None),
            P("dp"),
            P("dp"),
            P("dp", "tensor"),
            P(("tensor", "dp")),
            P(("tensor", "dp"), None),
        ),
        check_vma=False,
    )
```

profile of v0, /device:TPU:0, one launch (start us, length us, event | category | flops | bytes accessed | tf_op | source)
XLA Modules:
  0.0 764.0 jit_solution(6756772383985416356)
XLA Ops:
  13.8 23.3 %all-reduce.9 = (bf16[512]{0:T(512)(128)(2,1)S(1)}, bf16[512]{0:T(512)(128)(2,1)S(1)}, bf16[512]{0:T(512)(128)(2,1)S(1)}, bf16[512]{0:T(512)(128)(2,1)S(1)}, bf16[512]{0:T(512)(128)(2,1)S(1)}) all-reduce(bf16[512]{0:T(512)(128)(2,1)S(1)} %dynamic-update-slice.1, ...), channel_id=1, replica_groups=mesh['dp'=8,'tensor'=4] {'dp'}, use_global_device_ids=true, to_apply=%add.5 | all-reduce | flops 2560 | bytes 10240
  37.3 31.0 %all_gather.29 = bf16[512,3,128]{2,0,1:T(8,128)(2,1)S(1)} all-gather(bf16[64,3,128]{2,0,1:T(8,128)(2,1)S(1)} %copy-done.44), channel_id=1, replica_groups=mesh['dp'=8,'tensor'=4] {'dp'}, dimensions={0}, use_global_device_ids=true | all-gather | bytes 442368 | tf_op jit(solution)/shard_map/all_gather | solution.py:231
  74.1 30.7 %all_gather.30 = bf16[128,512]{1,0:T(8,128)(2,1)S(1)} all-gather(bf16[16,512]{1,0:T(8,128)(2,1)S(1)} %copy-done.45), channel_id=1, replica_groups=mesh['dp'=8,'tensor'=4] {'dp'}, dimensions={0}, use_global_device_ids=true | all-gather | bytes 147456 | tf_op jit(solution)/shard_map/all_gather | solution.py:232
  104.9 6.5 fusion.85
  144.9 31.6 %while.26 = (s32[]{:T(128)}, bf16[4,704,2,64]{1,3,2,0:T(8,128)(2,1)}, f32[4,2,704]{2,1,0:T(2,128)}, bf16[4,704,2,64]{1,3,2,0:T(8,128)(2,1)}, s32[4]{0:T(128)S(1)...) while((s32[]{:T(128)}, bf16[4,704,2,64]{1,3,2,0:T(8,128)(2,1)}, ...), condition=%wide.region_5.6_spmd, body=%wide.region_2.5_spmd.sunk | while | flops 263757120 | bytes 14712817 | solution.py:146
  188.4 31.8 %all_gather.33 = bf16[512,512]{1,0:T(8,128)(2,1)S(1)} all-gather(bf16[64,512]{1,0:T(8,128)(2,1)} %param.26), channel_id=1, replica_groups=mesh['dp'=8,'tensor'=4] {'dp'}, dimensions={0}, use_global_device_ids=true | all-gather | bytes 589824 | tf_op jit(solution)/shard_map/all_gather | solution.py:233
  220.2 33.4 %all_gather.35 = bf16[512,512]{1,0:T(8,128)(2,1)} all-gather(bf16[64,512]{1,0:T(8,128)(2,1)} %param.28), channel_id=1, replica_groups=mesh['dp'=8,'tensor'=4] {'dp'}, dimensions={0}, use_global_device_ids=true | all-gather | bytes 589824 | tf_op jit(solution)/shard_map/all_gather | solution.py:235
  253.5 41.4 %all-reduce.15.cloned.1.call-done = f32[2816,512]{1,0:T(8,128)} async-done(((f32[2816,512]{1,0:T(8,128)}), f32[2816,512]{1,0:T(8,128)}) %all-reduce.15.cloned.1.call-update) | async-done | bytes 5767184 | tf_op jit(solution)/shard_map/psum | solution.py:149
  303.4 16.5 %fusion.89 = (bf16[512]{0:T(512)(128)(2,1)}, bf16[2816,512]{1,0:T(8,128)(2,1)S(1)}, f32[2816,512]{1,0:T(8,128)}) fusion(f32[2816,512]{1,0:T(8,128)S(1)} %fusion.98, f32[512]{0:T(512)S(1)} %copy-done.48, bf16[2816,512]{1,0:T(8,128)(2,1)S(1)} %bitcast.198, bf16[512,512]{1,0:T(8,128)(2,1)S(1)} %copy-done.29), kind=kOutput, calls=%fused_computation.166 | convolution fusion | flops 1583087104 | bytes 17828864 | tf_op jit(solution)/shard_map/nd,fd->nf/dot_general | solution.py:161
  330.1 7.0 multiply_convert_fusion.1
  343.1 93.9 %all-reduce.17.cloned.1.call-done = f32[2816,512]{1,0:T(8,128)} async-done(((f32[2816,512]{1,0:T(8,128)}), f32[2816,512]{1,0:T(8,128)}) %all-reduce.17.cloned.1.call-update) | async-done | bytes 5767184 | tf_op jit(solution)/shard_map/psum | solution.py:166
  466.9 106.9 %while.27 = (s32[]{:T(128)}, f32[4,704,2,64]{1,0,3,2:T(4,128)}, f32[4,704,2,64]{1,0,3,2:T(4,128)}, bf16[4,704,2,64]{1,3,2,0:T(8,128)(2,1)}, bf16[4,704,2,64]{1,3...) while((s32[]{:T(128)}, f32[4,704,2,64]{1,0,3,2:T(4,128)}, ...), condition=%wide.region_15.16_spmd, body=%wide.region_13.15_spmd.sunk | while | flops 647273792 | bytes 44077144 | solution.py:177
  476.8 8.4 %dynamic_update_slice.30 = f32[4,704,2,64]{1,0,3,2:T(4,128)} dynamic-update-slice(f32[4,704,2,64]{1,0,3,2:T(4,128)} %get-tuple-element.440, f32[1,704,2,64]{1,0,3,2:T(1,128)S(1)} %copy.151, s32[]{:T(128)S(6)} %copy.177, s32[]{:T(128)} %constant.60.clone.1..sunk, s32[]{:T(128)} %constant.60.clone.1..sunk, s32[]{:T(128)} %constant.60.clone.1..sunk) | dynamic-update-slice | bytes 720900 | tf_op jit(solution)/shard_map/while/body/jit(dynamic_update_index_in_dim)/dynamic_update_slice | solution.py:177
  485.2 8.4 %dynamic_update_slice.29 = f32[4,704,2,64]{1,0,3,2:T(4,128)} dynamic-update-slice(f32[4,704,2,64]{1,0,3,2:T(4,128)} %get-tuple-element.439, f32[1,704,2,64]{1,0,3,2:T(1,128)S(1)} %copy.150, s32[]{:T(128)S(6)} %copy.177, s32[]{:T(128)} %constant.60.clone.1..sunk, s32[]{:T(128)} %constant.60.clone.1..sunk, s32[]{:T(128)} %constant.60.clone.1..sunk) | dynamic-update-slice | bytes 720900 | tf_op jit(solution)/shard_map/while/body/jit(dynamic_update_index_in_dim)/dynamic_update_slice | solution.py:177
  503.5 8.4 %dynamic_update_slice.30 = f32[4,704,2,64]{1,0,3,2:T(4,128)} dynamic-update-slice(f32[4,704,2,64]{1,0,3,2:T(4,128)} %get-tuple-element.440, f32[1,704,2,64]{1,0,3,2:T(1,128)S(1)} %copy.151, s32[]{:T(128)S(6)} %copy.177, s32[]{:T(128)} %constant.60.clone.1..sunk, s32[]{:T(128)} %constant.60.clone.1..sunk, s32[]{:T(128)} %constant.60.clone.1..sunk) | dynamic-update-slice | bytes 720900 | tf_op jit(solution)/shard_map/while/body/jit(dynamic_update_index_in_dim)/dynamic_update_slice | solution.py:177
  511.9 8.4 %dynamic_update_slice.29 = f32[4,704,2,64]{1,0,3,2:T(4,128)} dynamic-update-slice(f32[4,704,2,64]{1,0,3,2:T(4,128)} %get-tuple-element.439, f32[1,704,2,64]{1,0,3,2:T(1,128)S(1)} %copy.150, s32[]{:T(128)S(6)} %copy.177, s32[]{:T(128)} %constant.60.clone.1..sunk, s32[]{:T(128)} %constant.60.clone.1..sunk, s32[]{:T(128)} %constant.60.clone.1..sunk) | dynamic-update-slice | bytes 720900 | tf_op jit(solution)/shard_map/while/body/jit(dynamic_update_index_in_dim)/dynamic_update_slice | solution.py:177
  530.2 8.4 %dynamic_update_slice.30 = f32[4,704,2,64]{1,0,3,2:T(4,128)} dynamic-update-slice(f32[4,704,2,64]{1,0,3,2:T(4,128)} %get-tuple-element.440, f32[1,704,2,64]{1,0,3,2:T(1,128)S(1)} %copy.151, s32[]{:T(128)S(6)} %copy.177, s32[]{:T(128)} %constant.60.clone.1..sunk, s32[]{:T(128)} %constant.60.clone.1..sunk, s32[]{:T(128)} %constant.60.clone.1..sunk) | dynamic-update-slice | bytes 720900 | tf_op jit(solution)/shard_map/while/body/jit(dynamic_update_index_in_dim)/dynamic_update_slice | solution.py:177
  538.6 8.4 %dynamic_update_slice.29 = f32[4,704,2,64]{1,0,3,2:T(4,128)} dynamic-update-slice(f32[4,704,2,64]{1,0,3,2:T(4,128)} %get-tuple-element.439, f32[1,704,2,64]{1,0,3,2:T(1,128)S(1)} %copy.150, s32[]{:T(128)S(6)} %copy.177, s32[]{:T(128)} %constant.60.clone.1..sunk, s32[]{:T(128)} %constant.60.clone.1..sunk, s32[]{:T(128)} %constant.60.clone.1..sunk) | dynamic-update-slice | bytes 720900 | tf_op jit(solution)/shard_map/while/body/jit(dynamic_update_index_in_dim)/dynamic_update_slice | solution.py:177
  556.9 8.4 %dynamic_update_slice.30 = f32[4,704,2,64]{1,0,3,2:T(4,128)} dynamic-update-slice(f32[4,704,2,64]{1,0,3,2:T(4,128)} %get-tuple-element.440, f32[1,704,2,64]{1,0,3,2:T(1,128)S(1)} %copy.151, s32[]{:T(128)S(6)} %copy.177, s32[]{:T(128)} %constant.60.clone.1..sunk, s32[]{:T(128)} %constant.60.clone.1..sunk, s32[]{:T(128)} %constant.60.clone.1..sunk) | dynamic-update-slice | bytes 720900 | tf_op jit(solution)/shard_map/while/body/jit(dynamic_update_index_in_dim)/dynamic_update_slice | solution.py:177
  565.3 8.4 %dynamic_update_slice.29 = f32[4,704,2,64]{1,0,3,2:T(4,128)} dynamic-update-slice(f32[4,704,2,64]{1,0,3,2:T(4,128)} %get-tuple-element.439, f32[1,704,2,64]{1,0,3,2:T(1,128)S(1)} %copy.150, s32[]{:T(128)S(6)} %copy.177, s32[]{:T(128)} %constant.60.clone.1..sunk, s32[]{:T(128)} %constant.60.clone.1..sunk, s32[]{:T(128)} %constant.60.clone.1..sunk) | dynamic-update-slice | bytes 720900 | tf_op jit(solution)/shard_map/while/body/jit(dynamic_update_index_in_dim)/dynamic_update_slice | solution.py:177
  631.7 20.8 %all-to-all-done.4 = bf16[8,64,1026]{2,1,0:T(8,128)(2,1)} async-done(((bf16[8,64,1026]{2,1,0:T(8,128)(2,1)}), bf16[8,64,1026]{2,1,0:T(8,128)(2,1)}, u32[]{:S(2)}, u32[]{:S(2)}) %all-to-all-start.4) | async-done | bytes 1050656 | tf_op jit(solution)/shard_map/all_to_all | solution.py:23
  655.6 54.0 %all-reduce.19.cloned.1.call-done = (bf16[2816,512]{1,0:T(8,128)(2,1)}, bf16[2816,512]{1,0:T(8,128)(2,1)}) async-done(((bf16[2816,512]{1,0:T(8,128)(2,1)}, bf16[2816,512]{1,0:T(8,128)(2,1)}), (bf16[2816,512]{1,0:T(8,128)(2,1)}, bf16[2816,512]{1,0:T(8,128)(2,1)})) %all-reduce.19.cloned.1.call-update) | async-done | bytes 5767184 | tf_op jit(solution)/shard_map/psum | solution.py:157
  726.5 8.1 %add_add_fusion.2 = f32[2816,512]{1,0:T(8,128)} fusion(bf16[4,704,512]{2,1,0:T(8,128)(2,1)S(1)} %copy-done.2, bf16[2816,512]{1,0:T(8,128)(2,1)} %get-tuple-element.256, f32[2816,512]{1,0:T(8,128)} %get-tuple-element.261, f32[2816]{0:T(1024)S(1)} %negate_multiply_fusion.1, f32[2816]{0:T(1024)S(1)} %multiply_multiply_fusion.5, ...), kind=kLoop, calls=%fused_computation.83 | loop fusion | flops 18743296 | bytes 20243456 | tf_op jit(solution)/shard_map/add | solution.py:196
  748.6 7.1 all-to-all-done.1
  (330 shorter events, 274.8 us)
Async XLA Ops:
  7.3 30.0 %copy-start.44 = (bf16[64,3,128]{2,0,1:T(8,128)(2,1)S(1)}, bf16[64,3,128]{2,0,1:T(8,128)(2,1)}, u32[]{:S(2)}) copy-start(bf16[64,3,128]{2,0,1:T(8,128)(2,1)} %param.22) | copy-start | bytes 147460
  7.3 287.7 %all-reduce.15.cloned.1.call-start = ((), (), s32[]{:S(2)}) async-start(), calls=%async_computation.5 | async-start | bytes 11534336 | tf_op jit(solution)/shard_map/psum | solution.py:149
  7.3 97.5 %copy-start.49 = (f32[32]{0:T(128)}, f32[32]{0:T(128)S(1)}, u32[]{:S(2)}) copy-start(f32[32]{0:T(128)S(1)} %multiply_exponential_fusion) | copy-start | bytes 388
  9.9 60.0 %copy-start.31 = (f32[2816]{0:T(1024)}, f32[2816]{0:T(1024)S(1)}, u32[]{:S(2)}) copy-start(f32[2816]{0:T(1024)S(1)} %div.47) | copy-start | bytes 33796
  37.1 34.2 %copy-start.41 = (f32[512]{0:T(512)}, f32[512]{0:T(512)S(1)}, u32[]{:S(2)}) copy-start(f32[512]{0:T(512)S(1)} %convert_element_type.198) | copy-start | bytes 6148
  37.3 34.1 %copy-start.37 = (f32[2816]{0:T(1024)}, f32[2816]{0:T(1024)S(1)}, u32[]{:S(2)}) copy-start(f32[2816]{0:T(1024)S(1)} %add.103) | copy-start | bytes 33796
  37.3 31.1 %copy-start.33 = (f32[2816]{0:T(1024)}, f32[2816]{0:T(1024)S(1)}, u32[]{:S(2)}) copy-start(f32[2816]{0:T(1024)S(1)} %rsqrt.20) | copy-start | bytes 33796
  186.5 250.5 %all-reduce.17.cloned.1.call-start = ((), (), s32[]{:S(2)}) async-start(), calls=%async_computation.6 | async-start | bytes 11534336 | tf_op jit(solution)/shard_map/psum | solution.py:166
  303.2 16.7 %copy-start.5 = (f32[2816,512]{1,0:T(8,128)}, f32[2816,512]{1,0:T(8,128)S(1)}, u32[]{:S(2)}) copy-start(f32[2816,512]{1,0:T(8,128)S(1)} %fusion.98) | copy-start | bytes 17301508
  340.6 96.4 %copy-start.36 = (f32[2816]{0:T(1024)S(1)}, f32[2816]{0:T(1024)}, u32[]{:S(2)}) copy-start(f32[2816]{0:T(1024)} %copy-done.35) | copy-start | bytes 33796
  343.1 100.2 %copy-start.40 = (f32[2816]{0:T(1024)S(1)}, f32[2816]{0:T(1024)}, u32[]{:S(2)}) copy-start(f32[2816]{0:T(1024)} %copy-done.39) | copy-start | bytes 33796
  443.3 12.7 %copy-start.10 = (bf16[4,704,512]{2,1,0:T(8,128)(2,1)S(1)}, bf16[4,704,512]{2,1,0:T(8,128)(2,1)}, u32[]{:S(2)}) copy-start(bf16[4,704,512]{2,1,0:T(8,128)(2,1)} %param.29) | copy-start | bytes 8650756
  450.4 151.2 %all-to-all-start.3 = ((bf16[8,1,64]{2,1,0:T(2,128)(2,1)}), bf16[8,1,64]{2,1,0:T(2,128)(2,1)S(1)}, u32[]{:S(2)}, u32[]{:S(2)}) async-start(bf16[8,1,64]{2,1,0:T(2,128)(2,1)} %convert_element_type.240), calls=%async_computation.3 | async-start | bytes 8192 | tf_op jit(solution)/shard_map/all_to_all | solution.py:23
  456.0 253.6 %all-reduce.19.cloned.1.call-start = ((), (), s32[]{:S(2)}) async-start(), calls=%async_computation.7 | async-start | bytes 11534336 | tf_op jit(solution)/shard_map/psum | solution.py:157
  601.6 17.4 %all-to-all-start.2 = ((bf16[8,16,512]{2,1,0:T(8,128)(2,1)}), bf16[8,16,512]{2,1,0:T(8,128)(2,1)}, u32[]{:S(2)}, u32[]{:S(2)}) async-start(bf16[8,16,512]{2,1,0:T(8,128)(2,1)} %bitcast.31), calls=%async_computation.2 | async-start | bytes 262144 | tf_op jit(solution)/shard_map/all_to_all | solution.py:23
  607.5 7.9 %copy-start.28 = (bf16[512,512]{1,0:T(8,128)(2,1)S(1)}, bf16[512,512]{1,0:T(8,128)(2,1)}, u32[]{:S(2)}) copy-start(bf16[512,512]{1,0:T(8,128)(2,1)} %convolution_convert_fusion.3) | copy-start | bytes 1572868
  612.8 12.2 %copy-start.12 = (bf16[2816,512]{1,0:T(8,128)(2,1)S(1)}, bf16[2816,512]{1,0:T(8,128)(2,1)}, u32[]{:S(2)}) copy-start(bf16[2816,512]{1,0:T(8,128)(2,1)} %copy-done.11) | copy-start | bytes 8650756
  619.0 33.6 %all-to-all-start.4 = ((bf16[8,64,1026]{2,1,0:T(8,128)(2,1)}), bf16[8,64,1026]{2,1,0:T(8,128)(2,1)}, u32[]{:S(2)}, u32[]{:S(2)}) async-start(bf16[8,64,1026]{2,1,0:T(8,128)(2,1)} %concatenate.60), calls=%async_computation.4 | async-start | bytes 2359296 | tf_op jit(solution)/shard_map/all_to_all | solution.py:23
  624.9 84.6 %copy-start.32 = (f32[2816]{0:T(1024)S(1)}, f32[2816]{0:T(1024)}, u32[]{:S(2)}) copy-start(f32[2816]{0:T(1024)} %copy-done.31) | copy-start | bytes 33796
  625.0 84.6 %copy-start.42 = (f32[512]{0:T(512)S(1)}, f32[512]{0:T(512)}, u32[]{:S(2)}) copy-start(f32[512]{0:T(512)} %copy-done.41) | copy-start | bytes 6148
  628.2 81.4 %copy-start.2 = (bf16[4,704,512]{2,1,0:T(8,128)(2,1)S(1)}, bf16[4,704,512]{2,1,0:T(8,128)(2,1)}, u32[]{:S(2)}) copy-start(bf16[4,704,512]{2,1,0:T(8,128)(2,1)} %param.17) | copy-start | bytes 8650756
  720.7 15.3 %all-to-all-start = ((bf16[8,1,64]{2,1,0:T(2,128)(2,1)}), bf16[8,1,64]{2,1,0:T(2,128)(2,1)S(1)}, u32[]{:S(2)}, u32[]{:S(2)}) async-start(bf16[8,1,64]{2,1,0:T(2,128)(2,1)} %convert_element_type.238), calls=%async_computation | async-start | bytes 8192 | tf_op jit(solution)/shard_map/all_to_all | solution.py:23
  726.5 8.3 %copy-start.21 = (bf16[8,64,384]{2,1,0:T(8,128)(2,1)S(1)}, bf16[8,64,384]{2,1,0:T(8,128)(2,1)}, u32[]{:S(2)}) copy-start(bf16[8,64,384]{2,1,0:T(8,128)(2,1)} %concatenate.55) | copy-start | bytes 1179652
  736.0 19.8 %all-to-all-start.1 = ((bf16[8,64,385]{2,1,0:T(8,128)(2,1)}), bf16[8,64,385]{2,1,0:T(8,128)(2,1)S(1)}, u32[]{:S(2)}, u32[]{:S(2)}) async-start(bf16[8,64,385]{2,1,0:T(8,128)(2,1)} %pad_maximum_fusion.5), calls=%async_computation.1 | async-start | bytes 1048576 | tf_op jit(solution)/shard_map/all_to_all | solution.py:23
  (49 other events, 167.2 us)
Sparse Core Ops, SparseCore 0:
  186.6 108.3 all-reduce.14
  325.7 111.2 all-reduce.16
  597.6 111.8 all-reduce.18
where the time goes:
time: 773 us; the launch traced here: 764 us
  waiting for transfers between devices  217 us (28%)
  local copies, waits for them, and re-layouts  151 us (20%)
  blocking collectives  150 us (19%)
  other arithmetic  107 us (14%)
  matrix products  92.4 us (12%)
  starting transfers between devices  29.4 us (4%)
  between operations  15.5 us (2%)
    psum x1, waiting for transfers between devices, run_layer(): ffn_in_grad = lax.psum(ffn_in_part, 'tensor')  93.9 us
    dynamic_update_slice x16, local copies, waits for them, and re-layouts, run_layer(): lax.map(attend_backward, (queries, key_rows, value_rows, seg_count, log_t...  70.8 us
    psum x1, waiting for transfers between devices, run_layer(): lax.psum(ffn_part.astype(jnp.bfloat16), 'tensor').astype(jnp.float32)  54 us
    psum x1, waiting for transfers between devices, run_layer(): attn_full = lax.psum(attn_part, 'tensor')  41.4 us
    all_gather x1, blocking collectives, local(): lax.all_gather(down_weight, 'dp', axis=0, tiled=True)  33.4 us
    all_gather x1, blocking collectives, local(): lax.all_gather(up_weight, 'dp', axis=0, tiled=True)  31.8 us
    all_gather x1, blocking collectives, local(): lax.all_gather(qkv_weight, 'dp', axis=0, tiled=True)  31 us
    all_gather x1, blocking collectives, local(): lax.all_gather(out_weight, 'dp', axis=0, tiled=True)  30.7 us
  transfers between devices with their start and end apart: 8, of which 5 were waited for; matrix products, arithmetic and copies ran while one was open for 26% of the time, Pallas kernels for 0%

commit v1 on v0

v1 whole, which is shorter than its diff:
```python
import math

import jax
import jax.numpy as jnp
from jax import lax
from jax.experimental import pallas as pl
from jax.experimental.pallas import tpu as pltpu
from jax.sharding import PartitionSpec as P

HEAD = 64
PAIR = 2 * HEAD
BLOCK = 256
EPSILON = 1e-05
MASKED = -1e30
BF16 = jnp.bfloat16
F32 = jnp.float32
EXTRA = 16


def nn(a, b):
    return lax.dot_general(a, b, (((1,), (0,)), ((), ())), preferred_element_type=F32)


def nt(a, b):
    return lax.dot_general(a, b, (((1,), (1,)), ((), ())), preferred_element_type=F32)


def call(kernel, operands, outs, scratch=(), scalars=0, name=None):
    inner = [pl.BlockSpec(memory_space=pltpu.SMEM) for _ in range(scalars)]
    inner += [pl.BlockSpec(memory_space=pltpu.VMEM) for _ in operands[scalars:]]
    return pl.pallas_call(
        kernel,
        in_specs=inner,
        out_specs=[pl.BlockSpec(memory_space=pltpu.VMEM) for _ in outs],
        out_shape=[jax.ShapeDtypeStruct(s, d) for s, d in outs],
        scratch_shapes=list(scratch),
        compiler_params=pltpu.CompilerParams(vmem_limit_bytes=40 * 1024 * 1024),
        name=name,
    )(*operands)


def digits(size):
    out = []
    while size > 1:
        radix = math.gcd(size, 8)
        radix = size if radix == 1 else radix
        out.insert(0, radix)
        size //= radix
    return out or [1]


def step_list(radices):
    steps = [()]
    for radix in radices:
        steps = [s + (k,) for s in steps for k in range(radix)]
    return steps


def moved(index, radices, steps):
    target, scale = 0, 1
    for radix, step in zip(reversed(radices), reversed(steps)):
        target = target + (index % radix + step + radix) % radix * scale
        index = index // radix
        scale *= radix
    return target


def sent_ahead(value, radices, steps):
    size = math.prod(radices)
    return lax.ppermute(value, "dp", [(i, moved(i, radices, steps)) for i in range(size)])


def one_step(radices, place, k):
    return tuple(k if p == place else 0 for p in range(len(radices)))


def gather_pieces(piece, radices):
    held = {(): piece}
    for place, radix in enumerate(radices):
        held = {
            key + (k,): sent_ahead(value, radices, one_step(radices, place, k)) if k else value
            for key, value in held.items()
            for k in range(radix)
        }
    return [held[s] for s in step_list(radices)]


def scatter_pieces(pieces, radices):
    held = dict(zip(step_list(radices), pieces))
    for place in range(len(radices)):
        arrived = {}
        for key, value in held.items():
            steps = one_step(radices, place, key[0])
            got = sent_ahead(value, radices, steps) if key[0] else value
            arrived.setdefault(key[1:], []).append(got)
        last = place + 1 == len(radices)
        held = {
            key: (sum(v.astype(F32) for v in values) if last else
                  sum(v.astype(F32) for v in values).astype(values[0].dtype))
            for key, values in arrived.items()
        }
    return held[()]


def swap(value, bit):
    return lax.ppermute(value, "tensor", [(t, t ^ bit) for t in range(lax.axis_size("tensor"))])


def behind(radices):
    here = lax.axis_index("dp")
    return [moved(here, radices, tuple(-k for k in s)) for s in step_list(radices)]


def ahead(radices):
    here = lax.axis_index("dp")
    return [moved(here, radices, s) for s in step_list(radices)]


def in_place(pieces, order, parts):
    if all(rows % 16 == 0 for rows in parts):
        return pieces, order, parts
    count = len(pieces)
    stacked = jnp.stack(pieces)
    where = jnp.zeros((count,), jnp.int32).at[order].set(jnp.arange(count, dtype=jnp.int32))
    stacked = stacked[where]
    laid, at = [], 0
    for rows in parts:
        laid.append(stacked[:, at : at + rows].reshape(count * rows, -1))
        at += rows
    if at < stacked.shape[1]:
        laid.append(stacked[:, at:].astype(F32).sum(axis=0).astype(stacked.dtype))
    return [jnp.concatenate(laid)], jnp.zeros((1,), jnp.int32), [count * r for r in parts]


def norm_parts(rows):
    centred = rows - jnp.mean(rows, axis=-1, keepdims=True)
    rstd = lax.rsqrt(jnp.mean(centred * centred, axis=-1, keepdims=True) + EPSILON)
    return centred * rstd, rstd


def norm_pull(grad, gain, xhat, rstd):
    scaled = grad * gain
    level = jnp.mean(scaled, axis=-1, keepdims=True)
    along = jnp.mean(scaled * xhat, axis=-1, keepdims=True)
    return rstd * (scaled - level - xhat * along)


def colsum(rows):
    return jnp.sum(rows, axis=0, keepdims=True)


def enter(seg, pieces, order, rows, seg_len, padded, width, cols):
    count = len(pieces)

    def kernel(order_ref, seg_ref, *refs):
        parts = refs[:count]
        w_out, xt_out, vec_out, x_scr = refs[count:]
        for k in range(count):
            start = pl.multiple_of(order_ref[k] * rows, 16)
            w_out[pl.ds(start, rows), :] = parts[k][0:rows, :]
        vec = parts[0][rows:, :].astype(F32)
        for k in range(1, count):
            vec = vec + parts[k][rows:, :].astype(F32)
        vec_out[...] = jnp.zeros(vec_out.shape, F32)
        for v in range(5):
            vec_out[v : v + 1, 0:cols] = vec[2 * v : 2 * v + 1, :]
            vec_out[v : v + 1, cols:width] = vec[2 * v + 1 : 2 * v + 2, 0 : width - cols]
        gain = vec_out[0:1, :]
        shift = vec_out[1:2, :]
        step = seg_len // 4

        def body(c, carry):
            at = pl.multiple_of(c * step, 16)
            xhat, _ = norm_parts(seg_ref[pl.ds(at, step), :].astype(F32))
            x_scr[pl.ds(at, step), :] = (xhat * gain + shift).astype(BF16)
            return carry

        lax.fori_loop(0, 4, body, 0)
        x_scr[seg_len:padded, :] = jnp.zeros((padded - seg_len, width), BF16)
        xt_out[...] = x_scr[...].T

    return call(
        kernel,
        (order, seg, *pieces),
        [((width, cols), BF16), ((width, padded), BF16), ((8, width), F32)],
        [pltpu.VMEM((padded, width), BF16)],
        scalars=1,
        name="enter",
    )


def lay_out(pieces, order, parts, vec, width):
    count = len(pieces)
    out_rows, up_rows, down_rows = parts

    def kernel(order_ref, vec_ref, *refs):
        got = refs[:count]
        out_ref, ud_ref = refs[count:]
        up_all = count * up_rows
        down_all = count * down_rows
        for k in range(count):
            o = order_ref[k]
            piece = got[k]
            a, b = out_rows, out_rows + up_rows
            out_ref[pl.ds(pl.multiple_of(o * out_rows, 16), out_rows), :] = piece[0:a, :]
            ud_ref[pl.ds(pl.multiple_of(o * up_rows, 16), up_rows), :] = piece[a:b, :]
            ud_ref[pl.ds(pl.multiple_of(up_all + o * down_rows, 16), down_rows), :] = piece[b:, :]
        ud_ref[up_all + down_all :, :] = jnp.broadcast_to(vec_ref[4:5, :], (EXTRA, width)).astype(BF16)

    return call(
        kernel,
        (order, vec, *pieces),
        [
            ((count * out_rows, width), BF16),
            ((count * (up_rows + down_rows) + EXTRA, width), BF16),
        ],
        scalars=1,
        name="lay_out",
    )


def blocks_of(seg_len):
    return [(s, min(s + BLOCK, seg_len)) for s in range(0, seg_len, BLOCK)]


def one_head(block, h):
    zero = jnp.zeros_like(block)
    return jnp.concatenate([block, zero] if h == 0 else [zero, block], axis=0)


def allowed_slots(live, start, stop):
    place = lax.broadcasted_iota(jnp.int32, (1, BLOCK), 1) + start
    bound = jnp.minimum(place, live - 1)
    return lax.broadcasted_iota(jnp.int32, (stop, BLOCK), 0) <= bound


def attend_forward(live, xt, w, cos, sin, seg_len):
    width, padded = xt.shape
    half = HEAD // 2

    def kernel(live_ref, xt_ref, w_ref, cos_ref, sin_ref, qkv_out, ot_out, mixed_out, lse_out):
        proj = nn(w_ref[0:width, :].T, xt_ref[...])
        cosine = cos_ref[...]
        sine = sin_ref[...]

        def rot(z):
            a, b = z[0:half], z[half:]
            return jnp.concatenate([a * cosine - b * sine, b * cosine + a * sine], axis=0)

        for h in range(2):
            r = h * HEAD
            qkv_out[r : r + HEAD, :] = (rot(proj[r : r + HEAD]) * HEAD ** (-0.5)).astype(BF16)
            r = r + PAIR
            qkv_out[r : r + HEAD, :] = rot(proj[r : r + HEAD]).astype(BF16)
        qkv_out[2 * PAIR :, :] = proj[2 * PAIR :].astype(BF16)
        keys = qkv_out[PAIR : 2 * PAIR, :].T
        lse_out[...] = jnp.zeros(lse_out.shape, F32)
        for start, stop in blocks_of(seg_len):
            cols = slice(start, start + BLOCK)
            allowed = allowed_slots(live_ref[0], start, stop)
            for h in range(2):
                r = h * HEAD
                query = one_head(qkv_out[r : r + HEAD, cols], h)
                scores = jnp.where(allowed, nn(keys[0:stop], query), MASKED)
                top = jnp.max(scores, axis=0, keepdims=True)
                weights = jnp.exp(scores - top)
                total = colsum(weights)
                probs = (weights * (1.0 / total)).astype(BF16)
                value = qkv_out[2 * PAIR + r : 2 * PAIR + r + HEAD, 0:stop]
                ot_out[r : r + HEAD, cols] = nn(value, probs).astype(BF16)
                lse_out[h : h + 1, cols] = top + jnp.log(total)
        mixed_out[...] = ot_out[...].T[0:seg_len]

    return call(
        kernel,
        (live, xt, w, cos, sin),
        [
            ((3 * PAIR, padded), BF16),
            ((PAIR, padded), BF16),
            ((seg_len, PAIR), BF16),
            ((8, padded), F32),
        ],
        scalars=1,
        name="attend_forward",
    )


def emit(whole, pieces, order_ref, spans):
    for k, piece in enumerate(pieces):
        at = 0
        for first, rows in spans:
            start = pl.multiple_of(first + order_ref[k] * rows, 16)
            piece[at : at + rows, :] = whole[pl.ds(start, rows), :]
            at += rows


def attend_backward(live, xt, w, cos, sin, qkv, ot, lse, dot, acc, seg_len):
    width, padded = xt.shape
    half = HEAD // 2
    n_acc = len(acc)

    def kernel(live_ref, xt_ref, w_ref, cos_ref, sin_ref, qkv_ref, ot_ref, lse_ref, dot_ref, *refs):
        acc_refs = refs[:n_acc]
        acc_out, grad_out, d_scr, pg_scr = refs[n_acc:]
        cosine = cos_ref[...]
        sine = sin_ref[...]
        keys = qkv_ref[PAIR : 2 * PAIR, :].T
        values = qkv_ref[2 * PAIR :, :].T
        prod = dot_ref[...].astype(F32) * ot_ref[...].astype(F32)
        inner = [colsum(prod[h * HEAD : h * HEAD + HEAD]) for h in range(2)]
        d_scr[...] = jnp.zeros(d_scr.shape, F32)
        for start, stop in blocks_of(seg_len):
            cols = slice(start, start + BLOCK)
            allowed = allowed_slots(live_ref[0], start, stop)
            for h in range(2):
                r = h * HEAD
                k = PAIR + r
                v = 2 * PAIR + r
                query = qkv_ref[r : r + HEAD, cols]
                out_grad = dot_ref[r : r + HEAD, cols]
                scores = jnp.where(allowed, nn(keys[0:stop], one_head(query, h)), MASKED)
                probs = jnp.exp(scores - lse_ref[h : h + 1, cols])
                prob_grad = nn(values[0:stop], one_head(out_grad, h))
                score_grad = (probs * (prob_grad - inner[h][:, cols])).astype(BF16)
                d_scr[r : r + HEAD, cols] = nn(qkv_ref[k : k + HEAD, 0:stop], score_grad)
                d_scr[k : k + HEAD, 0:stop] += nt(query, score_grad)
                d_scr[v : v + HEAD, 0:stop] += nt(out_grad, probs.astype(BF16))

        def unrot(z):
            a, b = z[0:half], z[half:]
            return jnp.concatenate([a * cosine + b * sine, b * cosine - a * sine], axis=0)

        for h in range(2):
            r = h * HEAD
            pg_scr[r : r + HEAD, :] = (unrot(d_scr[r : r + HEAD, :]) * HEAD ** (-0.5)).astype(BF16)
            r = r + PAIR
            pg_scr[r : r + HEAD, :] = unrot(d_scr[r : r + HEAD, :]).astype(BF16)
        pg_scr[2 * PAIR :, :] = d_scr[2 * PAIR :, :].astype(BF16)
        part = nn(w_ref[0:width, :], pg_scr[...])
        acc_out[...] = acc_refs[0][...] + part if n_acc else part
        grad_out[...] = nt(xt_ref[...], pg_scr[...]).astype(BF16)

    return call(
        kernel,
        (live, xt, w, cos, sin, qkv, ot, lse, dot, *acc),
        [((width, padded), F32), ((width, 3 * PAIR), BF16)],
        [pltpu.VMEM((3 * PAIR, padded), F32), pltpu.VMEM((3 * PAIR, padded), BF16)],
        scalars=1,
        name="attend_backward",
    )


def combine(parts, order, spans, count, keep):
    rows, cols = parts[0].shape
    tail = rows - keep
    piece_rows = sum(r for _, r in spans) + tail

    def kernel(order_ref, *refs):
        got = refs[: len(parts)]
        pieces = refs[len(parts) : -1]
        whole = refs[-1]
        total = got[0][...].astype(F32)
        for p in got[1:]:
            total = total + p[...].astype(F32)
        whole[...] = total.astype(BF16)
        emit(whole, pieces, order_ref, spans)
        if tail:
            for piece in pieces:
                piece[piece_rows - tail :, :] = whole[keep:, :]

    return call(
        kernel,
        (order, *parts),
        [((piece_rows, cols), BF16)] * count,
        [pltpu.VMEM((rows, cols), BF16)],
        scalars=1,
        name="combine",
    )


def merge_attention(seg, mixed, outs, vec):
    rows, width = seg.shape
    n = len(mixed)

    def kernel(seg_ref, vec_ref, *refs):
        mixed_refs, out_refs = refs[:n], refs[n : 2 * n]
        res_out, ffn_out = refs[2 * n :]
        gain = vec_ref[2:3, :]
        shift = vec_ref[3:4, :]
        step = rows // 2

        def body(c, carry):
            at = pl.multiple_of(c * step, 16)
            here = pl.ds(at, step)
            total = nn(mixed_refs[0][here, :], out_refs[0][...])
            for r in range(1, n):
                total = total + nn(mixed_refs[r][here, :], out_refs[r][...])
            total = total + seg_ref[here, :].astype(F32)
            res_out[here, :] = total
            xhat, _ = norm_parts(total)
            ffn_out[here, :] = (xhat * gain + shift).astype(BF16)
            return carry

        lax.fori_loop(0, 2, body, 0)

    return call(
        kernel,
        (seg, vec, *mixed, *outs),
        [((rows, width), F32), ((rows, width), BF16)],
        name="merge_attention",
    )


def feed_forward(ffn_in, cot, ud, acc):
    rows, width = ffn_in.shape
    units = (ud.shape[0] - EXTRA) // 2
    n_acc = len(acc)

    def kernel(x_ref, cot_ref, ud_ref, *refs):
        acc_refs = refs[:n_acc]
        out_acc, back_acc, grad_out, act_scr, pg_scr = refs[n_acc:]
        step = rows // 2
        bias = ud_ref[2 * units : 2 * units + 1, :].astype(F32)

        def body(c, total):
            at = pl.multiple_of(c * step, 16)
            here = pl.ds(at, step)
            up = ud_ref[0:units, :]
            down = ud_ref[units : 2 * units, :]
            pre = nn(x_ref[here, :], up) + bias
            below = 0.5 + 0.5 * lax.erf(pre * 0.5**0.5)
            act = (pre * below).astype(BF16)
            slope = below + pre * (jnp.exp(-0.5 * (pre * pre)) * (1.0 / math.sqrt(2.0 * math.pi)))
            pre_grad = (nt(cot_ref[here, :], down) * slope).astype(BF16)
            act_scr[here, :] = act
            pg_scr[here, :] = pre_grad
            fwd = nn(act, down)
            back = nt(pre_grad, up)
            if n_acc:
                fwd = fwd + acc_refs[0][here, :]
                back = back + acc_refs[1][here, :]
            out_acc[here, :] = fwd
            back_acc[here, :] = back
            return total + colsum(pre_grad.astype(F32))

        total = lax.fori_loop(0, 2, body, jnp.zeros((1, units), F32))
        grad_out[0:units, :] = nn(x_ref[...].T, pg_scr[...]).astype(BF16)
        grad_out[units : 2 * units, :] = nn(act_scr[...].T, cot_ref[...]).astype(BF16)
        grad_out[2 * units :, :] = jnp.broadcast_to(total, (EXTRA, units)).astype(BF16)

    return call(
        kernel,
        (ffn_in, cot, ud, *acc),
        [((rows, width), F32), ((rows, width), F32), ((2 * units + EXTRA, width), BF16)],
        [pltpu.VMEM((rows, units), BF16), pltpu.VMEM((rows, units), BF16)],
        name="feed_forward",
    )


def turn_back(res, forward, backward, cot, vec, mixed_t, outs, padded):
    rows, width = res.shape
    n = len(outs)

    def kernel(res_ref, fwd_ref, back_ref, cot_ref, vec_ref, *refs):
        mixed_refs, out_refs = refs[:n], refs[n : 2 * n]
        block_out, resid_out, vec_out = refs[2 * n : 2 * n + 3]
        grad_outs = refs[2 * n + 3 : 3 * n + 3]
        dot_outs = refs[3 * n + 3 : 4 * n + 3]
        low_scr = refs[-1]
        gain = vec_ref[2:3, :]
        step = rows // 4

        def body(c, sums):
            here = pl.ds(pl.multiple_of(c * step, 16), step)
            res_rows = res_ref[here, :]
            back = back_ref[here, :]
            block_out[here, :] = (res_rows + fwd_ref[here, :]).astype(BF16)
            xhat, rstd = norm_parts(res_rows)
            resid = cot_ref[here, :].astype(F32) + norm_pull(back, gain, xhat, rstd)
            resid_out[here, :] = resid
            low_scr[here, :] = resid.astype(BF16)
            return sums[0] + colsum(back * xhat), sums[1] + colsum(back)

        zero = jnp.zeros((1, width), F32)
        gain_grad, shift_grad = lax.fori_loop(0, 4, body, (zero, zero))
        vec_out[...] = jnp.zeros(vec_out.shape, F32)
        vec_out[0:1, :] = gain_grad
        vec_out[1:2, :] = shift_grad
        low_scr[rows:, :] = jnp.zeros((padded - rows, width), BF16)
        for r in range(n):
            dot_outs[r][...] = nt(out_refs[r][...], low_scr[...]).astype(BF16)
            grad_outs[r][...] = nn(mixed_refs[r][...], low_scr[...]).astype(BF16)

    return call(
        kernel,
        (res, forward, backward, cot, vec, *mixed_t, *outs),
        [((rows, width), BF16), ((rows, width), F32), ((8, width), F32)]
        + [((PAIR, width), BF16)] * n
        + [((PAIR, padded), BF16)] * n,
        [pltpu.VMEM((padded, width), BF16)],
        name="turn_back",
    )


def leave(seg, resid, acc, vec):
    rows, width = seg.shape
    padded = acc.shape[1]

    def kernel(seg_ref, resid_ref, acc_ref, vec_ref, seg_out, vec_out, acc_scr):
        gain = vec_ref[0:1, :]
        step = rows // 4
        acc_scr[...] = acc_ref[...].T

        def body(c, sums):
            here = pl.ds(pl.multiple_of(c * step, 16), step)
            grad = acc_scr[here, :]
            xhat, rstd = norm_parts(seg_ref[here, :].astype(F32))
            seg_out[here, :] = (resid_ref[here, :] + norm_pull(grad, gain, xhat, rstd)).astype(BF16)
            return sums[0] + colsum(grad * xhat), sums[1] + colsum(grad)

        zero = jnp.zeros((1, width), F32)
        gain_grad, shift_grad = lax.fori_loop(0, 4, body, (zero, zero))
        vec_out[...] = jnp.zeros(vec_out.shape, F32)
        vec_out[0:1, :] = gain_grad
        vec_out[1:2, :] = shift_grad

    return call(
        kernel,
        (seg, resid, acc, vec),
        [((rows, width), BF16), ((8, width), F32)],
        [pltpu.VMEM((padded, width), F32)],
        name="leave",
    )


def spread(mine, tensor_index, dtype):
    other = swap(mine, 2)
    near = swap(mine, 1)
    far = swap(other, 1)
    got = [mine, near, other, far]
    odd = (tensor_index & 1) == 1
    high = (tensor_index & 2) == 2
    low = [jnp.where(odd, got[1], got[0]), jnp.where(odd, got[0], got[1])]
    top = [jnp.where(odd, got[3], got[2]), jnp.where(odd, got[2], got[3])]
    out = [jnp.where(high, top[a], low[a]) for a in range(2)]
    out += [jnp.where(high, low[a], top[a]) for a in range(2)]
    return jnp.stack(out).astype(dtype)


def rotary_tables(starts, padded):
    half = HEAD // 2
    inverse = jnp.exp(jnp.arange(half).astype(F32) * (-math.log(10000.0) / half))
    angles = inverse[:, None] * starts.astype(F32)[None, :]
    angles = jnp.pad(angles, ((0, 0), (0, padded - starts.shape[0])))
    return jnp.cos(angles), jnp.sin(angles)


def vector_rows(vectors, here, width, cols):
    rows = []
    for v in vectors:
        full = jnp.zeros((width,), BF16)
        full = lax.dynamic_update_slice(full, v, (here * v.shape[0],))
        rows.append(jnp.pad(full, (0, 2 * cols - width)).reshape(2, cols))
    rows.append(jnp.zeros((EXTRA - 2 * len(vectors), cols), BF16))
    return jnp.concatenate(rows)


def cut(total, here, spans_rows):
    out, at = [], 0
    for rows in spans_rows:
        out.append(total[at : at + rows])
        at += rows
    return out


def local(
    segments,
    seg_start,
    seg_count,
    norm_gain,
    norm_shift,
    qkv_weight,
    out_weight,
    ffn_gain,
    ffn_shift,
    up_weight,
    up_bias,
    down_weight,
    cotangent,
):
    seq_local, seg_len, width = segments.shape
    tensor = lax.axis_size("tensor")
    members = lax.axis_size("dp")
    assert seq_local == tensor == 4
    padded = -(-seg_len // BLOCK) * BLOCK
    radices = digits(members)
    here = lax.axis_index("dp")
    mine = lax.axis_index("tensor")
    cols = 3 * qkv_weight.shape[2]
    assert cols == 3 * PAIR and width * 2 > cols
    groups = range(tensor)

    seg = lax.dynamic_index_in_dim(segments, mine, 0, keepdims=False)
    cot = lax.dynamic_index_in_dim(cotangent, mine, 0, keepdims=False)
    starts = lax.dynamic_index_in_dim(seg_start, mine, 0, keepdims=False)
    live = lax.dynamic_slice_in_dim(seg_count, mine, 1)
    cos, sin = rotary_tables(starts, padded)
    back_order = jnp.stack(behind(radices)).astype(jnp.int32)
    ahead_order = jnp.stack(ahead(radices)).astype(jnp.int32)

    vectors = (norm_gain, norm_shift, ffn_gain, ffn_shift, up_bias)
    first = jnp.concatenate(
        [qkv_weight.reshape(-1, cols), vector_rows(vectors, here, width, cols)]
    )
    second = jnp.concatenate([out_weight, up_weight, down_weight])
    second_parts = (out_weight.shape[0], up_weight.shape[0], down_weight.shape[0])
    got = gather_pieces(first, radices)
    pieces, order, parts = in_place(got, back_order, (qkv_weight.shape[0],))
    w0, xt, vec = enter(seg, pieces, order, parts[0], seg_len, padded, width, cols)
    second, w0 = lax.optimization_barrier((second, w0))
    w = [w0, swap(w0, 1), swap(w0, 2), None]
    w[3] = swap(w[2], 1)
    got = gather_pieces(second, radices)
    pieces, order, parts = in_place(got, back_order, second_parts)
    o0, ud0 = lay_out(pieces, order, parts, vec, width)
    outs = [o0, swap(o0, 1), swap(o0, 2), None]
    outs[3] = swap(outs[2], 1)
    uds = [ud0, swap(ud0, 1), swap(ud0, 2), None]
    uds[3] = swap(uds[2], 1)

    heads = [attend_forward(live, xt, w[r], cos, sin, seg_len) for r in groups]
    res, ffn_in = merge_attention(seg, [h[2] for h in heads], outs, vec)
    acc = ()
    ffn_grads = [None] * 4
    for r in (3, 2, 1, 0):
        out_acc, back_acc, ffn_grads[r] = feed_forward(ffn_in, cot, uds[r], acc)
        acc = (out_acc, back_acc)
    turned = turn_back(res, *acc, cot, vec, [h[1] for h in heads], outs, padded)
    block_mine, resid, ffn_vec = turned[0:3]
    out_grads = turned[3:7]
    dots = turned[7:11]
    block_out = spread(block_mine, mine, BF16)

    def reduced(grads, parts_rows, keep):
        sums = [grads[0], swap(grads[1], 1)]
        two = (grads[2].astype(F32) + swap(grads[3], 1).astype(F32)).astype(BF16)
        sums.append(swap(two, 2))
        whole = grads[0].shape[0]
        thin = not all(rows % 16 == 0 for rows in parts_rows)
        spans, at = [], 0
        for rows in parts_rows:
            spans.append((at, rows))
            at += rows * members
        if not thin:
            pieces = combine(sums, ahead_order, spans, members, keep)
        else:
            total = sum(s.astype(F32) for s in sums).astype(BF16)
            pieces = []
            for k in range(members):
                rows = [
                    lax.dynamic_slice_in_dim(total, first + ahead_order[k] * n, n, 0)
                    for first, n in spans
                ]
                pieces.append(jnp.concatenate(rows + [total[keep:]]))
        total = scatter_pieces(pieces, radices)
        found, at = [], 0
        for rows in parts_rows:
            found.append(total[at : at + rows])
            at += rows
        return found, total[at:]

    (up_g, down_g), bias_rows = reduced(
        ffn_grads, (up_weight.shape[0], down_weight.shape[0]), ffn_grads[0].shape[0] - EXTRA
    )
    bias_g = lax.dynamic_slice_in_dim(bias_rows[0], here * up_bias.shape[0], up_bias.shape[0])
    (out_g,), _ = reduced(out_grads, (out_weight.shape[0],), out_grads[0].shape[0])

    acc = ()
    qkv_grads = [None] * 4
    for r in (3, 2, 1, 0):
        qkv, ot, _, lse = heads[r]
        total, qkv_grads[r] = attend_backward(
            live, xt, w[r], cos, sin, qkv, ot, lse, dots[r], acc, seg_len
        )
        acc = (total,)
    seg_mine, norm_vec = leave(seg, resid, total, vec)
    segments_grad = spread(seg_mine, mine, F32)
    (qkv_g,), _ = reduced(qkv_grads, (qkv_weight.shape[0],), width)

    vecs = jnp.concatenate([norm_vec[0:2], ffn_vec[0:2], jnp.zeros((4, width), F32)])
    vecs = vecs + swap(vecs, 1)
    vecs = vecs + swap(vecs, 2)
    vecs = scatter_pieces([vecs] * members, radices)
    vecs = lax.dynamic_slice_in_dim(vecs, here * norm_gain.shape[0], norm_gain.shape[0], 1)

    return (
        block_out,
        segments_grad,
        vecs[0],
        vecs[1],
        qkv_g.reshape(qkv_weight.shape),
        out_g,
        vecs[2],
        vecs[3],
        up_g,
        bias_g,
        down_g,
    )


def solution(mesh):
    placed = (
        P("dp", None, None),
        P("dp", None),
        P("dp"),
        P("dp"),
        P("dp"),
        P("dp", None, "tensor"),
        P(("tensor", "dp"), None),
        P("dp"),
        P("dp"),
        P("dp", "tensor"),
        P(("tensor", "dp")),
        P(("tensor", "dp"), None),
        P("dp", None, None),
    )
    return jax.shard_map(
        local,
        mesh=mesh,
        in_specs=placed,
        out_specs=(
            P("dp", None, None),
            P("dp", None, None),
            P("dp"),
            P("dp"),
            P("dp", None, "tensor"),
            P(("tensor", "dp"), None),
            P("dp"),
            P("dp"),
            P("dp", "tensor"),
            P(("tensor", "dp")),
            P(("tensor", "dp"), None),
        ),
        check_vma=False,
    )
```

time: 773 us -> 312 us (0.40)
  the two profiles are of different devices: /device:TPU:0 before, /device:TPU:11 now
where the time goes in v1:
time: 312 us; the launch traced here: 308 us
  waiting for transfers between devices  134 us (43%)
  starting transfers between devices  80.9 us (26%)
  Pallas kernels  62 us (20%)
  other arithmetic  16 us (5%)
  local copies, waits for them, and re-layouts  14.2 us (5%)
    ppermute x26, waiting for transfers between devices, swap(): lax.ppermute(value, 'tensor', [(t, t ^ bit) for t in range(lax.axis_size(...  70.5 us
    ppermute x42, waiting for transfers between devices, sent_ahead(): lax.ppermute(value, 'dp', [(i, moved(i, radices, steps)) for i in range(s...  63.5 us
    pallas_call x20, Pallas kernels, call(): pl.pallas_call(kernel, in_specs=inner, out_specs=[pl.BlockSpec(memory_spa...  62 us
    ppermute x42, starting transfers between devices, sent_ahead(): lax.ppermute(value, 'dp', [(i, moved(i, radices, steps)) for i in range(s...  47.1 us
    ppermute x26, starting transfers between devices, swap(): lax.ppermute(value, 'tensor', [(t, t ^ bit) for t in range(lax.axis_size(...  33.7 us
  transfers between devices with their start and end apart: 68, of which 29 were waited for; matrix products, arithmetic and copies ran while one was open for 6% of the time, Pallas kernels for 16%

profile of v1, /device:TPU:11, one launch (start us, length us, event | category | flops | bytes accessed | tf_op | source)
XLA Modules:
  0.0 308.2 jit_solution(13210492779633231573)
XLA Ops:
  31.8 14.7 %collective-permute-done.12.refs_3_ = bf16[144,512]{1,0:T(8,128)(2,1)S(1)} collective-permute-done((bf16[144,512]{1,0:T(8,128)(2,1)S(1)}, bf16[144,512]{1,0:T(8,128)(2,1)S(1)}, u32[]{:S(2)}, u32[]{:S(2)}) %collective-permute-start.12) | collective-permute-done | bytes 147488 | tf_op jit(solution)/shard_map/ppermute | solution.py:70
  56.4 23.3 %collective-permute-done.21.ud_ref = bf16[1040,512]{1,0:T(8,128)(2,1)S(1)} collective-permute-done((bf16[1040,512]{1,0:T(8,128)(2,1)S(1)}, bf16[1040,512]{1,0:T(8,128)(2,1)S(1)}, u32[]{:S(2)}, u32[]{:S(2)}) %collective-permute-start.21) | collective-permute-done | bytes 1064992 | tf_op jit(solution)/shard_map/ppermute | solution.py:106
  84.1 7.1 %collective-permute-done.8.w_ref = bf16[512,384]{1,0:T(8,128)(2,1)S(1)} collective-permute-done((bf16[512,384]{1,0:T(8,128)(2,1)S(1)}, bf16[512,384]{1,0:T(8,128)(2,1)S(1)}, u32[]{:S(2)}, u32[]{:S(2)}) %collective-permute-start.8) | collective-permute-done | bytes 393248 | tf_op jit(solution)/shard_map/ppermute | solution.py:106
  97.2 4.1 %attend_forward.4 = (bf16[384,768]{1,0:T(8,128)(2,1)S(1)}, bf16[128,768]{1,0:T(8,128)(2,1)S(1)}, bf16[704,128]{1,0:T(8,128)(2,1)S(1)}, f32[8,768]{1,0:T(8,128)S(1)}) custom-call(s32[1]{0:T(128)} %dynamic_slice.23.live_ref, bf16[512,768]{1,0:T(8,128)(2,1)S(1)} %get-tuple-element.94.xt_ref, bf16[512,384]{1,0:T(8,128)(2,1)S(1)} %get-tuple-element.96.w_ref, ...), custom_call_target="tpu_custom_call" | custom-call | tf_op jit(solution)/shard_map/attend_forward/pallas_call | solution.py:31
  101.3 4.1 %attend_forward.6 = (bf16[384,768]{1,0:T(8,128)(2,1)S(1)}, bf16[128,768]{1,0:T(8,128)(2,1)S(1)}, bf16[704,128]{1,0:T(8,128)(2,1)S(1)}, f32[8,768]{1,0:T(8,128)S(1)}) custom-call(s32[1]{0:T(128)} %dynamic_slice.23.live_ref, bf16[512,768]{1,0:T(8,128)(2,1)S(1)} %get-tuple-element.94.xt_ref, bf16[512,384]{1,0:T(8,128)(2,1)S(1)} %collective-permute-done.8.w_ref, ...), custom_call_target="tpu_custom_call" | custom-call | tf_op jit(solution)/shard_map/attend_forward/pallas_call | solution.py:31
  105.4 4.2 %attend_forward.5 = (bf16[384,768]{1,0:T(8,128)(2,1)S(1)}, bf16[128,768]{1,0:T(8,128)(2,1)S(1)}, bf16[704,128]{1,0:T(8,128)(2,1)S(1)}, f32[8,768]{1,0:T(8,128)S(1)}) custom-call(s32[1]{0:T(128)} %dynamic_slice.23.live_ref, bf16[512,768]{1,0:T(8,128)(2,1)S(1)} %get-tuple-element.94.xt_ref, bf16[512,384]{1,0:T(8,128)(2,1)S(1)} %collective-permute-done.7.w_ref, ...), custom_call_target="tpu_custom_call" | custom-call | tf_op jit(solution)/shard_map/attend_forward/pallas_call | solution.py:31
  109.6 4.1 %attend_forward.7 = (bf16[384,768]{1,0:T(8,128)(2,1)S(1)}, bf16[128,768]{1,0:T(8,128)(2,1)S(1)}, bf16[704,128]{1,0:T(8,128)(2,1)S(1)}, f32[8,768]{1,0:T(8,128)S(1)}) custom-call(s32[1]{0:T(128)} %dynamic_slice.23.live_ref, bf16[512,768]{1,0:T(8,128)(2,1)S(1)} %get-tuple-element.94.xt_ref, bf16[512,384]{1,0:T(8,128)(2,1)S(1)} %collective-permute-done.9.w_ref, ...), custom_call_target="tpu_custom_call" | custom-call | tf_op jit(solution)/shard_map/attend_forward/pallas_call | solution.py:31
  115.5 4.1 %feed_forward.4 = (f32[704,512]{1,0:T(8,128)S(1)}, f32[704,512]{1,0:T(8,128)S(1)}, bf16[1040,512]{1,0:T(8,128)(2,1)}) custom-call(bf16[704,512]{1,0:T(8,128)(2,1)S(1)} %get-tuple-element.104.x_ref, bf16[704,512]{1,0:T(8,128)(2,1)S(1)} %dynamic-slice_bitcast_fusion.cot_ref, bf16[1040,512]{1,0:T(8,128)(2,1)S(1)} %collective-permute-done.22.ud_ref), custom_call_target="tpu_custom_call" | custom-call | tf_op jit(solution)/shard_map/feed_forward/pallas_call | solution.py:31
  129.0 3.3 %turn_back.1 = (bf16[704,512]{1,0:T(8,128)(2,1)S(1)}, f32[704,512]{1,0:T(8,128)S(1)}, f32[8,512]{1,0:T(8,128)S(1)}, bf16[128,512]{1,0:T(8,128)(2,1)S(1)}, bf16[1...) custom-call(f32[704,512]{1,0:T(8,128)S(1)} %get-tuple-element.103.re, ...), custom_call_target="tpu_custom_call" | custom-call | tf_op jit(solution)/shard_map/turn_back/pallas_call | solution.py:31
  133.0 5.2 %attend_backward.4 = (f32[512,768]{1,0:T(8,128)S(1)}, bf16[512,384]{1,0:T(8,128)(2,1)}) custom-call(s32[1]{0:T(128)} %dynamic_slice.23.live_ref, bf16[512,768]{1,0:T(8,128)(2,1)S(1)} %get-tuple-element.94.xt_ref, bf16[512,384]{1,0:T(8,128)(2,1)S(1)} %collective-permute-done.9.w_ref, f32[32,768]{1,0:T(8,128)S(1)} %get-tuple-element.208.cos_ref, ...), custom_call_target="tpu_custom_call" | custom-call | tf_op jit(solution)/shard_map/attend_backward/pallas_call | solution.py:31
  138.6 4.4 %attend_backward.5 = (f32[512,768]{1,0:T(8,128)S(1)}, bf16[512,384]{1,0:T(8,128)(2,1)S(1)}) custom-call(s32[1]{0:T(128)} %dynamic_slice.23.live_ref, bf16[512,768]{1,0:T(8,128)(2,1)S(1)} %get-tuple-element.94.xt_ref, bf16[512,384]{1,0:T(8,128)(2,1)S(1)} %collective-permute-done.8.w_ref, f32[32,768]{1,0:T(8,128)S(1)} %get-tuple-element.208.cos_ref, ...), custom_call_target="tpu_custom_call" | custom-call | tf_op jit(solution)/shard_map/attend_backward/pallas_call | solution.py:31
  143.1 5.2 %attend_backward.6 = (f32[512,768]{1,0:T(8,128)S(1)}, bf16[512,384]{1,0:T(8,128)(2,1)}) custom-call(s32[1]{0:T(128)} %dynamic_slice.23.live_ref, bf16[512,768]{1,0:T(8,128)(2,1)S(1)} %get-tuple-element.94.xt_ref, bf16[512,384]{1,0:T(8,128)(2,1)S(1)} %collective-permute-done.7.w_ref, f32[32,768]{1,0:T(8,128)S(1)} %get-tuple-element.208.cos_ref, ...), custom_call_target="tpu_custom_call" | custom-call | tf_op jit(solution)/shard_map/attend_backward/pallas_call | solution.py:31
  148.3 4.6 %attend_backward.7 = (f32[512,768]{1,0:T(8,128)S(1)}, bf16[512,384]{1,0:T(8,128)(2,1)S(1)}) custom-call(s32[1]{0:T(128)} %dynamic_slice.23.live_ref, bf16[512,768]{1,0:T(8,128)(2,1)S(1)} %get-tuple-element.94.xt_ref, bf16[512,384]{1,0:T(8,128)(2,1)S(1)} %get-tuple-element.96.w_ref, f32[32,768]{1,0:T(8,128)S(1)} %get-tuple-element.208.cos_ref, ...), custom_call_target="tpu_custom_call" | custom-call | tf_op jit(solution)/shard_map/attend_backward/pallas_call | solution.py:31
  170.7 3.7 %collective-permute-done.34 = f32[8,512]{1,0:T(8,128)S(1)} collective-permute-done((f32[8,512]{1,0:T(8,128)}, f32[8,512]{1,0:T(8,128)S(1)}, u32[]{:S(2)}, u32[]{:S(2)}) %collective-permute-start.34) | collective-permute-done | bytes 16416 | tf_op jit(solution)/shard_map/ppermute | solution.py:70
  174.4 5.9 %collective-permute-start.59 = (bf16[1040,512]{1,0:T(8,128)(2,1)}, bf16[1040,512]{1,0:T(8,128)(2,1)}, u32[]{:S(2)}, u32[]{:S(2)}) collective-permute-start(bf16[1040,512]{1,0:T(8,128)(2,1)} %get-tuple-element.166), channel_id=1, source_target_pairs={{0,1},{1,0},{2,3},{3,2},{4,5},{5,4},{6,7},{7,6},{8,9},{9,8},{10,11... | collective-permute-start | bytes 3194888 | tf_op jit(solution)/shard_map/ppermute | solution.py:106
  189.2 3.2 %collective-permute-start.53 = (bf16[16,512]{1,0:T(8,128)(2,1)S(1)}, bf16[16,512]{1,0:T(8,128)(2,1)S(1)}, u32[]{:S(2)}, u32[]{:S(2)}) collective-permute-start(bf16[16,512]{1,0:T(8,128)(2,1)S(1)} %get-tuple-element.158), channel_id=1, source_target_pairs={{0,12},{4,16},{8,20},{12,24},{16,28},{20,0},{24,4},{28,8},{1,13},{... | collective-permute-start | bytes 49160 | tf_op jit(solution)/shard_map/ppermute | solution.py:70
  193.8 3.3 %collective-permute-start.55 = (bf16[16,512]{1,0:T(8,128)(2,1)S(1)}, bf16[16,512]{1,0:T(8,128)(2,1)S(1)}, u32[]{:S(2)}, u32[]{:S(2)}) collective-permute-start(bf16[16,512]{1,0:T(8,128)(2,1)S(1)} %get-tuple-element.160), channel_id=1, source_target_pairs={{0,20},{4,24},{8,28},{12,0},{16,4},{20,8},{24,12},{28,16},{1,21},{... | collective-permute-start | bytes 49160 | tf_op jit(solution)/shard_map/ppermute | solution.py:70
  198.4 4.4 %collective-permute-start.28 = (bf16[704,512]{1,0:T(8,128)(2,1)}, bf16[704,512]{1,0:T(8,128)(2,1)}, u32[]{:S(2)}, u32[]{:S(2)}) collective-permute-start(bf16[704,512]{1,0:T(8,128)(2,1)} %copy-done.4), channel_id=1, source_target_pairs={{0,1},{1,0},{2,3},{3,2},{4,5},{5,4},{6,7},{7,6},{8,9},{9,8},{10,11... | collective-permute-start | bytes 2162696 | tf_op jit(solution)/shard_map/ppermute | solution.py:106
  209.0 11.0 %collective-permute-done.40.refs_2_ = bf16[512,384]{1,0:T(8,128)(2,1)} collective-permute-done((bf16[512,384]{1,0:T(8,128)(2,1)}, bf16[512,384]{1,0:T(8,128)(2,1)}, u32[]{:S(2)}, u32[]{:S(2)}) %collective-permute-start.40) | collective-permute-done | bytes 393248 | tf_op jit(solution)/shard_map/ppermute | solution.py:106
  228.2 7.2 %collective-permute-done.23 = bf16[704,512]{1,0:T(8,128)(2,1)} collective-permute-done((bf16[704,512]{1,0:T(8,128)(2,1)S(1)}, bf16[704,512]{1,0:T(8,128)(2,1)}, u32[]{:S(2)}, u32[]{:S(2)}) %collective-permute-start.23) | collective-permute-done | bytes 720928 | tf_op jit(solution)/shard_map/ppermute | solution.py:106
  235.5 4.4 %collective-permute-start.27 = (bf16[704,512]{1,0:T(8,128)(2,1)}, bf16[704,512]{1,0:T(8,128)(2,1)S(1)}, u32[]{:S(2)}, u32[]{:S(2)}) collective-permute-start(bf16[704,512]{1,0:T(8,128)(2,1)} %collective-permute-done.26), channel_id=1, source_target_pairs={{0,1},{1,0},{2,3},{3,2},{4,5},{5,4},{6,7},{7,6},{8,9},{9,8},{10,11... | collective-permute-start | bytes 2162696 | tf_op jit(solution)/shard_map/ppermute | solution.py:106
  254.9 19.0 %collective-permute-done.60.refs_2_ = bf16[1040,512]{1,0:T(8,128)(2,1)S(1)} collective-permute-done((bf16[1040,512]{1,0:T(8,128)(2,1)S(1)}, bf16[1040,512]{1,0:T(8,128)(2,1)S(1)}, u32[]{:S(2)}, u32[]{:S(2)}) %collective-permute-start.60) | collective-permute-done | bytes 1064992 | tf_op jit(solution)/shard_map/ppermute | solution.py:106
  288.8 8.3 %collective-permute-done.63 = bf16[144,512]{1,0:T(8,128)(2,1)S(1)} collective-permute-done((bf16[144,512]{1,0:T(8,128)(2,1)S(1)}, bf16[144,512]{1,0:T(8,128)(2,1)S(1)}, u32[]{:S(2)}, u32[]{:S(2)}) %collective-permute-start.63) | collective-permute-done | bytes 147488 | tf_op jit(solution)/shard_map/ppermute | solution.py:70
  300.3 4.0 %collective-permute-done.66 = bf16[144,512]{1,0:T(8,128)(2,1)S(1)} collective-permute-done((bf16[144,512]{1,0:T(8,128)(2,1)S(1)}, bf16[144,512]{1,0:T(8,128)(2,1)S(1)}, u32[]{:S(2)}, u32[]{:S(2)}) %collective-permute-start.66) | collective-permute-done | bytes 147488 | tf_op jit(solution)/shard_map/ppermute | solution.py:70
  (226 shorter events, 144.1 us)
Async XLA Ops:
  25.0 21.5 %collective-permute-start.12 = (bf16[144,512]{1,0:T(8,128)(2,1)S(1)}, bf16[144,512]{1,0:T(8,128)(2,1)S(1)}, u32[]{:S(2)}, u32[]{:S(2)}) collective-permute-start(bf16[144,512]{1,0:T(8,128)(2,1)S(1)} %pad_maximum_fusion.1.refs_0_), channel_id=1, source_target_pairs={{0,12},{4,16},{8,20},{12,24},{16,28},{20,0},{24,4},{28,8},{1,13},{... | collective-permute-start | bytes 442376 | tf_op jit(solution)/shard_map/ppermute | solution.py:70
  28.0 21.7 %collective-permute-start.13 = (bf16[144,512]{1,0:T(8,128)(2,1)S(1)}, bf16[144,512]{1,0:T(8,128)(2,1)S(1)}, u32[]{:S(2)}, u32[]{:S(2)}) collective-permute-start(bf16[144,512]{1,0:T(8,128)(2,1)S(1)} %pad_maximum_fusion.1.refs_0_), channel_id=1, source_target_pairs={{0,16},{4,20},{8,24},{12,28},{16,0},{20,4},{24,8},{28,12},{1,17},{... | collective-permute-start | bytes 442376 | tf_op jit(solution)/shard_map/ppermute | solution.py:70
  28.5 21.2 %collective-permute-start.14 = (bf16[144,512]{1,0:T(8,128)(2,1)S(1)}, bf16[144,512]{1,0:T(8,128)(2,1)S(1)}, u32[]{:S(2)}, u32[]{:S(2)}) collective-permute-start(bf16[144,512]{1,0:T(8,128)(2,1)S(1)} %pad_maximum_fusion.1.refs_0_), channel_id=1, source_target_pairs={{0,20},{4,24},{8,28},{12,0},{16,4},{20,8},{24,12},{28,16},{1,21},{... | collective-permute-start | bytes 442376 | tf_op jit(solution)/shard_map/ppermute | solution.py:70
  29.5 22.5 %collective-permute-start.15 = (bf16[144,512]{1,0:T(8,128)(2,1)S(1)}, bf16[144,512]{1,0:T(8,128)(2,1)S(1)}, u32[]{:S(2)}, u32[]{:S(2)}) collective-permute-start(bf16[144,512]{1,0:T(8,128)(2,1)S(1)} %pad_maximum_fusion.1.refs_0_), channel_id=1, source_target_pairs={{0,24},{4,28},{8,0},{12,4},{16,8},{20,12},{24,16},{28,20},{1,25},{... | collective-permute-start | bytes 442376 | tf_op jit(solution)/shard_map/ppermute | solution.py:70
  31.3 23.1 %collective-permute-start.16 = (bf16[144,512]{1,0:T(8,128)(2,1)S(1)}, bf16[144,512]{1,0:T(8,128)(2,1)S(1)}, u32[]{:S(2)}, u32[]{:S(2)}) collective-permute-start(bf16[144,512]{1,0:T(8,128)(2,1)S(1)} %pad_maximum_fusion.1.refs_0_), channel_id=1, source_target_pairs={{0,28},{4,0},{8,4},{12,8},{16,12},{20,16},{24,20},{28,24},{1,29},{... | collective-permute-start | bytes 442376 | tf_op jit(solution)/shard_map/ppermute | solution.py:70
  55.1 24.7 %collective-permute-start.21 = (bf16[1040,512]{1,0:T(8,128)(2,1)S(1)}, bf16[1040,512]{1,0:T(8,128)(2,1)S(1)}, u32[]{:S(2)}, u32[]{:S(2)}) collective-permute-start(bf16[1040,512]{1,0:T(8,128)(2,1)S(1)} %get-tuple-element.105.ud_ref), channel_id=1, source_target_pairs={{0,2},{1,3},{2,0},{3,1},{4,6},{5,7},{6,4},{7,5},{8,10},{9,11},{10,... | collective-permute-start | bytes 3194888 | tf_op jit(solution)/shard_map/ppermute | solution.py:106
  79.7 35.7 %collective-permute-start.22 = (bf16[1040,512]{1,0:T(8,128)(2,1)S(1)}, bf16[1040,512]{1,0:T(8,128)(2,1)S(1)}, u32[]{:S(2)}, u32[]{:S(2)}) collective-permute-start(bf16[1040,512]{1,0:T(8,128)(2,1)S(1)} %collective-permute-done.21.ud_ref), channel_id=1, source_target_pairs={{0,1},{1,0},{2,3},{3,2},{4,5},{5,4},{6,7},{7,6},{8,9},{9,8},{10,11... | collective-permute-start | bytes 3194888 | tf_op jit(solution)/shard_map/ppermute | solution.py:106
  81.0 41.7 %collective-permute-start.20 = (bf16[1040,512]{1,0:T(8,128)(2,1)S(1)}, bf16[1040,512]{1,0:T(8,128)(2,1)S(1)}, u32[]{:S(2)}, u32[]{:S(2)}) collective-permute-start(bf16[1040,512]{1,0:T(8,128)(2,1)S(1)} %get-tuple-element.105.ud_ref), channel_id=1, source_target_pairs={{0,1},{1,0},{2,3},{3,2},{4,5},{5,4},{6,7},{7,6},{8,9},{9,8},{10,11... | collective-permute-start | bytes 3194888 | tf_op jit(solution)/shard_map/ppermute | solution.py:106
  91.2 18.4 %collective-permute-start.9 = (bf16[512,384]{1,0:T(8,128)(2,1)S(1)}, bf16[512,384]{1,0:T(8,128)(2,1)S(1)}, u32[]{:S(2)}, u32[]{:S(2)}) collective-permute-start(bf16[512,384]{1,0:T(8,128)(2,1)S(1)} %collective-permute-done.8.w_ref), channel_id=1, source_target_pairs={{0,1},{1,0},{2,3},{3,2},{4,5},{5,4},{6,7},{7,6},{8,9},{9,8},{10,11... | collective-permute-start | bytes 1179656 | tf_op jit(solution)/shard_map/ppermute | solution.py:106
  94.0 19.7 %collective-permute-start.17 = (bf16[128,512]{1,0:T(8,128)(2,1)S(1)}, bf16[128,512]{1,0:T(8,128)(2,1)S(1)}, u32[]{:S(2)}, u32[]{:S(2)}) collective-permute-start(bf16[128,512]{1,0:T(8,128)(2,1)S(1)} %get-tuple-element.102.refs_4_), channel_id=1, source_target_pairs={{0,1},{1,0},{2,3},{3,2},{4,5},{5,4},{6,7},{7,6},{8,9},{9,8},{10,11... | collective-permute-start | bytes 393224 | tf_op jit(solution)/shard_map/ppermute | solution.py:106
  132.4 23.3 %collective-permute-start.49 = (bf16[128,512]{1,0:T(8,128)(2,1)S(1)}, bf16[128,512]{1,0:T(8,128)(2,1)S(1)}, u32[]{:S(2)}, u32[]{:S(2)}) collective-permute-start(bf16[128,512]{1,0:T(8,128)(2,1)S(1)} %get-tuple-element.154), channel_id=1, source_target_pairs={{0,1},{1,0},{2,3},{3,2},{4,5},{5,4},{6,7},{7,6},{8,9},{9,8},{10,11... | collective-permute-start | bytes 393224 | tf_op jit(solution)/shard_map/ppermute | solution.py:106
  132.9 47.3 %collective-permute-start.48 = (bf16[128,512]{1,0:T(8,128)(2,1)S(1)}, bf16[128,512]{1,0:T(8,128)(2,1)S(1)}, u32[]{:S(2)}, u32[]{:S(2)}) collective-permute-start(bf16[128,512]{1,0:T(8,128)(2,1)S(1)} %get-tuple-element.152), channel_id=1, source_target_pairs={{0,1},{1,0},{2,3},{3,2},{4,5},{5,4},{6,7},{7,6},{8,9},{9,8},{10,11... | collective-permute-start | bytes 393224 | tf_op jit(solution)/shard_map/ppermute | solution.py:106
  138.2 64.5 %collective-permute-start.39 = (bf16[512,384]{1,0:T(8,128)(2,1)}, bf16[512,384]{1,0:T(8,128)(2,1)}, u32[]{:S(2)}, u32[]{:S(2)}) collective-permute-start(bf16[512,384]{1,0:T(8,128)(2,1)} %get-tuple-element.142), channel_id=1, source_target_pairs={{0,1},{1,0},{2,3},{3,2},{4,5},{5,4},{6,7},{7,6},{8,9},{9,8},{10,11... | collective-permute-start | bytes 1179656 | tf_op jit(solution)/shard_map/ppermute | solution.py:106
  155.7 26.0 %collective-permute-start.50 = (bf16[128,512]{1,0:T(8,128)(2,1)S(1)}, bf16[128,512]{1,0:T(8,128)(2,1)S(1)}, u32[]{:S(2)}, u32[]{:S(2)}) collective-permute-start(bf16[128,512]{1,0:T(8,128)(2,1)S(1)} %add_convert_fusion.2), channel_id=1, source_target_pairs={{0,2},{1,3},{2,0},{3,1},{4,6},{5,7},{6,4},{7,5},{8,10},{9,11},{10,... | collective-permute-start | bytes 393224 | tf_op jit(solution)/shard_map/ppermute | solution.py:106
  161.4 46.7 %collective-permute-start.38 = (bf16[512,384]{1,0:T(8,128)(2,1)}, bf16[512,384]{1,0:T(8,128)(2,1)}, u32[]{:S(2)}, u32[]{:S(2)}) collective-permute-start(bf16[512,384]{1,0:T(8,128)(2,1)} %get-tuple-element.140), channel_id=1, source_target_pairs={{0,1},{1,0},{2,3},{3,2},{4,5},{5,4},{6,7},{7,6},{8,9},{9,8},{10,11... | collective-permute-start | bytes 1179656 | tf_op jit(solution)/shard_map/ppermute | solution.py:106
  174.4 68.6 %collective-permute-start.59 = (bf16[1040,512]{1,0:T(8,128)(2,1)}, bf16[1040,512]{1,0:T(8,128)(2,1)}, u32[]{:S(2)}, u32[]{:S(2)}) collective-permute-start(bf16[1040,512]{1,0:T(8,128)(2,1)} %get-tuple-element.166), channel_id=1, source_target_pairs={{0,1},{1,0},{2,3},{3,2},{4,5},{5,4},{6,7},{7,6},{8,9},{9,8},{10,11... | collective-permute-start | bytes 3194888 | tf_op jit(solution)/shard_map/ppermute | solution.py:106
  197.1 27.5 %collective-permute-start.26 = (bf16[704,512]{1,0:T(8,128)(2,1)}, bf16[704,512]{1,0:T(8,128)(2,1)}, u32[]{:S(2)}, u32[]{:S(2)}) collective-permute-start(bf16[704,512]{1,0:T(8,128)(2,1)} %copy-done.4), channel_id=1, source_target_pairs={{0,2},{1,3},{2,0},{3,1},{4,6},{5,7},{6,4},{7,5},{8,10},{9,11},{10,... | collective-permute-start | bytes 2162696 | tf_op jit(solution)/shard_map/ppermute | solution.py:106
  198.4 28.2 %collective-permute-start.28 = (bf16[704,512]{1,0:T(8,128)(2,1)}, bf16[704,512]{1,0:T(8,128)(2,1)}, u32[]{:S(2)}, u32[]{:S(2)}) collective-permute-start(bf16[704,512]{1,0:T(8,128)(2,1)} %copy-done.4), channel_id=1, source_target_pairs={{0,1},{1,0},{2,3},{3,2},{4,5},{5,4},{6,7},{7,6},{8,9},{9,8},{10,11... | collective-permute-start | bytes 2162696 | tf_op jit(solution)/shard_map/ppermute | solution.py:106
  208.1 27.4 %collective-permute-start.23 = (bf16[704,512]{1,0:T(8,128)(2,1)S(1)}, bf16[704,512]{1,0:T(8,128)(2,1)}, u32[]{:S(2)}, u32[]{:S(2)}) collective-permute-start(bf16[704,512]{1,0:T(8,128)(2,1)S(1)} %get-tuple-element.118), channel_id=1, source_target_pairs={{0,2},{1,3},{2,0},{3,1},{4,6},{5,7},{6,4},{7,5},{8,10},{9,11},{10,... | collective-permute-start | bytes 2162696 | tf_op jit(solution)/shard_map/ppermute | solution.py:106
  249.3 24.6 %collective-permute-start.60 = (bf16[1040,512]{1,0:T(8,128)(2,1)S(1)}, bf16[1040,512]{1,0:T(8,128)(2,1)S(1)}, u32[]{:S(2)}, u32[]{:S(2)}) collective-permute-start(bf16[1040,512]{1,0:T(8,128)(2,1)S(1)} %add_convert_fusion), channel_id=1, source_target_pairs={{0,2},{1,3},{2,0},{3,1},{4,6},{5,7},{6,4},{7,5},{8,10},{9,11},{10,... | collective-permute-start | bytes 3194888 | tf_op jit(solution)/shard_map/ppermute | solution.py:106
  281.5 18.8 %collective-permute-start.64 = (bf16[144,512]{1,0:T(8,128)(2,1)S(1)}, bf16[144,512]{1,0:T(8,128)(2,1)S(1)}, u32[]{:S(2)}, u32[]{:S(2)}) collective-permute-start(bf16[144,512]{1,0:T(8,128)(2,1)S(1)} %get-tuple-element.171), channel_id=1, source_target_pairs={{0,16},{4,20},{8,24},{12,28},{16,0},{20,4},{24,8},{28,12},{1,17},{... | collective-permute-start | bytes 442376 | tf_op jit(solution)/shard_map/ppermute | solution.py:70
  281.5 18.8 %collective-permute-start.65 = (bf16[144,512]{1,0:T(8,128)(2,1)S(1)}, bf16[144,512]{1,0:T(8,128)(2,1)S(1)}, u32[]{:S(2)}, u32[]{:S(2)}) collective-permute-start(bf16[144,512]{1,0:T(8,128)(2,1)S(1)} %get-tuple-element.172), channel_id=1, source_target_pairs={{0,20},{4,24},{8,28},{12,0},{16,4},{20,8},{24,12},{28,16},{1,21},{... | collective-permute-start | bytes 442376 | tf_op jit(solution)/shard_map/ppermute | solution.py:70
  282.8 21.6 %collective-permute-start.66 = (bf16[144,512]{1,0:T(8,128)(2,1)S(1)}, bf16[144,512]{1,0:T(8,128)(2,1)S(1)}, u32[]{:S(2)}, u32[]{:S(2)}) collective-permute-start(bf16[144,512]{1,0:T(8,128)(2,1)S(1)} %get-tuple-element.173), channel_id=1, source_target_pairs={{0,24},{4,28},{8,0},{12,4},{16,8},{20,12},{24,16},{28,20},{1,25},{... | collective-permute-start | bytes 442376 | tf_op jit(solution)/shard_map/ppermute | solution.py:70
  284.4 22.2 %collective-permute-start.67 = (bf16[144,512]{1,0:T(8,128)(2,1)S(1)}, bf16[144,512]{1,0:T(8,128)(2,1)S(1)}, u32[]{:S(2)}, u32[]{:S(2)}) collective-permute-start(bf16[144,512]{1,0:T(8,128)(2,1)S(1)} %get-tuple-element.174), channel_id=1, source_target_pairs={{0,28},{4,0},{8,4},{12,8},{16,12},{20,16},{24,20},{28,24},{1,29},{... | collective-permute-start | bytes 442376 | tf_op jit(solution)/shard_map/ppermute | solution.py:70
  (63 other events, 577.1 us)

commit v2 on v1

v2 whole, which is shorter than its diff:
```python
import math

import jax
import jax.numpy as jnp
from jax import lax
from jax.experimental import pallas as pl
from jax.experimental.pallas import tpu as pltpu
from jax.sharding import PartitionSpec as P

HEAD = 64
PAIR = 2 * HEAD
BLOCK = 256
EPSILON = 1e-05
MASKED = -1e30
BF16 = jnp.bfloat16
F32 = jnp.float32
EXTRA = 16


def nn(a, b):
    return lax.dot_general(a, b, (((1,), (0,)), ((), ())), preferred_element_type=F32)


def nt(a, b):
    return lax.dot_general(a, b, (((1,), (1,)), ((), ())), preferred_element_type=F32)


def call(kernel, operands, outs, scratch=(), scalars=0, name=None, us=1.0, specs=None):
    inner = [pl.BlockSpec(memory_space=pltpu.SMEM) for _ in range(scalars)]
    inner += [pl.BlockSpec(memory_space=pltpu.VMEM) for _ in operands[scalars:]]
    for at, spec in (specs or {}).items():
        inner[at] = spec
    moved = sum(math.prod(s) * jnp.dtype(d).itemsize for s, d in outs)
    return pl.pallas_call(
        kernel,
        grid=(1,),
        in_specs=inner,
        out_specs=[pl.BlockSpec(memory_space=pltpu.VMEM) for _ in outs],
        out_shape=[jax.ShapeDtypeStruct(s, d) for s, d in outs],
        scratch_shapes=list(scratch),
        compiler_params=pltpu.CompilerParams(vmem_limit_bytes=20 * 1024 * 1024),
        cost_estimate=pl.CostEstimate(
            flops=int(us * 1.1e9), bytes_accessed=int(min(2 * moved, us * 3e6)), transcendentals=0
        ),
        name=name,
    )(*operands)


def bits_of(size):
    assert size & (size - 1) == 0
    return [size >> (k + 1) for k in range(size.bit_length() - 1)]


def across(value, bit):
    return lax.ppermute(value, "dp", [(i, i ^ bit) for i in range(lax.axis_size("dp"))])


def joined(arrays):
    return arrays[0] if len(arrays) == 1 else jnp.concatenate(arrays)


def widened(arrays, order, bit, step=across):
    whole = joined(arrays)
    return [whole, step(whole, bit)], order + [o ^ bit for o in order]


def halving_order(bits):
    order = [0]
    for bit in reversed(bits):
        order = order + [o ^ bit for o in order]
    return order


def swap(value, bit):
    return lax.ppermute(value, "tensor", [(t, t ^ bit) for t in range(lax.axis_size("tensor"))])


def gate(value, *earlier):
    return lax.optimization_barrier((value, *earlier))


class Held:
    def __init__(self, kept):
        self.kept = kept


class Halving(Held):
    def __init__(self, halves, steps):
        self.kept, self.sent = halves
        self.steps = list(steps)

    def step(self, *earlier):
        (move, bit), *self.steps = self.steps
        got, *kept = gate(move(self.sent, bit), *(e.kept for e in earlier))
        for e, k in zip(earlier, kept):
            e.kept = k
        if self.steps:
            half = self.kept.shape[0] // 2
            parts = [slice(None, half), slice(half, None)]
            self.kept, self.sent = (
                (self.kept[p].astype(F32) + got[p].astype(F32)).astype(BF16) for p in parts
            )
        else:
            self.kept, self.sent = self.kept[0].astype(F32) + got[0].astype(F32), None
        return self


def in_place(arrays, order, parts):
    if all(rows % 16 == 0 for rows in parts):
        return arrays, order, parts
    count = order.shape[0]
    stacked = joined(arrays)
    where = jnp.zeros((count,), jnp.int32).at[order].set(jnp.arange(count, dtype=jnp.int32))
    stacked = stacked[where]
    laid, at = [], 0
    for rows in parts:
        laid.append(stacked[:, at : at + rows].reshape(count * rows, -1))
        at += rows
    if at < stacked.shape[1]:
        laid.append(stacked[:, at:].astype(F32).sum(axis=0).astype(stacked.dtype))
    whole = jnp.concatenate(laid)[None]
    return [whole], jnp.zeros((1,), jnp.int32), [count * r for r in parts]


def norm_parts(rows):
    centred = rows - jnp.mean(rows, axis=-1, keepdims=True)
    rstd = lax.rsqrt(jnp.mean(centred * centred, axis=-1, keepdims=True) + EPSILON)
    return centred * rstd, rstd


def norm_pull(grad, gain, xhat, rstd):
    scaled = grad * gain
    level = jnp.mean(scaled, axis=-1, keepdims=True)
    along = jnp.mean(scaled * xhat, axis=-1, keepdims=True)
    return rstd * (scaled - level - xhat * along)


def colsum(rows):
    return jnp.sum(rows, axis=0, keepdims=True)


def each_piece(refs):
    k = 0
    for ref in refs:
        for j in range(ref.shape[0]):
            yield k, ref, j
            k += 1


def enter(seg, arrays, order, rows, seg_len, padded, width, cols):
    count = len(arrays)

    def kernel(order_ref, seg_ref, *refs):
        parts = refs[:count]
        w_out, xt_out, vec_out, x_scr = refs[count:]
        vec = 0.0
        for k, ref, j in each_piece(parts):
            start = pl.multiple_of(order_ref[k] * rows, 16)
            w_out[pl.ds(start, rows), :] = ref[j, 0:rows, :]
            vec = vec + ref[j, rows:, :].astype(F32)
        w_out[width:, :] = vec.astype(BF16)
        vec_out[...] = jnp.zeros(vec_out.shape, F32)
        for v in range(4):
            vec_out[v : v + 1, 0:cols] = vec[2 * v : 2 * v + 1, :]
            vec_out[v : v + 1, cols:width] = vec[2 * v + 1 : 2 * v + 2, 0 : width - cols]
        gain = vec_out[0:1, :]
        shift = vec_out[1:2, :]
        step = seg_len // 4

        def body(c, carry):
            at = pl.multiple_of(c * step, 16)
            xhat, _ = norm_parts(seg_ref[pl.ds(at, step), :].astype(F32))
            x_scr[pl.ds(at, step), :] = (xhat * gain + shift).astype(BF16)
            return carry

        lax.fori_loop(0, 4, body, 0)
        x_scr[seg_len:padded, :] = jnp.zeros((padded - seg_len, width), BF16)
        xt_out[...] = x_scr[...].T

    return call(
        kernel,
        (order, seg, *arrays),
        [((width + EXTRA, cols), BF16), ((width, padded), BF16), ((8, width), F32)],
        [pltpu.VMEM((padded, width), BF16)],
        scalars=1,
        name="enter",
        us=2.0,
    )


def lay_out(first, second, orders, parts, w, width):
    n_first, n_second = len(first), len(second)
    (out_rows, up_rows), (down_rows,) = parts
    cols = w.shape[1]
    counts = [sum(a.shape[0] for a in first), sum(a.shape[0] for a in second)]
    up_at = counts[0] * out_rows
    down_at = up_at + counts[0] * up_rows
    bias_at = down_at + counts[1] * down_rows

    def kernel(first_order, second_order, w_ref, *refs):
        wide = refs[-1]
        for k, ref, j in each_piece(refs[:n_first]):
            o = first_order[k]
            wide[pl.ds(pl.multiple_of(o * out_rows, 16), out_rows), :] = ref[j, 0:out_rows, :]
            start = pl.multiple_of(up_at + o * up_rows, 16)
            wide[pl.ds(start, up_rows), :] = ref[j, out_rows:, :]
        for k, ref, j in each_piece(refs[n_first : n_first + n_second]):
            start = pl.multiple_of(down_at + second_order[k] * down_rows, 16)
            wide[pl.ds(start, down_rows), :] = ref[j]
        bias = jnp.concatenate([w_ref[8:9, :], w_ref[9:10, 0 : width - cols]], axis=1)
        wide[bias_at:, :] = jnp.broadcast_to(bias, (EXTRA, width))

    return call(
        kernel,
        (*orders, w, *first, *second),
        [((bias_at + EXTRA, width), BF16)],
        scalars=2,
        name="lay_out",
        us=1.0,
        specs={2: pl.BlockSpec((EXTRA, cols), lambda i: (width // EXTRA, 0))},
    )[0]


def blocks_of(seg_len):
    return [(s, min(s + BLOCK, seg_len)) for s in range(0, seg_len, BLOCK)]


def one_head(block, h):
    row = lax.broadcasted_iota(jnp.int32, block.shape, 0)
    return jnp.where(row // HEAD == h, block, jnp.zeros_like(block))


def allowed_slots(live, start, stop):
    place = lax.broadcasted_iota(jnp.int32, (1, BLOCK), 1) + start
    bound = jnp.minimum(place, live - 1)
    return lax.broadcasted_iota(jnp.int32, (stop, BLOCK), 0) <= bound


def attend_forward(live, xt, w, cos, sin, seg_len):
    width, padded = xt.shape
    half = HEAD // 2

    def kernel(live_ref, xt_ref, w_ref, cos_ref, sin_ref, qkv_out, ot_out, mixed_out, lse_out):
        proj = nn(w_ref[0:width, :].T, xt_ref[...])
        cosine = cos_ref[...]
        sine = sin_ref[...]

        def rot(z):
            a, b = z[0:half], z[half:]
            return jnp.concatenate([a * cosine - b * sine, b * cosine + a * sine], axis=0)

        for h in range(2):
            r = h * HEAD
            qkv_out[r : r + HEAD, :] = (rot(proj[r : r + HEAD]) * HEAD ** (-0.5)).astype(BF16)
            r = r + PAIR
            qkv_out[r : r + HEAD, :] = rot(proj[r : r + HEAD]).astype(BF16)
        qkv_out[2 * PAIR :, :] = proj[2 * PAIR :].astype(BF16)
        keys = qkv_out[PAIR : 2 * PAIR, :].T
        lse_out[...] = jnp.zeros(lse_out.shape, F32)
        def head(h, carry):
            r = pl.multiple_of(h * HEAD, HEAD)
            for start, stop in blocks_of(seg_len):
                cols = slice(start, start + BLOCK)
                allowed = allowed_slots(live_ref[0], start, stop)
                query = one_head(qkv_out[0:PAIR, cols], h)
                scores = jnp.where(allowed, nn(keys[0:stop], query), MASKED)
                top = jnp.max(scores, axis=0, keepdims=True)
                weights = jnp.exp(scores - top)
                total = colsum(weights)
                probs = (weights * (1.0 / total)).astype(BF16)
                value = qkv_out[pl.ds(2 * PAIR + r, HEAD), 0:stop]
                ot_out[pl.ds(r, HEAD), cols] = nn(value, probs).astype(BF16)
                lse_out[pl.ds(h, 1), cols] = top + jnp.log(total)
            return carry

        lax.fori_loop(0, 2, head, 0)
        mixed_out[...] = ot_out[...].T[0:seg_len]

    return call(
        kernel,
        (live, xt, w, cos, sin),
        [
            ((3 * PAIR, padded), BF16),
            ((PAIR, padded), BF16),
            ((seg_len, PAIR), BF16),
            ((8, padded), F32),
        ],
        scalars=1,
        name="attend_forward",
        us=4.0,
    )


def emit(cut, order_ref, kept, sent):
    half = kept.shape[0]
    for k in range(2 * half):
        target, j = (kept, k) if k < half else (sent, k - half)
        cut(order_ref[k], target.at[j])


def attend_backward(live, xt, w, cos, sin, qkv, ot, lse, dot, acc, seg_len):
    width, padded = xt.shape
    half = HEAD // 2
    n_acc = len(acc)

    def kernel(live_ref, xt_ref, w_ref, cos_ref, sin_ref, qkv_ref, ot_ref, lse_ref, dot_ref, *refs):
        acc_refs = refs[:n_acc]
        acc_out, grad_out, d_scr, pg_scr, inner_scr = refs[n_acc:]
        cosine = cos_ref[...]
        sine = sin_ref[...]
        keys = qkv_ref[PAIR : 2 * PAIR, :].T
        values = qkv_ref[2 * PAIR :, :].T
        prod = dot_ref[...].astype(F32) * ot_ref[...].astype(F32)
        d_scr[...] = jnp.zeros(d_scr.shape, F32)
        for h in range(2):
            inner_scr[h : h + 1, :] = colsum(prod[h * HEAD : h * HEAD + HEAD])

        def head(h, carry):
            r = pl.multiple_of(h * HEAD, HEAD)
            q_at, k_at, v_at = (pl.ds(part * PAIR + r, HEAD) for part in range(3))
            for start, stop in blocks_of(seg_len):
                cols = slice(start, start + BLOCK)
                allowed = allowed_slots(live_ref[0], start, stop)
                query = one_head(qkv_ref[0:PAIR, cols], h)
                scores = jnp.where(allowed, nn(keys[0:stop], query), MASKED)
                probs = jnp.exp(scores - lse_ref[pl.ds(h, 1), cols])
                prob_grad = nn(values[0:stop], one_head(dot_ref[:, cols], h))
                score_grad = (probs * (prob_grad - inner_scr[pl.ds(h, 1), cols])).astype(BF16)
                d_scr[q_at, cols] = nn(qkv_ref[k_at, 0:stop], score_grad)
                d_scr[k_at, 0:stop] += nt(qkv_ref[q_at, cols], score_grad)
                d_scr[v_at, 0:stop] += nt(dot_ref[pl.ds(r, HEAD), cols], probs.astype(BF16))
            return carry

        lax.fori_loop(0, 2, head, 0)

        def unrot(z):
            a, b = z[0:half], z[half:]
            return jnp.concatenate([a * cosine + b * sine, b * cosine - a * sine], axis=0)

        for h in range(2):
            r = h * HEAD
            pg_scr[r : r + HEAD, :] = (unrot(d_scr[r : r + HEAD, :]) * HEAD ** (-0.5)).astype(BF16)
            r = r + PAIR
            pg_scr[r : r + HEAD, :] = unrot(d_scr[r : r + HEAD, :]).astype(BF16)
        pg_scr[2 * PAIR :, :] = d_scr[2 * PAIR :, :].astype(BF16)
        part = nn(w_ref[0:width, :], pg_scr[...])
        acc_out[...] = acc_refs[0][...] + part if n_acc else part
        grad_out[...] = nt(xt_ref[...], pg_scr[...]).astype(BF16)

    return call(
        kernel,
        (live, xt, w, cos, sin, qkv, ot, lse, dot, *acc),
        [((width, padded), F32), ((width, 3 * PAIR), BF16)],
        [
            pltpu.VMEM((3 * PAIR, padded), F32),
            pltpu.VMEM((3 * PAIR, padded), BF16),
            pltpu.VMEM((8, padded), F32),
        ],
        scalars=1,
        name="attend_backward",
        us=1.0,
    )


def rows_of(whole, first, index, rows):
    return whole[pl.ds(pl.multiple_of(first + index * rows, 16), rows), :]


def halves_call(kernel, operands, count, rows, cols, scratch, name):
    return call(
        kernel,
        operands,
        [((count // 2, rows, cols), BF16)] * 2,
        scratch,
        scalars=1,
        name=name,
        us=1.5,
    )


def cut_heads(grads, vec, order, rows):
    whole_rows, cols = grads[0].shape
    width = vec.shape[1]
    count = order.shape[0]

    def kernel(order_ref, a_ref, b_ref, c_ref, vec_ref, kept, sent, whole):
        whole[...] = (a_ref[...].astype(F32) + b_ref[...].astype(F32) + c_ref[...].astype(F32)).astype(BF16)
        tail = jnp.zeros((EXTRA - 4, cols), F32)
        blank = jnp.zeros((1, 2 * cols - width), F32)
        v0, v1 = vec_ref[0:1, :], vec_ref[1:2, :]
        parts = []
        for v in (v0, v1):
            parts.append(v[:, 0:cols])
            parts.append(jnp.concatenate([v[:, cols:width], blank], axis=1))
        last = jnp.concatenate(parts + [tail], axis=0).astype(BF16)

        def cut(index, piece):
            piece[0:rows, :] = rows_of(whole, 0, index, rows)
            piece[rows:, :] = last

        emit(cut, order_ref, kept, sent)

    return halves_call(
        kernel,
        (order, *grads, vec),
        count,
        rows + EXTRA,
        cols,
        [pltpu.VMEM((whole_rows, cols), BF16)],
        "cut_heads",
    )


def cut_down(downs, outs, out_near, order, down_rows, out_rows):
    width = downs[0].shape[1]
    count = order.shape[0]
    down = down_rows * count
    tall = out_rows * count + EXTRA
    end = down + tall - EXTRA

    def kernel(order_ref, *refs):
        down_refs, out_refs = refs[0:2], refs[2:4]
        near_ref, kept, sent = refs[4:7]
        wholes = refs[7:9]
        for side, whole in enumerate(wholes):
            near = near_ref[side * tall : (side + 1) * tall, :].astype(F32)
            outs_sum = out_refs[side][...].astype(F32) + near
            whole[0 : tall - EXTRA, :] = outs_sum[0 : tall - EXTRA].astype(BF16)
            bias = down_refs[side][down:, :].astype(F32)
            whole[tall - EXTRA :, :] = (outs_sum[tall - EXTRA :] + bias).astype(BF16)
        half = kept.shape[0]
        for k in range(count):
            for side, whole in enumerate(wholes):
                j = 2 * k + side
                target, j = (kept, j) if j < half else (sent, j - half)
                index = order_ref[k]
                target[j, 0:down_rows, :] = rows_of(down_refs[side], 0, index, down_rows)
                target[j, down_rows : down_rows + out_rows, :] = rows_of(whole, 0, index, out_rows)
                target[j, down_rows + out_rows :, :] = whole[tall - EXTRA :, :]

    return halves_call(
        kernel,
        (order, *downs, *outs, out_near),
        2 * count,
        down_rows + out_rows + EXTRA,
        width,
        [pltpu.VMEM((tall, width), BF16)] * 2,
        "cut_down",
    )


def cut_up(grads, order, rows):
    height, width = grads[0].shape
    count = order.shape[0]
    whole_rows = rows * count

    def kernel(order_ref, a_ref, b_ref, c_ref, d_ref, kept, sent, rest_near, rest_far, near, far):
        here = slice(0, whole_rows)
        rest = slice(whole_rows, height)
        for x_ref, y_ref, up, other in ((a_ref, b_ref, near, rest_near), (c_ref, d_ref, far, rest_far)):
            up[...] = (x_ref[here, :].astype(F32) + y_ref[here, :].astype(F32)).astype(BF16)
            other[...] = (x_ref[rest, :].astype(F32) + y_ref[rest, :].astype(F32)).astype(BF16)
        half = kept.shape[0]
        for k in range(count):
            for side, whole in enumerate((near, far)):
                j = 2 * k + side
                target, j = (kept, j) if j < half else (sent, j - half)
                target[j] = rows_of(whole, 0, order_ref[k], rows)

    kept, sent, *rest = call(
        kernel,
        (order, *grads),
        [((count, rows, width), BF16)] * 2 + [((height - whole_rows, width), BF16)] * 2,
        [pltpu.VMEM((whole_rows, width), BF16)] * 2,
        scalars=1,
        name="cut_up",
        us=1.5,
    )
    return (kept, sent), rest


def cut_thin(totals, order, spans, last):
    pieces = []
    for k in range(order.shape[0]):
        for total in totals:
            piece = [
                lax.dynamic_slice_in_dim(total, first + order[k] * rows, rows, 0)
                for first, rows in spans
            ]
            pieces.append(jnp.concatenate(piece + ([total[-EXTRA:]] if last is None else last)))
    pieces = jnp.stack(pieces)
    half = pieces.shape[0] // 2
    return pieces[:half], pieces[half:]


def added(arrays):
    return sum(a.astype(F32) for a in arrays).astype(BF16)


def merge_attention(seg, mixed, outs, vec):
    rows, width = seg.shape
    n = len(mixed)

    def kernel(seg_ref, vec_ref, *refs):
        mixed_refs, out_refs = refs[:n], refs[n : 2 * n]
        res_out, ffn_out = refs[2 * n :]
        gain = vec_ref[2:3, :]
        shift = vec_ref[3:4, :]
        step = rows // 2

        def body(c, carry):
            at = pl.multiple_of(c * step, 16)
            here = pl.ds(at, step)
            total = nn(mixed_refs[0][here, :], out_refs[0][...])
            for r in range(1, n):
                total = total + nn(mixed_refs[r][here, :], out_refs[r][...])
            total = total + seg_ref[here, :].astype(F32)
            res_out[here, :] = total
            xhat, _ = norm_parts(total)
            ffn_out[here, :] = (xhat * gain + shift).astype(BF16)
            return carry

        lax.fori_loop(0, 2, body, 0)

    return call(
        kernel,
        (seg, vec, *mixed, *outs),
        [((rows, width), F32), ((rows, width), BF16)],
        name="merge_attention",
        us=2.0,
        specs={2 + n + r: pl.BlockSpec((PAIR, width), lambda i: (0, 0)) for r in range(n)},
    )


def feed_forward(ffn_in, cot, wide, acc):
    rows, width = ffn_in.shape
    units = (wide.shape[0] - EXTRA - PAIR) // 2
    up_at, down_at, bias_at = PAIR, PAIR + units, PAIR + 2 * units
    n_acc = len(acc)

    def kernel(x_ref, cot_ref, ud_ref, *refs):
        acc_refs = refs[:n_acc]
        out_acc, back_acc, grad_out, act_scr, pg_scr = refs[n_acc:]
        step = rows // 2
        bias = ud_ref[bias_at : bias_at + 1, :].astype(F32)

        def body(c, total):
            at = pl.multiple_of(c * step, 16)
            here = pl.ds(at, step)
            up = ud_ref[up_at:down_at, :]
            down = ud_ref[down_at:bias_at, :]
            pre = nn(x_ref[here, :], up) + bias
            below = 0.5 + 0.5 * lax.erf(pre * 0.5**0.5)
            act = (pre * below).astype(BF16)
            slope = below + pre * (jnp.exp(-0.5 * (pre * pre)) * (1.0 / math.sqrt(2.0 * math.pi)))
            pre_grad = (nt(cot_ref[here, :], down) * slope).astype(BF16)
            act_scr[here, :] = act
            pg_scr[here, :] = pre_grad
            fwd = nn(act, down)
            back = nt(pre_grad, up)
            if n_acc:
                fwd = fwd + acc_refs[0][here, :]
                back = back + acc_refs[1][here, :]
            out_acc[here, :] = fwd
            back_acc[here, :] = back
            return total + colsum(pre_grad.astype(F32))

        total = lax.fori_loop(0, 2, body, jnp.zeros((1, units), F32))
        grad_out[0:units, :] = nn(x_ref[...].T, pg_scr[...]).astype(BF16)
        grad_out[units : 2 * units, :] = nn(act_scr[...].T, cot_ref[...]).astype(BF16)
        last = jnp.concatenate([total, jnp.zeros((EXTRA - 1, units), F32)], axis=0)
        grad_out[2 * units :, :] = last.astype(BF16)

    return call(
        kernel,
        (ffn_in, cot, wide, *acc),
        [((rows, width), F32), ((rows, width), F32), ((2 * units + EXTRA, width), BF16)],
        [pltpu.VMEM((rows, units), BF16), pltpu.VMEM((rows, units), BF16)],
        name="feed_forward",
        us=3.0,
    )


def turn_back(res, forward, backward, cot, vec, mixed_t, wides, padded):
    rows, width = res.shape
    n = len(wides)
    out_rows = PAIR + EXTRA

    def kernel(res_ref, fwd_ref, back_ref, cot_ref, vec_ref, *refs):
        mixed_refs, out_refs = refs[:n], refs[n : 2 * n]
        block_out, resid_out, own_out, other_out, near_out = refs[2 * n : 2 * n + 5]
        dot_outs = refs[2 * n + 5 : 3 * n + 5]
        low_scr = refs[-1]
        gain = vec_ref[2:3, :]
        step = rows // 4

        def body(c, sums):
            here = pl.ds(pl.multiple_of(c * step, 16), step)
            res_rows = res_ref[here, :]
            back = back_ref[here, :]
            block_out[here, :] = (res_rows + fwd_ref[here, :]).astype(BF16)
            xhat, rstd = norm_parts(res_rows)
            resid = cot_ref[here, :].astype(F32) + norm_pull(back, gain, xhat, rstd)
            resid_out[here, :] = resid
            low_scr[here, :] = resid.astype(BF16)
            return sums[0] + colsum(back * xhat), sums[1] + colsum(back)

        zero = jnp.zeros((1, width), F32)
        gain_grad, shift_grad = lax.fori_loop(0, 4, body, (zero, zero))
        last = [zero, gain_grad, shift_grad, jnp.zeros((EXTRA - 3, width), F32)]
        last = jnp.concatenate(last, axis=0).astype(BF16)
        low_scr[rows:, :] = jnp.zeros((padded - rows, width), BF16)
        places = [(own_out, 0), (near_out, 0), (other_out, 0), (near_out, out_rows)]
        for r, (target, at) in enumerate(places):
            dot_outs[r][...] = nt(out_refs[r][...], low_scr[...]).astype(BF16)
            grad = nn(mixed_refs[r][...], low_scr[...]).astype(BF16)
            target[at : at + PAIR, :] = grad
            target[at + PAIR : at + out_rows, :] = last

    return call(
        kernel,
        (res, forward, backward, cot, vec, *mixed_t, *wides),
        [((rows, width), BF16), ((rows, width), F32)]
        + [((out_rows, width), BF16)] * 2
        + [((2 * out_rows, width), BF16)]
        + [((PAIR, padded), BF16)] * n,
        [pltpu.VMEM((padded, width), BF16)],
        name="turn_back",
        us=0.5,
        specs={5 + n + r: pl.BlockSpec((PAIR, width), lambda i: (0, 0)) for r in range(n)},
    )


def leave(seg, resid, acc, vec):
    rows, width = seg.shape
    padded = acc.shape[1]

    def kernel(seg_ref, resid_ref, acc_ref, vec_ref, seg_out, vec_out, acc_scr):
        gain = vec_ref[0:1, :]
        step = rows // 4
        acc_scr[...] = acc_ref[...].T

        def body(c, sums):
            here = pl.ds(pl.multiple_of(c * step, 16), step)
            grad = acc_scr[here, :]
            xhat, rstd = norm_parts(seg_ref[here, :].astype(F32))
            seg_out[here, :] = (resid_ref[here, :] + norm_pull(grad, gain, xhat, rstd)).astype(BF16)
            return sums[0] + colsum(grad * xhat), sums[1] + colsum(grad)

        zero = jnp.zeros((1, width), F32)
        gain_grad, shift_grad = lax.fori_loop(0, 4, body, (zero, zero))
        vec_out[...] = jnp.zeros(vec_out.shape, F32)
        vec_out[0:1, :] = gain_grad
        vec_out[1:2, :] = shift_grad

    return call(
        kernel,
        (seg, resid, acc, vec),
        [((rows, width), BF16), ((8, width), F32)],
        [pltpu.VMEM((padded, width), F32)],
        name="leave",
        us=0.5,
    )


def spread(mine, other, tensor_index, dtype):
    rows, width = mine.shape
    parts = [mine, swap(mine, 1), other, swap(other, 1)]

    def kernel(index_ref, *refs):
        out = refs[-1]
        for r, ref in enumerate(refs[:-1]):
            @pl.when(pl.program_id(0) == r)
            def _():
                out[0] = ref[...].astype(dtype)

    return pl.pallas_call(
        kernel,
        grid_spec=pltpu.PrefetchScalarGridSpec(
            num_scalar_prefetch=1,
            grid=(len(parts),),
            in_specs=[pl.BlockSpec((rows, width), lambda i, t: (0, 0)) for _ in parts],
            out_specs=pl.BlockSpec((1, rows, width), lambda i, t: (t[0] ^ i, 0, 0)),
        ),
        out_shape=jax.ShapeDtypeStruct((len(parts), rows, width), dtype),
        compiler_params=pltpu.CompilerParams(vmem_limit_bytes=24 * 1024 * 1024),
        name="spread",
    )(jnp.reshape(tensor_index, (1,)).astype(jnp.int32), *parts)


def own_shares(norm_vecs, ffn_vecs, place, share):
    width = ffn_vecs.shape[1]
    cols = norm_vecs.shape[1]

    def kernel(place_ref, norm_ref, ffn_ref, *outs):
        whole = jnp.concatenate([norm_ref[0:2, 0:width], ffn_ref[0:8, :]], axis=0)
        total = jnp.zeros((whole.shape[0], share), F32)
        for k in range(width // share):
            part = whole[:, k * share : (k + 1) * share]
            total = total + jnp.where(place_ref[0] == k, part, jnp.zeros_like(part))
        for v, out in enumerate(outs):
            out[...] = total[v : v + 1]

    outs = call(
        kernel,
        (jnp.reshape(place, (1,)).astype(jnp.int32), norm_vecs, ffn_vecs),
        [((1, share), F32)] * 5,
        scalars=1,
        name="own_shares",
    )
    return [o.reshape(share) for o in outs]


def rotary_tables(starts, padded):
    half = HEAD // 2
    inverse = jnp.exp(jnp.arange(half).astype(F32) * (-math.log(10000.0) / half))
    angles = inverse[:, None] * starts.astype(F32)[None, :]
    angles = jnp.pad(angles, ((0, 0), (0, padded - starts.shape[0])))
    return jnp.cos(angles), jnp.sin(angles)


def vector_rows(vectors, here, width, cols):
    own = vectors[0].shape[0]
    tiled = jnp.concatenate([jnp.tile(v, 2 * cols // own).reshape(2, cols) for v in vectors])
    tiled = jnp.pad(tiled, ((0, EXTRA - tiled.shape[0]), (0, 0)))
    row = lax.broadcasted_iota(jnp.int32, tiled.shape, 0)
    place = lax.broadcasted_iota(jnp.int32, tiled.shape, 1) + row % 2 * cols
    return jnp.where(place // own == here, tiled, jnp.zeros_like(tiled))


def local(
    segments,
    seg_start,
    seg_count,
    norm_gain,
    norm_shift,
    qkv_weight,
    out_weight,
    ffn_gain,
    ffn_shift,
    up_weight,
    up_bias,
    down_weight,
    cotangent,
):
    seq_local, seg_len, width = segments.shape
    tensor = lax.axis_size("tensor")
    members = lax.axis_size("dp")
    assert seq_local == tensor == 4
    padded = -(-seg_len // BLOCK) * BLOCK
    bits = bits_of(members)
    here = lax.axis_index("dp")
    mine = lax.axis_index("tensor")
    cols = 3 * qkv_weight.shape[2]
    assert cols == 3 * PAIR and width * 2 > cols
    groups = range(tensor)
    thin = any(
        a.shape[0] % 16 for a in (qkv_weight, out_weight, up_weight, down_weight)
    )

    seg = lax.dynamic_index_in_dim(segments, mine, 0, keepdims=False)
    cot = lax.dynamic_index_in_dim(cotangent, mine, 0, keepdims=False)
    starts = lax.dynamic_index_in_dim(seg_start, mine, 0, keepdims=False)
    live = lax.dynamic_slice_in_dim(seg_count, mine, 1)
    cos, sin = rotary_tables(starts, padded)

    def indices(distances):
        return here ^ jnp.asarray(distances, jnp.int32)

    qkv_rows, out_rows = qkv_weight.shape[0], out_weight.shape[0]
    up_rows, down_rows = up_weight.shape[0], down_weight.shape[0]
    vectors = (norm_gain, norm_shift, ffn_gain, ffn_shift, up_bias)
    first = jnp.concatenate(
        [qkv_weight.reshape(-1, cols), vector_rows(vectors, here, width, cols)]
    )
    arrays, order = [first[None]], [0]
    side, side_order = [jnp.concatenate([out_weight, up_weight])[None]], [0]
    down, down_order = [down_weight[None]], [0]
    for bit in bits[:-1]:
        arrays, order = widened(arrays, order, bit)
        side, side_order = widened(side, side_order, bit)
        down, down_order = widened(down, down_order, bit)
    arrays, order = widened(arrays, order, bits[-1])
    side, side_order = widened(side, side_order, bits[-1])
    down = joined(down)
    down = [down, swap(down, 2)]
    down_far = [across(d, bits[-1]) for d in down]
    down_order = down_order + [o ^ bits[-1] for o in down_order]

    pieces, places, parts = in_place(arrays, indices(order), (qkv_rows,))
    w0, xt, vec = enter(seg, pieces, places, parts[0], seg_len, padded, width, cols)
    w = [w0, swap(w0, 1), swap(w0, 2), None]
    w[3] = swap(w[2], 1)
    wides = []
    sides = [side, [swap(s, 2) for s in side]]
    for r in range(2):
        s, s_places, s_parts = in_place(sides[r], indices(side_order), (out_rows, up_rows))
        d, d_places, d_parts = in_place([down[r], down_far[r]], indices(down_order), (down_rows,))
        wide = lay_out(s, d, (s_places, d_places), (s_parts, d_parts), w[2 * r], width)
        wides += [wide, swap(wide, 1)]

    heads = [attend_forward(live, xt, w[r], cos, sin, seg_len) for r in groups]
    res, ffn_in = merge_attention(seg, [h[2] for h in heads], wides, vec)
    back_bits = bits[::-1]
    dp_steps = [(across, b) for b in back_bits]
    ahead = indices(halving_order(back_bits))
    acc = ()
    ffn_grads = [None] * 4
    for r in (3, 2, 1, 0):
        out_acc, back_acc, ffn_grads[r] = feed_forward(ffn_in, cot, wides[r], acc)
        acc = (out_acc, back_acc)
    ups = (ffn_grads[0], swap(ffn_grads[1], 1), ffn_grads[2], swap(ffn_grads[3], 1))
    units = (ffn_grads[0].shape[0] - EXTRA) // 2
    if thin:
        up_halves = cut_thin(
            [added([ups[0], ups[1]])[:width], added([ups[2], ups[3]])[:width]],
            ahead, [(0, up_rows)], [],
        )
    else:
        up_halves, downs = cut_up(ups, ahead, up_rows)
    res, up_halves = lax.optimization_barrier((res, up_halves))
    turned = turn_back(res, *acc, cot, vec, [h[1] for h in heads], wides, padded)
    block_mine, resid, out_own, out_other, out_near = turned[0:5]
    dots = list(turned[5:9])
    block_out = spread(block_mine, swap(block_mine, 2), mine, BF16)
    out_near = swap(out_near, 1)
    if thin:
        down_totals = []
        for side, own_out in enumerate((out_own, out_other)):
            tall = own_out.shape[0]
            out_sum = own_out.astype(F32) + out_near[side * tall : (side + 1) * tall].astype(F32)
            ffn_sum = added([ups[2 * side][units:], ups[2 * side + 1][units:]])
            last = out_sum[-EXTRA:] + ffn_sum[-EXTRA:].astype(F32)
            down_totals.append(
                jnp.concatenate([ffn_sum[:-EXTRA], out_sum[:-EXTRA].astype(BF16), last.astype(BF16)])
            )
        down_halves = cut_thin(
            down_totals, ahead, [(0, down_rows), (units, out_rows)], None
        )
    else:
        down_halves = cut_down(downs, (out_own, out_other), out_near, ahead, down_rows, out_rows)
    up = Halving(up_halves, dp_steps + [(swap, 2)])
    down = Halving(down_halves, dp_steps + [(swap, 2)])

    acc = ()
    qkv_grads = [None] * 4
    for r in (3, 2, 1, 0):
        if r == 2:
            up.step()
            dots[r], up.kept, up.sent, down.kept, down.sent = gate(
                dots[r], up.kept, up.sent, down.kept, down.sent
            )
        if r == 1:
            up.step()
            dots[r], up.kept, up.sent, other = gate(dots[r], up.kept, up.sent, other)
        qkv, ot, _, lse = heads[r]
        total, qkv_grads[r] = attend_backward(
            live, xt, w[r], cos, sin, qkv, ot, lse, dots[r], acc, seg_len
        )
        acc = (total,)
        if r == 2:
            other = added([qkv_grads[2], swap(qkv_grads[3], 1)])
    seg_mine, norm_vec = leave(seg, resid, total, vec)
    seg_mine = Held(seg_mine)
    down.step(seg_mine)
    up.step(down)
    other = swap(other, 2)
    other, up.kept = gate(other, up.kept)
    parts = (qkv_grads[0], swap(qkv_grads[1], 1), other)
    if thin:
        last = jnp.pad(norm_vec[0:2], ((0, 0), (0, 2 * cols - width))).reshape(4, cols)
        last = jnp.pad(last, ((0, EXTRA - 4), (0, 0))).astype(BF16)
        qkv_halves = cut_thin([added(parts)], ahead, [(0, qkv_rows)], [last])
    else:
        qkv_halves = cut_heads(parts, norm_vec, ahead, qkv_rows)
    heads_sum = Halving(qkv_halves, dp_steps)
    previous, seg_other = heads_sum, Held(swap(seg_mine.kept, 2))
    sums = (down, up, heads_sum)
    turns = 0
    while any(part.steps for part in sums):
        for part in sums:
            if part.steps:
                part.step(previous)
                previous = part
        turns += 1
        if turns == 2:
            seg_other.kept, previous.kept = gate(seg_other.kept, previous.kept)
            segments_grad = spread(seg_mine.kept, seg_other.kept, mine, F32)
    up_g, total_down, total = up.kept, down.kept, heads_sum.kept
    down_g = total_down[0:down_rows]
    out_g = total_down[down_rows : down_rows + out_rows]
    ffn_vecs = total_down[down_rows + out_rows :]
    qkv_g = total[0:qkv_rows]
    norm_vecs = total[qkv_rows : qkv_rows + 4].reshape(2, 2 * cols)
    norm_vecs = norm_vecs + swap(norm_vecs, 1)
    norm_vecs = norm_vecs + swap(norm_vecs, 2)

    share = norm_gain.shape[0]
    assert up_bias.shape[0] == share
    norm_gain_g, norm_shift_g, bias_g, ffn_gain_g, ffn_shift_g = own_shares(
        norm_vecs, ffn_vecs, here, share
    )
    return (
        block_out,
        segments_grad,
        norm_gain_g,
        norm_shift_g,
        qkv_g.reshape(qkv_weight.shape),
        out_g,
        ffn_gain_g,
        ffn_shift_g,
        up_g,
        bias_g,
        down_g,
    )


def solution(mesh):
    placed = (
        P("dp", None, None),
        P("dp", None),
        P("dp"),
        P("dp"),
        P("dp"),
        P("dp", None, "tensor"),
        P(("tensor", "dp"), None),
        P("dp"),
        P("dp"),
        P("dp", "tensor"),
        P(("tensor", "dp")),
        P(("tensor", "dp"), None),
        P("dp", None, None),
    )
    return jax.shard_map(
        local,
        mesh=mesh,
        in_specs=placed,
        out_specs=(
            P("dp", None, None),
            P("dp", None, None),
            P("dp"),
            P("dp"),
            P("dp", None, "tensor"),
            P(("tensor", "dp"), None),
            P("dp"),
            P("dp"),
            P("dp", "tensor"),
            P(("tensor", "dp")),
            P(("tensor", "dp"), None),
        ),
        check_vma=False,
    )
```

time: 312 us -> 177 us (0.57)
  the two profiles are of different devices: /device:TPU:11 before, /device:TPU:0 now
where the time goes in v2:
time: 177 us
  Pallas kernels  69.4 us (39%)
  waiting for transfers between devices  50.5 us (29%)
  starting transfers between devices  42.7 us (24%)
  local copies, waits for them, and re-layouts  8.93 us (5%)
  other arithmetic  4.11 us (2%)
    pallas_call x22, Pallas kernels, call(): pl.pallas_call(kernel, grid=(1,), in_specs=inner, out_specs=[pl.BlockSpec...  62.5 us
    ppermute x19, waiting for transfers between devices, across(): lax.ppermute(value, 'dp', [(i, i ^ bit) for i in range(lax.axis_size('dp'...  32.6 us
    ppermute x19, starting transfers between devices, across(): lax.ppermute(value, 'dp', [(i, i ^ bit) for i in range(lax.axis_size('dp'...  27.8 us
    ppermute x24, waiting for transfers between devices, swap(): lax.ppermute(value, 'tensor', [(t, t ^ bit) for t in range(lax.axis_size(...  17.9 us
    ppermute x24, starting transfers between devices, swap(): lax.ppermute(value, 'tensor', [(t, t ^ bit) for t in range(lax.axis_size(...  14.9 us
    pallas_call x2, Pallas kernels, spread(): pl.pallas_call(kernel, grid_spec=pltpu.PrefetchScalarGridSpec(num_scalar_...  6.93 us
    another operation x15, local copies, waits for them, and re-layouts, vector_rows(): jnp.tile(v, 2 * cols // own).reshape(2, cols)  3.89 us
  transfers between devices with their start and end apart: 43, of which 16 were waited for; matrix products, arithmetic and copies ran while one was open for 5% of the time, Pallas kernels for 29%

profile of v2, /device:TPU:0, one launch (start us, length us, event | category | flops | bytes accessed | tf_op | source)
XLA Modules:
  0.0 176.8 jit_solution(7216763787196246514)
XLA Ops:
  5.6 4.1 %collective-permute-start = (bf16[1,80,384]{2,1,0:T(8,128)(2,1)S(1)}, bf16[1,80,384]{2,1,0:T(8,128)(2,1)S(1)}, u32[]{:S(2)}, u32[]{:S(2)}) collective-permute-start(bf16[1,80,384]{2,1,0:T(8,128)(2,1)S(1)} %maximum_bitcast_fusion.1), channel_id=1, source_target_pairs={{0,16},{4,20},{8,24},{12,28},{16,0},{20,4},{24,8},{28,12},{1,17},{... | collective-permute-start | bytes 184328 | tf_op jit(solution)/shard_map/ppermute | solution.py:55
  10.6 2.8 %collective-permute-start.6 = (bf16[1,80,512]{2,1,0:T(8,128)(2,1)S(1)}, bf16[1,80,512]{2,1,0:T(8,128)(2,1)S(1)}, u32[]{:S(2)}, u32[]{:S(2)}) collective-permute-start(bf16[1,80,512]{2,1,0:T(8,128)(2,1)S(1)} %maximum_bitcast_fusion), channel_id=1, source_target_pairs={{0,16},{4,20},{8,24},{12,28},{16,0},{20,4},{24,8},{28,12},{1,17},{... | collective-permute-start | bytes 245768 | tf_op jit(solution)/shard_map/ppermute | solution.py:55
  24.1 2.8 %collective-permute-done.7 = bf16[2,80,512]{2,1,0:T(8,128)(2,1)S(1)} collective-permute-done((bf16[2,80,512]{2,1,0:T(8,128)(2,1)S(1)}, bf16[2,80,512]{2,1,0:T(8,128)(2,1)S(1)}, u32[]{:S(2)}, u32[]{:S(2)}) %collective-permute-start.7) | collective-permute-done | bytes 163872 | tf_op jit(solution)/shard_map/ppermute | solution.py:55
  41.0 4.3 %attend_forward.4 = (bf16[384,768]{1,0:T(8,128)(2,1)S(1)}, bf16[128,768]{1,0:T(8,128)(2,1)S(1)}, bf16[704,128]{1,0:T(8,128)(2,1)S(1)}, f32[8,768]{1,0:T(8,128)S(1)}) custom-call(s32[1]{0:T(128)} %dynamic_slice.15.live_ref, bf16[512,768]{1,0:T(8,128)(2,1)S(1)} %get-tuple-element.111.xt_ref, bf16[528,384]{1,0:T(8,128)(2,1)S(1)} %get-tuple-element.112.w_ref, ...), custom_call_target="tpu_custom_call" | custom-call | flops 4400000000 | bytes 1982464 | tf_op jit(solution)/shard_map/attend_forward/pallas_call | solution.py:34
  46.6 6.8 %collective-permute-done.4.w_ref = bf16[528,384]{1,0:T(8,128)(2,1)S(1)} collective-permute-done((bf16[528,384]{1,0:T(8,128)(2,1)S(1)}, bf16[528,384]{1,0:T(8,128)(2,1)S(1)}, u32[]{:S(2)}, u32[]{:S(2)}) %collective-permute-start.4) | collective-permute-done | bytes 405536 | tf_op jit(solution)/shard_map/ppermute | solution.py:75
  53.4 5.0 %collective-permute-done.14.refs_1_ = bf16[4,80,512]{2,1,0:T(8,128)(2,1)S(1)} collective-permute-done((bf16[4,80,512]{2,1,0:T(8,128)(2,1)S(1)}, bf16[4,80,512]{2,1,0:T(8,128)(2,1)S(1)}, u32[]{:S(2)}, u32[]{:S(2)}) %collective-permute-start.14) | collective-permute-done | bytes 327712 | tf_op jit(solution)/shard_map/ppermute | solution.py:75
  59.2 4.3 %attend_forward.6 = (bf16[384,768]{1,0:T(8,128)(2,1)S(1)}, bf16[128,768]{1,0:T(8,128)(2,1)S(1)}, bf16[704,128]{1,0:T(8,128)(2,1)S(1)}, f32[8,768]{1,0:T(8,128)S(1)}) custom-call(s32[1]{0:T(128)} %dynamic_slice.15.live_ref, bf16[512,768]{1,0:T(8,128)(2,1)S(1)} %get-tuple-element.111.xt_ref, bf16[528,384]{1,0:T(8,128)(2,1)S(1)} %collective-permute-done.4.w_ref, ...), custom_call_target="tpu_custom_call" | custom-call | flops 4400000000 | bytes 1982464 | tf_op jit(solution)/shard_map/attend_forward/pallas_call | solution.py:34
  63.5 4.3 %attend_forward.5 = (bf16[384,768]{1,0:T(8,128)(2,1)S(1)}, bf16[128,768]{1,0:T(8,128)(2,1)S(1)}, bf16[704,128]{1,0:T(8,128)(2,1)S(1)}, f32[8,768]{1,0:T(8,128)S(1)}) custom-call(s32[1]{0:T(128)} %dynamic_slice.15.live_ref, bf16[512,768]{1,0:T(8,128)(2,1)S(1)} %get-tuple-element.111.xt_ref, bf16[528,384]{1,0:T(8,128)(2,1)S(1)} %collective-permute-done.3.w_ref, ...), custom_call_target="tpu_custom_call" | custom-call | flops 4400000000 | bytes 1982464 | tf_op jit(solution)/shard_map/attend_forward/pallas_call | solution.py:34
  67.9 4.3 %attend_forward.7 = (bf16[384,768]{1,0:T(8,128)(2,1)S(1)}, bf16[128,768]{1,0:T(8,128)(2,1)S(1)}, bf16[704,128]{1,0:T(8,128)(2,1)S(1)}, f32[8,768]{1,0:T(8,128)S(1)}) custom-call(s32[1]{0:T(128)} %dynamic_slice.15.live_ref, bf16[512,768]{1,0:T(8,128)(2,1)S(1)} %get-tuple-element.111.xt_ref, bf16[528,384]{1,0:T(8,128)(2,1)S(1)} %collective-permute-done.5.w_ref, ...), custom_call_target="tpu_custom_call" | custom-call | flops 4400000000 | bytes 1982464 | tf_op jit(solution)/shard_map/attend_forward/pallas_call | solution.py:34
  73.6 3.1 %feed_forward.4 = (f32[704,512]{1,0:T(8,128)S(1)}, f32[704,512]{1,0:T(8,128)S(1)}, bf16[1040,512]{1,0:T(8,128)(2,1)S(1)}) custom-call(bf16[704,512]{1,0:T(8,128)(2,1)S(1)} %get-tuple-element.118.x_ref, bf16[704,512]{1,0:T(8,128)(2,1)S(1)} %dynamic-slice_bitcast_fusion.cot_ref, bf16[1168,512]{1,0:T(8,128)(2,1)S(1)} %collective-permute-done.17.refs_7_.ud_ref), custom_call_target="tpu_custom_call" | custom-call | flops 3300000000 | bytes 7897088 | tf_op jit(solution)/shard_map/feed_forward/pallas_call | solution.py:34
  76.8 3.1 %feed_forward.5 = (f32[704,512]{1,0:T(8,128)S(1)}, f32[704,512]{1,0:T(8,128)S(1)}, bf16[1040,512]{1,0:T(8,128)(2,1)S(1)}) custom-call(bf16[704,512]{1,0:T(8,128)(2,1)S(1)} %get-tuple-element.118.x_ref, bf16[704,512]{1,0:T(8,128)(2,1)S(1)} %dynamic-slice_bitcast_fusion.cot_ref, bf16[1168,512]{1,0:T(8,128)(2,1)S(1)} %lay_out.3.refs_6_.ud_ref, ...), custom_call_target="tpu_custom_call" | custom-call | flops 3300000000 | bytes 7897088 | tf_op jit(solution)/shard_map/feed_forward/pallas_call | solution.py:34
  79.9 3.3 %feed_forward.6 = (f32[704,512]{1,0:T(8,128)S(1)}, f32[704,512]{1,0:T(8,128)S(1)}, bf16[1040,512]{1,0:T(8,128)(2,1)S(1)}) custom-call(bf16[704,512]{1,0:T(8,128)(2,1)S(1)} %get-tuple-element.118.x_ref, bf16[704,512]{1,0:T(8,128)(2,1)S(1)} %dynamic-slice_bitcast_fusion.cot_ref, bf16[1168,512]{1,0:T(8,128)(2,1)S(1)} %collective-permute-done.12.refs_5_.ud_ref, ...), custom_call_target="tpu_custom_call" | custom-call | flops 3300000000 | bytes 7897088 | tf_op jit(solution)/shard_map/feed_forward/pallas_call | solution.py:34
  83.9 3.1 %feed_forward.7 = (f32[704,512]{1,0:T(8,128)S(1)}, f32[704,512]{1,0:T(8,128)S(1)}, bf16[1040,512]{1,0:T(8,128)(2,1)S(1)}) custom-call(bf16[704,512]{1,0:T(8,128)(2,1)S(1)} %get-tuple-element.118.x_ref, bf16[704,512]{1,0:T(8,128)(2,1)S(1)} %dynamic-slice_bitcast_fusion.cot_ref, bf16[1168,512]{1,0:T(8,128)(2,1)S(1)} %lay_out.2.refs_4_.ud_ref, ...), custom_call_target="tpu_custom_call" | custom-call | flops 3300000000 | bytes 7897088 | tf_op jit(solution)/shard_map/feed_forward/pallas_call | solution.py:34
  91.0 2.9 %turn_back.1 = (bf16[704,512]{1,0:T(8,128)(2,1)S(1)}, f32[704,512]{1,0:T(8,128)S(1)}, bf16[144,512]{1,0:T(8,128)(2,1)S(1)}, bf16[144,512]{1,0:T(8,128)(2,1)S(1)}...) custom-call(f32[704,512]{1,0:T(8,128)S(1)} %get-tuple-element.131.re, ...), custom_call_target="tpu_custom_call" | custom-call | flops 550000000 | bytes 1500000 | tf_op jit(solution)/shard_map/turn_back/pallas_call | solution.py:34
  95.6 4.6 %attend_backward.4 = (f32[512,768]{1,0:T(8,128)S(1)}, bf16[512,384]{1,0:T(8,128)(2,1)S(1)}) custom-call(s32[1]{0:T(128)} %dynamic_slice.15.live_ref, bf16[512,768]{1,0:T(8,128)(2,1)S(1)} %get-tuple-element.111.xt_ref, bf16[528,384]{1,0:T(8,128)(2,1)S(1)} %collective-permute-done.5.w_ref, f32[32,768]{1,0:T(8,128)S(1)} %get-tuple-element.250.cos_ref, ...), custom_call_target="tpu_custom_call" | custom-call | flops 1100000000 | bytes 3000000 | tf_op jit(solution)/shard_map/attend_backward/pallas_call | solution.py:34
  106.0 4.6 %attend_backward.5 = (f32[512,768]{1,0:T(8,128)S(1)}, bf16[512,384]{1,0:T(8,128)(2,1)S(1)}) custom-call(s32[1]{0:T(128)} %dynamic_slice.15.live_ref, bf16[512,768]{1,0:T(8,128)(2,1)S(1)} %get-tuple-element.111.xt_ref, bf16[528,384]{1,0:T(8,128)(2,1)S(1)} %collective-permute-done.4.w_ref, f32[32,768]{1,0:T(8,128)S(1)} %get-tuple-element.250.cos_ref, ...), custom_call_target="tpu_custom_call" | custom-call | flops 1100000000 | bytes 3000000 | tf_op jit(solution)/shard_map/attend_backward/pallas_call | solution.py:34
  111.5 2.7 %collective-permute-start.30 = (bf16[2,64,512]{2,1,0:T(8,128)(2,1)S(1)}, bf16[2,64,512]{2,1,0:T(8,128)(2,1)S(1)}, u32[]{:S(2)}, u32[]{:S(2)}) collective-permute-start(bf16[2,64,512]{2,1,0:T(8,128)(2,1)S(1)} %get-tuple-element.174), channel_id=1, source_target_pairs={{0,16},{4,20},{8,24},{12,28},{16,0},{20,4},{24,8},{28,12},{1,17},{... | collective-permute-start | bytes 393224 | tf_op jit(solution)/shard_map/ppermute | solution.py:55
  114.2 4.9 %attend_backward.6 = (f32[512,768]{1,0:T(8,128)S(1)}, bf16[512,384]{1,0:T(8,128)(2,1)S(1)}) custom-call(s32[1]{0:T(128)} %dynamic_slice.15.live_ref, bf16[512,768]{1,0:T(8,128)(2,1)S(1)} %get-tuple-element.111.xt_ref, bf16[528,384]{1,0:T(8,128)(2,1)S(1)} %collective-permute-done.3.w_ref, f32[32,768]{1,0:T(8,128)S(1)} %get-tuple-element.250.cos_ref, ...), custom_call_target="tpu_custom_call" | custom-call | flops 1100000000 | bytes 3000000 | tf_op jit(solution)/shard_map/attend_backward/pallas_call | solution.py:34
  120.8 4.6 %attend_backward.7 = (f32[512,768]{1,0:T(8,128)S(1)}, bf16[512,384]{1,0:T(8,128)(2,1)S(1)}) custom-call(s32[1]{0:T(128)} %dynamic_slice.15.live_ref, bf16[512,768]{1,0:T(8,128)(2,1)S(1)} %get-tuple-element.111.xt_ref, bf16[528,384]{1,0:T(8,128)(2,1)S(1)} %get-tuple-element.112.w_ref, f32[32,768]{1,0:T(8,128)S(1)} %get-tuple-element.250.cos_ref, ...), custom_call_target="tpu_custom_call" | custom-call | flops 1100000000 | bytes 3000000 | tf_op jit(solution)/shard_map/attend_backward/pallas_call | solution.py:34
  134.6 4.9 %collective-permute-done.31 = bf16[4,96,512]{2,1,0:T(8,128)(2,1)S(1)} collective-permute-done((bf16[4,96,512]{2,1,0:T(8,128)(2,1)S(1)}, bf16[4,96,512]{2,1,0:T(8,128)(2,1)S(1)}, u32[]{:S(2)}, u32[]{:S(2)}) %collective-permute-start.31) | collective-permute-done | bytes 393248 | tf_op jit(solution)/shard_map/ppermute | solution.py:55
  141.3 12.1 %collective-permute-done.34 = bf16[2,96,512]{2,1,0:T(8,128)(2,1)S(1)} collective-permute-done((bf16[2,96,512]{2,1,0:T(8,128)(2,1)S(1)}, bf16[2,96,512]{2,1,0:T(8,128)(2,1)S(1)}, u32[]{:S(2)}, u32[]{:S(2)}) %collective-permute-start.34) | collective-permute-done | bytes 196640 | tf_op jit(solution)/shard_map/ppermute | solution.py:55
  153.4 4.9 %collective-permute-done.37 = bf16[2,80,384]{2,1,0:T(8,128)(2,1)S(1)} collective-permute-done((bf16[2,80,384]{2,1,0:T(8,128)(2,1)S(1)}, bf16[2,80,384]{2,1,0:T(8,128)(2,1)S(1)}, u32[]{:S(2)}, u32[]{:S(2)}) %collective-permute-start.37) | collective-permute-done | bytes 122912 | tf_op jit(solution)/shard_map/ppermute | solution.py:55
  160.1 2.8 %collective-permute-done.39 = bf16[1,96,512]{2,1,0:T(8,128)(2,1)S(1)} collective-permute-done((bf16[1,96,512]{2,1,0:T(8,128)(2,1)S(1)}, bf16[1,96,512]{2,1,0:T(8,128)(2,1)S(1)}, u32[]{:S(2)}, u32[]{:S(2)}) %collective-permute-start.39) | collective-permute-done | bytes 98336 | tf_op jit(solution)/shard_map/ppermute | solution.py:75
  172.0 4.8 %spread.3 = f32[4,704,512]{2,1,0:T(8,128)} custom-call(s32[1]{0:T(128)} %bitcast.index_ref, bf16[704,512]{1,0:T(8,128)(2,1)} %get-tuple-element.173.refs_0_, bf16[704,512]{1,0:T(8,128)(2,1)} %collective-permute-done.28.refs_1_, bf16[704,512]{1,0:T(8,128)(2,1)} %collective-permute-done.29.refs_2_, bf16[704,512]{1,0:T(8,128)(2,1)} %collective-permute-done.38.refs_3_), custom_call_target="tpu_custom_call" | custom-call | tf_op jit(solution)/shard_map/spread/pallas_call | solution.py:677
  (151 shorter events, 70.3 us)
Async XLA Ops:
  5.6 10.6 %collective-permute-start = (bf16[1,80,384]{2,1,0:T(8,128)(2,1)S(1)}, bf16[1,80,384]{2,1,0:T(8,128)(2,1)S(1)}, u32[]{:S(2)}, u32[]{:S(2)}) collective-permute-start(bf16[1,80,384]{2,1,0:T(8,128)(2,1)S(1)} %maximum_bitcast_fusion.1), channel_id=1, source_target_pairs={{0,16},{4,20},{8,24},{12,28},{16,0},{20,4},{24,8},{28,12},{1,17},{... | collective-permute-start | bytes 184328 | tf_op jit(solution)/shard_map/ppermute | solution.py:55
  22.5 10.7 %collective-permute-start.2 = (bf16[4,80,384]{2,1,0:T(8,128)(2,1)S(1)}, bf16[4,80,384]{2,1,0:T(8,128)(2,1)S(1)}, u32[]{:S(2)}, u32[]{:S(2)}) collective-permute-start(bf16[4,80,384]{2,1,0:T(8,128)(2,1)S(1)} %pad_maximum_fusion.2.refs_0_), channel_id=1, source_target_pairs={{0,4},{4,0},{8,12},{12,8},{16,20},{20,16},{24,28},{28,24},{1,5},{5... | collective-permute-start | bytes 737288 | tf_op jit(solution)/shard_map/ppermute | solution.py:55
  26.9 12.6 %collective-permute-start.8 = (bf16[4,80,512]{2,1,0:T(8,128)(2,1)S(1)}, bf16[4,80,512]{2,1,0:T(8,128)(2,1)S(1)}, u32[]{:S(2)}, u32[]{:S(2)}) collective-permute-start(bf16[4,80,512]{2,1,0:T(8,128)(2,1)S(1)} %pad_maximum_fusion.refs_0_), channel_id=1, source_target_pairs={{0,4},{4,0},{8,12},{12,8},{16,20},{20,16},{24,28},{28,24},{1,5},{5... | collective-permute-start | bytes 983048 | tf_op jit(solution)/shard_map/ppermute | solution.py:55
  31.3 14.1 %collective-permute-start.11 = (bf16[4,64,512]{2,1,0:T(8,128)(2,1)S(1)}, bf16[4,64,512]{2,1,0:T(8,128)(2,1)S(1)}, u32[]{:S(2)}, u32[]{:S(2)}) collective-permute-start(bf16[4,64,512]{2,1,0:T(8,128)(2,1)S(1)} %pad_maximum_fusion.1.refs_2_), channel_id=1, source_target_pairs={{0,4},{4,0},{8,12},{12,8},{16,20},{20,16},{24,28},{28,24},{1,5},{5... | collective-permute-start | bytes 786440 | tf_op jit(solution)/shard_map/ppermute | solution.py:55
  32.8 13.3 %collective-permute-start.13 = (bf16[4,80,512]{2,1,0:T(8,128)(2,1)S(1)}, bf16[4,80,512]{2,1,0:T(8,128)(2,1)S(1)}, u32[]{:S(2)}, u32[]{:S(2)}) collective-permute-start(bf16[4,80,512]{2,1,0:T(8,128)(2,1)S(1)} %pad_maximum_fusion.refs_0_), channel_id=1, source_target_pairs={{0,2},{1,3},{2,0},{3,1},{4,6},{5,7},{6,4},{7,5},{8,10},{9,11},{10,... | collective-permute-start | bytes 983048 | tf_op jit(solution)/shard_map/ppermute | solution.py:75
  35.0 18.4 %collective-permute-start.4 = (bf16[528,384]{1,0:T(8,128)(2,1)S(1)}, bf16[528,384]{1,0:T(8,128)(2,1)S(1)}, u32[]{:S(2)}, u32[]{:S(2)}) collective-permute-start(bf16[528,384]{1,0:T(8,128)(2,1)S(1)} %get-tuple-element.112.w_ref), channel_id=1, source_target_pairs={{0,2},{1,3},{2,0},{3,1},{4,6},{5,7},{6,4},{7,5},{8,10},{9,11},{10,... | collective-permute-start | bytes 1216520 | tf_op jit(solution)/shard_map/ppermute | solution.py:75
  37.7 15.7 %collective-permute-start.16 = (bf16[4,64,512]{2,1,0:T(8,128)(2,1)S(1)}, bf16[4,64,512]{2,1,0:T(8,128)(2,1)S(1)}, u32[]{:S(2)}, u32[]{:S(2)}) collective-permute-start(bf16[4,64,512]{2,1,0:T(8,128)(2,1)S(1)} %collective-permute-done.15.refs_2_), channel_id=1, source_target_pairs={{0,4},{4,0},{8,12},{12,8},{16,20},{20,16},{24,28},{28,24},{1,5},{5... | collective-permute-start | bytes 786440 | tf_op jit(solution)/shard_map/ppermute | solution.py:55
  39.5 19.0 %collective-permute-start.14 = (bf16[4,80,512]{2,1,0:T(8,128)(2,1)S(1)}, bf16[4,80,512]{2,1,0:T(8,128)(2,1)S(1)}, u32[]{:S(2)}, u32[]{:S(2)}) collective-permute-start(bf16[4,80,512]{2,1,0:T(8,128)(2,1)S(1)} %collective-permute-done.8.refs_1_), channel_id=1, source_target_pairs={{0,2},{1,3},{2,0},{3,1},{4,6},{5,7},{6,4},{7,5},{8,10},{9,11},{10,... | collective-permute-start | bytes 983048 | tf_op jit(solution)/shard_map/ppermute | solution.py:75
  45.4 18.2 %collective-permute-start.3 = (bf16[528,384]{1,0:T(8,128)(2,1)S(1)}, bf16[528,384]{1,0:T(8,128)(2,1)S(1)}, u32[]{:S(2)}, u32[]{:S(2)}) collective-permute-start(bf16[528,384]{1,0:T(8,128)(2,1)S(1)} %get-tuple-element.112.w_ref), channel_id=1, source_target_pairs={{0,1},{1,0},{2,3},{3,2},{4,5},{5,4},{6,7},{7,6},{8,9},{9,8},{10,11... | collective-permute-start | bytes 1216520 | tf_op jit(solution)/shard_map/ppermute | solution.py:75
  46.1 26.1 %collective-permute-start.12 = (bf16[1168,512]{1,0:T(8,128)(2,1)S(1)}, bf16[1168,512]{1,0:T(8,128)(2,1)S(1)}, u32[]{:S(2)}, u32[]{:S(2)}) collective-permute-start(bf16[1168,512]{1,0:T(8,128)(2,1)S(1)} %lay_out.2.refs_4_.ud_ref), channel_id=1, source_target_pairs={{0,1},{1,0},{2,3},{3,2},{4,5},{5,4},{6,7},{7,6},{8,9},{9,8},{10,11... | collective-permute-start | bytes 3588104 | tf_op jit(solution)/shard_map/ppermute | solution.py:75
  53.4 14.4 %collective-permute-start.5 = (bf16[528,384]{1,0:T(8,128)(2,1)S(1)}, bf16[528,384]{1,0:T(8,128)(2,1)S(1)}, u32[]{:S(2)}, u32[]{:S(2)}) collective-permute-start(bf16[528,384]{1,0:T(8,128)(2,1)S(1)} %collective-permute-done.4.w_ref), channel_id=1, source_target_pairs={{0,1},{1,0},{2,3},{3,2},{4,5},{5,4},{6,7},{7,6},{8,9},{9,8},{10,11... | collective-permute-start | bytes 1216520 | tf_op jit(solution)/shard_map/ppermute | solution.py:75
  59.1 13.1 %collective-permute-start.17 = (bf16[1168,512]{1,0:T(8,128)(2,1)S(1)}, bf16[1168,512]{1,0:T(8,128)(2,1)S(1)}, u32[]{:S(2)}, u32[]{:S(2)}) collective-permute-start(bf16[1168,512]{1,0:T(8,128)(2,1)S(1)} %lay_out.3.refs_6_.ud_ref), channel_id=1, source_target_pairs={{0,1},{1,0},{2,3},{3,2},{4,5},{5,4},{6,7},{7,6},{8,9},{9,8},{10,11... | collective-permute-start | bytes 3588104 | tf_op jit(solution)/shard_map/ppermute | solution.py:75
  89.2 14.3 %collective-permute-start.23 = (bf16[8,64,512]{2,1,0:T(8,128)(2,1)S(1)}, bf16[8,64,512]{2,1,0:T(8,128)(2,1)S(1)}, u32[]{:S(2)}, u32[]{:S(2)}) collective-permute-start(bf16[8,64,512]{2,1,0:T(8,128)(2,1)S(1)} %get-tuple-element.141), channel_id=1, source_target_pairs={{0,4},{4,0},{8,12},{12,8},{16,20},{20,16},{24,28},{28,24},{1,5},{5... | collective-permute-start | bytes 1572872 | tf_op jit(solution)/shard_map/ppermute | solution.py:55
  94.0 35.7 %collective-permute-start.21 = (bf16[704,512]{1,0:T(8,128)(2,1)S(1)}, bf16[704,512]{1,0:T(8,128)(2,1)S(1)}, u32[]{:S(2)}, u32[]{:S(2)}) collective-permute-start(bf16[704,512]{1,0:T(8,128)(2,1)S(1)} %get-tuple-element.138.refs_0_), channel_id=1, source_target_pairs={{0,2},{1,3},{2,0},{3,1},{4,6},{5,7},{6,4},{7,5},{8,10},{9,11},{10,... | collective-permute-start | bytes 2162696 | tf_op jit(solution)/shard_map/ppermute | solution.py:75
  104.5 23.5 %collective-permute-start.25 = (bf16[8,96,512]{2,1,0:T(8,128)(2,1)S(1)}, bf16[8,96,512]{2,1,0:T(8,128)(2,1)S(1)}, u32[]{:S(2)}, u32[]{:S(2)}) collective-permute-start(bf16[8,96,512]{2,1,0:T(8,128)(2,1)S(1)} %get-tuple-element.149), channel_id=1, source_target_pairs={{0,4},{4,0},{8,12},{12,8},{16,20},{20,16},{24,28},{28,24},{1,5},{5... | collective-permute-start | bytes 2359304 | tf_op jit(solution)/shard_map/ppermute | solution.py:55
  111.5 18.2 %collective-permute-start.30 = (bf16[2,64,512]{2,1,0:T(8,128)(2,1)S(1)}, bf16[2,64,512]{2,1,0:T(8,128)(2,1)S(1)}, u32[]{:S(2)}, u32[]{:S(2)}) collective-permute-start(bf16[2,64,512]{2,1,0:T(8,128)(2,1)S(1)} %get-tuple-element.174), channel_id=1, source_target_pairs={{0,16},{4,20},{8,24},{12,28},{16,0},{20,4},{24,8},{28,12},{1,17},{... | collective-permute-start | bytes 393224 | tf_op jit(solution)/shard_map/ppermute | solution.py:55
  119.1 13.1 %collective-permute-start.32 = (bf16[512,384]{1,0:T(8,128)(2,1)S(1)}, bf16[512,384]{1,0:T(8,128)(2,1)S(1)}, u32[]{:S(2)}, u32[]{:S(2)}) collective-permute-start(bf16[512,384]{1,0:T(8,128)(2,1)S(1)} %get-tuple-element.179), channel_id=1, source_target_pairs={{0,1},{1,0},{2,3},{3,2},{4,5},{5,4},{6,7},{7,6},{8,9},{9,8},{10,11... | collective-permute-start | bytes 1179656 | tf_op jit(solution)/shard_map/ppermute | solution.py:75
  119.2 11.5 %collective-permute-start.33 = (bf16[512,384]{1,0:T(8,128)(2,1)S(1)}, bf16[512,384]{1,0:T(8,128)(2,1)S(1)}, u32[]{:S(2)}, u32[]{:S(2)}) collective-permute-start(bf16[512,384]{1,0:T(8,128)(2,1)S(1)} %add_convert_fusion.2), channel_id=1, source_target_pairs={{0,2},{1,3},{2,0},{3,1},{4,6},{5,7},{6,4},{7,5},{8,10},{9,11},{10,... | collective-permute-start | bytes 1179656 | tf_op jit(solution)/shard_map/ppermute | solution.py:75
  128.3 11.2 %collective-permute-start.31 = (bf16[4,96,512]{2,1,0:T(8,128)(2,1)S(1)}, bf16[4,96,512]{2,1,0:T(8,128)(2,1)S(1)}, u32[]{:S(2)}, u32[]{:S(2)}) collective-permute-start(bf16[4,96,512]{2,1,0:T(8,128)(2,1)S(1)} %get-tuple-element.231), channel_id=1, source_target_pairs={{0,8},{4,12},{8,0},{12,4},{16,24},{20,28},{24,16},{28,20},{1,9},{5... | collective-permute-start | bytes 1179656 | tf_op jit(solution)/shard_map/ppermute | solution.py:55
  129.8 35.8 %collective-permute-start.20 = (bf16[704,512]{1,0:T(8,128)(2,1)S(1)}, bf16[704,512]{1,0:T(8,128)(2,1)S(1)}, u32[]{:S(2)}, u32[]{:S(2)}) collective-permute-start(bf16[704,512]{1,0:T(8,128)(2,1)S(1)} %get-tuple-element.138.refs_0_), channel_id=1, source_target_pairs={{0,1},{1,0},{2,3},{3,2},{4,5},{5,4},{6,7},{7,6},{8,9},{9,8},{10,11... | collective-permute-start | bytes 2162696 | tf_op jit(solution)/shard_map/ppermute | solution.py:75
  129.8 35.8 %collective-permute-start.22 = (bf16[704,512]{1,0:T(8,128)(2,1)S(1)}, bf16[704,512]{1,0:T(8,128)(2,1)S(1)}, u32[]{:S(2)}, u32[]{:S(2)}) collective-permute-start(bf16[704,512]{1,0:T(8,128)(2,1)S(1)} %collective-permute-done.21.refs_2_), channel_id=1, source_target_pairs={{0,1},{1,0},{2,3},{3,2},{4,5},{5,4},{6,7},{7,6},{8,9},{9,8},{10,11... | collective-permute-start | bytes 2162696 | tf_op jit(solution)/shard_map/ppermute | solution.py:75
  139.5 20.3 %collective-permute-start.29 = (bf16[704,512]{1,0:T(8,128)(2,1)}, bf16[704,512]{1,0:T(8,128)(2,1)}, u32[]{:S(2)}, u32[]{:S(2)}) collective-permute-start(bf16[704,512]{1,0:T(8,128)(2,1)} %get-tuple-element.173.refs_0_), channel_id=1, source_target_pairs={{0,2},{1,3},{2,0},{3,1},{4,6},{5,7},{6,4},{7,5},{8,10},{9,11},{10,... | collective-permute-start | bytes 2162696 | tf_op jit(solution)/shard_map/ppermute | solution.py:75
  140.2 31.8 %collective-permute-start.28 = (bf16[704,512]{1,0:T(8,128)(2,1)}, bf16[704,512]{1,0:T(8,128)(2,1)}, u32[]{:S(2)}, u32[]{:S(2)}) collective-permute-start(bf16[704,512]{1,0:T(8,128)(2,1)} %get-tuple-element.173.refs_0_), channel_id=1, source_target_pairs={{0,1},{1,0},{2,3},{3,2},{4,5},{5,4},{6,7},{7,6},{8,9},{9,8},{10,11... | collective-permute-start | bytes 2162696 | tf_op jit(solution)/shard_map/ppermute | solution.py:75
  140.9 12.4 %collective-permute-start.34 = (bf16[2,96,512]{2,1,0:T(8,128)(2,1)S(1)}, bf16[2,96,512]{2,1,0:T(8,128)(2,1)S(1)}, u32[]{:S(2)}, u32[]{:S(2)}) collective-permute-start(bf16[2,96,512]{2,1,0:T(8,128)(2,1)S(1)} %get-tuple-element.235), channel_id=1, source_target_pairs={{0,16},{4,20},{8,24},{12,28},{16,0},{20,4},{24,8},{28,12},{1,17},{... | collective-permute-start | bytes 589832 | tf_op jit(solution)/shard_map/ppermute | solution.py:55
  (23 other events, 169.1 us)

commit v3 on v2

--- a/solution.py
+++ b/solution.py
@@ -378,116 +378,117 @@
     )
 
 
-def cut_heads(grads, vec, order, rows):
+def packed(rows):
+    n = rows.shape[0]
+    tall = jnp.concatenate(jnp.split(rows, 3, axis=1))
+    return jnp.concatenate(jnp.split(tall, 4), axis=1)
+
+
+def unpacked(rows):
+    tall = jnp.concatenate(jnp.split(rows, 4, axis=1))
+    return jnp.stack(jnp.split(tall, 3), axis=1)
+
+
+def cut_heads(grads, vec, outs, order, rows, out_rows):
     whole_rows, cols = grads[0].shape
-    width = vec.shape[1]
+    tall, width = outs[0].shape
     count = order.shape[0]
-
-    def kernel(order_ref, a_ref, b_ref, c_ref, vec_ref, kept, sent, whole):
+    unit = rows // 4
+    high = 3 * unit
+
+    def kernel(order_ref, a_ref, b_ref, c_ref, vec_ref, own_ref, near_ref, far_ref, kept, sent, whole, out_whole):
         whole[...] = (a_ref[...].astype(F32) + b_ref[...].astype(F32) + c_ref[...].astype(F32)).astype(BF16)
-        tail = jnp.zeros((EXTRA - 4, cols), F32)
-        blank = jnp.zeros((1, 2 * cols - width), F32)
-        v0, v1 = vec_ref[0:1, :], vec_ref[1:2, :]
-        parts = []
-        for v in (v0, v1):
-            parts.append(v[:, 0:cols])
-            parts.append(jnp.concatenate([v[:, cols:width], blank], axis=1))
-        last = jnp.concatenate(parts + [tail], axis=0).astype(BF16)
+        out_sum = own_ref[...].astype(F32) + near_ref[0:tall, :].astype(F32) + far_ref[...].astype(F32)
+        out_whole[...] = out_sum[0 : tall - EXTRA].astype(BF16)
+        last = out_sum[tall - EXTRA :]
+        last = jnp.concatenate([last[0:3], vec_ref[0:2, :], last[5:]], axis=0).astype(BF16)
 
         def cut(index, piece):
-            piece[0:rows, :] = rows_of(whole, 0, index, rows)
-            piece[rows:, :] = last
+            for u in range(12):
+                start = pl.multiple_of(index * rows + unit * (u % 4), 16)
+                at, lane = unit * (u % 3), PAIR * (u // 3)
+                block = whole[pl.ds(start, unit), PAIR * (u // 4) : PAIR * (u // 4 + 1)]
+                piece[at : at + unit, lane : lane + PAIR] = block
+            piece[high : high + out_rows, :] = rows_of(out_whole, 0, index, out_rows)
+            piece[high + out_rows :, :] = last
 
         emit(cut, order_ref, kept, sent)
 
     return halves_call(
         kernel,
-        (order, *grads, vec),
+        (order, *grads, vec, *outs),
         count,
-        rows + EXTRA,
-        cols,
-        [pltpu.VMEM((whole_rows, cols), BF16)],
+        high + out_rows + EXTRA,
+        width,
+        [pltpu.VMEM((whole_rows, cols), BF16), pltpu.VMEM((tall - EXTRA, width), BF16)],
         "cut_heads",
     )
 
 
-def cut_down(downs, outs, out_near, order, down_rows, out_rows):
-    width = downs[0].shape[1]
-    count = order.shape[0]
-    down = down_rows * count
-    tall = out_rows * count + EXTRA
-    end = down + tall - EXTRA
-
-    def kernel(order_ref, *refs):
-        down_refs, out_refs = refs[0:2], refs[2:4]
-        near_ref, kept, sent = refs[4:7]
-        wholes = refs[7:9]
-        for side, whole in enumerate(wholes):
-            near = near_ref[side * tall : (side + 1) * tall, :].astype(F32)
-            outs_sum = out_refs[side][...].astype(F32) + near
-            whole[0 : tall - EXTRA, :] = outs_sum[0 : tall - EXTRA].astype(BF16)
-            bias = down_refs[side][down:, :].astype(F32)
-            whole[tall - EXTRA :, :] = (outs_sum[tall - EXTRA :] + bias).astype(BF16)
-        half = kept.shape[0]
-        for k in range(count):
-            for side, whole in enumerate(wholes):
-                j = 2 * k + side
-                target, j = (kept, j) if j < half else (sent, j - half)
-                index = order_ref[k]
-                target[j, 0:down_rows, :] = rows_of(down_refs[side], 0, index, down_rows)
-                target[j, down_rows : down_rows + out_rows, :] = rows_of(whole, 0, index, out_rows)
-                target[j, down_rows + out_rows :, :] = whole[tall - EXTRA :, :]
-
-    return halves_call(
-        kernel,
-        (order, *downs, *outs, out_near),
-        2 * count,
-        down_rows + out_rows + EXTRA,
-        width,
-        [pltpu.VMEM((tall, width), BF16)] * 2,
-        "cut_down",
-    )
-
-
-def cut_up(grads, order, rows):
+def end_heads(kept, got, rows, out_rows):
+    unit = rows // 4
+    high = 3 * unit
+    width = kept.shape[-1]
+
+    def kernel(kept_ref, got_ref, qkv_out, out_out, vec_out):
+        total = kept_ref[0].astype(F32) + got_ref[0].astype(F32)
+        for u in range(12):
+            at, lane = unit * (u % 3), PAIR * (u // 3)
+            first = unit * (u % 4)
+            qkv_out[first : first + unit, u // 4, :] = total[at : at + unit, lane : lane + PAIR]
+        out_out[...] = total[high : high + out_rows]
+        vec_out[...] = total[high + out_rows :]
+
+    return call(
+        kernel,
+        (kept, got),
+        [((rows, 3, PAIR), F32), ((out_rows, width), F32), ((EXTRA, width), F32)],
+        name="end_heads",
+        us=0.5,
+    )
+
+
+def cut_ffn(grads, up_order, down_order, rows):
     height, width = grads[0].shape
-    count = order.shape[0]
+    count = up_order.shape[0]
     whole_rows = rows * count
 
-    def kernel(order_ref, a_ref, b_ref, c_ref, d_ref, kept, sent, rest_near, rest_far, near, far):
-        here = slice(0, whole_rows)
-        rest = slice(whole_rows, height)
-        for x_ref, y_ref, up, other in ((a_ref, b_ref, near, rest_near), (c_ref, d_ref, far, rest_far)):
-            up[...] = (x_ref[here, :].astype(F32) + y_ref[here, :].astype(F32)).astype(BF16)
-            other[...] = (x_ref[rest, :].astype(F32) + y_ref[rest, :].astype(F32)).astype(BF16)
-        half = kept.shape[0]
-        for k in range(count):
-            for side, whole in enumerate((near, far)):
-                j = 2 * k + side
-                target, j = (kept, j) if j < half else (sent, j - half)
-                target[j] = rows_of(whole, 0, order_ref[k], rows)
-
-    kept, sent, *rest = call(
-        kernel,
-        (order, *grads),
-        [((count, rows, width), BF16)] * 2 + [((height - whole_rows, width), BF16)] * 2,
+    def kernel(up_ref, down_ref, a_ref, b_ref, c_ref, d_ref, up_kept, up_sent, down_kept, down_sent, near, far):
+        half = up_kept.shape[0]
+        for first, order_ref, kept, sent in (
+            (0, up_ref, up_kept, up_sent),
+            (whole_rows, down_ref, down_kept, down_sent),
+        ):
+            here = slice(first, first + whole_rows)
+            near[...] = (a_ref[here, :].astype(F32) + b_ref[here, :].astype(F32)).astype(BF16)
+            far[...] = (c_ref[here, :].astype(F32) + d_ref[here, :].astype(F32)).astype(BF16)
+            for k in range(count):
+                for side, whole in enumerate((near, far)):
+                    j = 2 * k + side
+                    target, j = (kept, j) if j < half else (sent, j - half)
+                    target[j] = rows_of(whole, 0, order_ref[k], rows)
+
+    outs = call(
+        kernel,
+        (up_order, down_order, *grads),
+        [((count, rows, width), BF16)] * 4,
         [pltpu.VMEM((whole_rows, width), BF16)] * 2,
-        scalars=1,
-        name="cut_up",
+        scalars=2,
+        name="cut_ffn",
         us=1.5,
     )
-    return (kept, sent), rest
-
-
-def cut_thin(totals, order, spans, last):
+    return outs[0:2], outs[2:4]
+
+
+def cut_thin(totals, order, spans, last=()):
     pieces = []
     for k in range(order.shape[0]):
         for total in totals:
             piece = [
-                lax.dynamic_slice_in_dim(total, first + order[k] * rows, rows, 0)
-                for first, rows in spans
+                pack(lax.dynamic_slice_in_dim(total[part], order[k] * rows, rows, 0))
+                for part, rows, pack in spans
             ]
-            pieces.append(jnp.concatenate(piece + ([total[-EXTRA:]] if last is None else last)))
+            pieces.append(jnp.concatenate(piece + list(last)))
     pieces = jnp.stack(pieces)
     half = pieces.shape[0] // 2
     return pieces[:half], pieces[half:]
@@ -581,15 +582,16 @@
     )
 
 
-def turn_back(res, forward, backward, cot, vec, mixed_t, wides, padded):
+def turn_back(res, forward, backward, cot, vec, mixed_t, wides, ffn_grads, padded):
     rows, width = res.shape
     n = len(wides)
     out_rows = PAIR + EXTRA
+    bias_at = ffn_grads[0].shape[0] // EXTRA - 1
 
     def kernel(res_ref, fwd_ref, back_ref, cot_ref, vec_ref, *refs):
-        mixed_refs, out_refs = refs[:n], refs[n : 2 * n]
-        block_out, resid_out, own_out, other_out, near_out = refs[2 * n : 2 * n + 5]
-        dot_outs = refs[2 * n + 5 : 3 * n + 5]
+        mixed_refs, out_refs, bias_refs = refs[:n], refs[n : 2 * n], refs[2 * n : 3 * n]
+        block_out, resid_out, own_out, other_out, near_out = refs[3 * n : 3 * n + 5]
+        dot_outs = refs[3 * n + 5 : 4 * n + 5]
         low_scr = refs[-1]
         gain = vec_ref[2:3, :]
         step = rows // 4
@@ -607,19 +609,19 @@
 
         zero = jnp.zeros((1, width), F32)
         gain_grad, shift_grad = lax.fori_loop(0, 4, body, (zero, zero))
-        last = [zero, gain_grad, shift_grad, jnp.zeros((EXTRA - 3, width), F32)]
-        last = jnp.concatenate(last, axis=0).astype(BF16)
+        tail = jnp.zeros((EXTRA - 3, width), F32)
         low_scr[rows:, :] = jnp.zeros((padded - rows, width), BF16)
         places = [(own_out, 0), (near_out, 0), (other_out, 0), (near_out, out_rows)]
         for r, (target, at) in enumerate(places):
             dot_outs[r][...] = nt(out_refs[r][...], low_scr[...]).astype(BF16)
             grad = nn(mixed_refs[r][...], low_scr[...]).astype(BF16)
             target[at : at + PAIR, :] = grad
-            target[at + PAIR : at + out_rows, :] = last
-
-    return call(
-        kernel,
-        (res, forward, backward, cot, vec, *mixed_t, *wides),
+            last = [bias_refs[r][0:1, :].astype(F32), gain_grad, shift_grad, tail]
+            target[at + PAIR : at + out_rows, :] = jnp.concatenate(last, axis=0).astype(BF16)
+
+    return call(
+        kernel,
+        (res, forward, backward, cot, vec, *mixed_t, *wides, *ffn_grads),
         [((rows, width), BF16), ((rows, width), F32)]
         + [((out_rows, width), BF16)] * 2
         + [((2 * out_rows, width), BF16)]
@@ -627,7 +629,10 @@
         [pltpu.VMEM((padded, width), BF16)],
         name="turn_back",
         us=0.5,
-        specs={5 + n + r: pl.BlockSpec((PAIR, width), lambda i: (0, 0)) for r in range(n)},
+        specs={
+            **{5 + n + r: pl.BlockSpec((PAIR, width), lambda i: (0, 0)) for r in range(n)},
+            **{5 + 2 * n + r: pl.BlockSpec((EXTRA, width), lambda i: (bias_at, 0)) for r in range(n)},
+        },
     )
 
 
@@ -690,10 +695,9 @@
 
 def own_shares(norm_vecs, ffn_vecs, place, share):
     width = ffn_vecs.shape[1]
-    cols = norm_vecs.shape[1]
 
     def kernel(place_ref, norm_ref, ffn_ref, *outs):
-        whole = jnp.concatenate([norm_ref[0:2, 0:width], ffn_ref[0:8, :]], axis=0)
+        whole = jnp.concatenate([norm_ref[3:5, :], ffn_ref[0:3, :]], axis=0)
         total = jnp.zeros((whole.shape[0], share), F32)
         for k in range(width // share):
             part = whole[:, k * share : (k + 1) * share]
@@ -721,11 +725,29 @@
 
 def vector_rows(vectors, here, width, cols):
     own = vectors[0].shape[0]
-    tiled = jnp.concatenate([jnp.tile(v, 2 * cols // own).reshape(2, cols) for v in vectors])
-    tiled = jnp.pad(tiled, ((0, EXTRA - tiled.shape[0]), (0, 0)))
-    row = lax.broadcasted_iota(jnp.int32, tiled.shape, 0)
-    place = lax.broadcasted_iota(jnp.int32, tiled.shape, 1) + row % 2 * cols
-    return jnp.where(place // own == here, tiled, jnp.zeros_like(tiled))
+    stacked = jnp.stack(vectors + (jnp.zeros_like(vectors[0]),) * (8 - len(vectors)))
+    lanes = -(-cols // own) * own
+
+    def kernel(here_ref, vec_ref, out):
+        tiled = jnp.concatenate([vec_ref[...].astype(F32)] * (lanes // own), axis=1)[:, 0:cols]
+        place = lax.broadcasted_iota(jnp.int32, tiled.shape, 1)
+        first = here_ref[0] * own
+        rows = []
+        for v in range(len(vectors)):
+            for at in (0, cols):
+                inside = (place + at >= first) & (place + at < first + own)
+                rows.append(jnp.where(inside, tiled, 0.0)[v : v + 1])
+        rows.append(jnp.zeros((EXTRA - len(rows), cols), F32))
+        out[...] = jnp.concatenate(rows, axis=0).astype(BF16)
+
+    return call(
+        kernel,
+        (jnp.reshape(here, (1,)).astype(jnp.int32), stacked),
+        [((EXTRA, cols), BF16)],
+        scalars=1,
+        name="vector_rows",
+        us=0.3,
+    )[0]
 
 
 def local(
@@ -789,21 +811,33 @@
 
     pieces, places, parts = in_place(arrays, indices(order), (qkv_rows,))
     w0, xt, vec = enter(seg, pieces, places, parts[0], seg_len, padded, width, cols)
+    def weights_of(side, down, w):
+        s, s_places, s_parts = in_place(side, indices(side_order), (out_rows, up_rows))
+        d, d_places, d_parts = in_place(down, indices(down_order), (down_rows,))
+        return lay_out(s, d, (s_places, d_places), (s_parts, d_parts), w, width)
+
+    def attend(w):
+        return list(attend_forward(live, xt, w, cos, sin, seg_len))
+
     w = [w0, swap(w0, 1), swap(w0, 2), None]
+    far = [swap(s, 2) for s in side]
+    heads = [attend(w[0])]
+    w[1], heads[0][2] = gate(w[1], heads[0][2])
+    heads.append(attend(w[1]))
+    *near, heads[1][2] = gate(*side, down[0], down_far[0], heads[1][2])
+    wides = [weights_of(near[:-2], near[-2:], w0)]
+    wides.append(swap(wides[0], 1))
+    w[2], wides[0] = gate(w[2], wides[0])
     w[3] = swap(w[2], 1)
-    wides = []
-    sides = [side, [swap(s, 2) for s in side]]
-    for r in range(2):
-        s, s_places, s_parts = in_place(sides[r], indices(side_order), (out_rows, up_rows))
-        d, d_places, d_parts = in_place([down[r], down_far[r]], indices(down_order), (down_rows,))
-        wide = lay_out(s, d, (s_places, d_places), (s_parts, d_parts), w[2 * r], width)
-        wides += [wide, swap(wide, 1)]
-
-    heads = [attend_forward(live, xt, w[r], cos, sin, seg_len) for r in groups]
+    heads.append(attend(w[2]))
+    w[3], heads[2][2] = gate(w[3], heads[2][2])
+    heads.append(attend(w[3]))
+    *far, heads[3][2] = gate(*far, down[1], down_far[1], heads[3][2])
+    wides.append(weights_of(far[:-2], far[-2:], w[2]))
+    wides.append(swap(wides[2], 1))
     res, ffn_in = merge_attention(seg, [h[2] for h in heads], wides, vec)
-    back_bits = bits[::-1]
-    dp_steps = [(across, b) for b in back_bits]
-    ahead = indices(halving_order(back_bits))
+    up_bits, down_bits = bits[::-1], bits[-2::-1] + bits[-1:]
+    ahead, down_ahead = (indices(halving_order(b)) for b in (up_bits, down_bits))
     acc = ()
     ffn_grads = [None] * 4
     for r in (3, 2, 1, 0):
@@ -812,47 +846,37 @@
     ups = (ffn_grads[0], swap(ffn_grads[1], 1), ffn_grads[2], swap(ffn_grads[3], 1))
     units = (ffn_grads[0].shape[0] - EXTRA) // 2
     if thin:
-        up_halves = cut_thin(
-            [added([ups[0], ups[1]])[:width], added([ups[2], ups[3]])[:width]],
-            ahead, [(0, up_rows)], [],
+        pairs = [added(ups[0:2]), added(ups[2:4])]
+        keep = lambda rows: rows
+        up_halves = cut_thin([[p[:units]] for p in pairs], ahead, [(0, up_rows, keep)])
+        down_halves = cut_thin(
+            [[p[units : 2 * units]] for p in pairs], down_ahead, [(0, down_rows, keep)]
         )
     else:
-        up_halves, downs = cut_up(ups, ahead, up_rows)
-    res, up_halves = lax.optimization_barrier((res, up_halves))
-    turned = turn_back(res, *acc, cot, vec, [h[1] for h in heads], wides, padded)
+        up_halves, down_halves = cut_ffn(ups, ahead, down_ahead, up_rows)
+    res, up_halves, down_halves = lax.optimization_barrier((res, up_halves, down_halves))
+    up = Halving(up_halves, [(across, b) for b in up_bits] + [(swap, 2)])
+    down = Halving(down_halves, [(across, b) for b in down_bits] + [(swap, 2)])
+    turned = turn_back(
+        res, *acc, cot, vec, [h[1] for h in heads], wides, ffn_grads, padded
+    )
     block_mine, resid, out_own, out_other, out_near = turned[0:5]
     dots = list(turned[5:9])
     block_out = spread(block_mine, swap(block_mine, 2), mine, BF16)
     out_near = swap(out_near, 1)
-    if thin:
-        down_totals = []
-        for side, own_out in enumerate((out_own, out_other)):
-            tall = own_out.shape[0]
-            out_sum = own_out.astype(F32) + out_near[side * tall : (side + 1) * tall].astype(F32)
-            ffn_sum = added([ups[2 * side][units:], ups[2 * side + 1][units:]])
-            last = out_sum[-EXTRA:] + ffn_sum[-EXTRA:].astype(F32)
-            down_totals.append(
-                jnp.concatenate([ffn_sum[:-EXTRA], out_sum[:-EXTRA].astype(BF16), last.astype(BF16)])
-            )
-        down_halves = cut_thin(
-            down_totals, ahead, [(0, down_rows), (units, out_rows)], None
-        )
-    else:
-        down_halves = cut_down(downs, (out_own, out_other), out_near, ahead, down_rows, out_rows)
-    up = Halving(up_halves, dp_steps + [(swap, 2)])
-    down = Halving(down_halves, dp_steps + [(swap, 2)])
+    out_far = swap(added([out_other, out_near[out_other.shape[0] :]]), 2)
 
     acc = ()
     qkv_grads = [None] * 4
     for r in (3, 2, 1, 0):
         if r == 2:
             up.step()
+            down.step()
             dots[r], up.kept, up.sent, down.kept, down.sent = gate(
                 dots[r], up.kept, up.sent, down.kept, down.sent
             )
         if r == 1:
-            up.step()
-            dots[r], up.kept, up.sent, other = gate(dots[r], up.kept, up.sent, other)
+            dots[r], other, out_far = gate(dots[r], other, out_far)
         qkv, ot, _, lse = heads[r]
         total, qkv_grads[r] = attend_backward(
             live, xt, w[r], cos, sin, qkv, ot, lse, dots[r], acc, seg_len
@@ -860,52 +884,66 @@
         acc = (total,)
         if r == 2:
             other = added([qkv_grads[2], swap(qkv_grads[3], 1)])
+    up.step()
+    down.step()
+    total, up.kept, up.sent, down.kept, down.sent = gate(
+        total, up.kept, up.sent, down.kept, down.sent
+    )
     seg_mine, norm_vec = leave(seg, resid, total, vec)
     seg_mine = Held(seg_mine)
-    down.step(seg_mine)
-    up.step(down)
-    other = swap(other, 2)
-    other, up.kept = gate(other, up.kept)
+    seg_other = Held(swap(seg_mine.kept, 2))
+    other, seg_mine.kept = gate(swap(other, 2), seg_mine.kept)
     parts = (qkv_grads[0], swap(qkv_grads[1], 1), other)
     if thin:
-        last = jnp.pad(norm_vec[0:2], ((0, 0), (0, 2 * cols - width))).reshape(4, cols)
-        last = jnp.pad(last, ((0, EXTRA - 4), (0, 0))).astype(BF16)
-        qkv_halves = cut_thin([added(parts)], ahead, [(0, qkv_rows)], [last])
+        tall = out_own.shape[0]
+        out_sum = added([out_own, out_near[:tall], out_far])
+        last = out_sum[-EXTRA:].at[3:5].set(norm_vec[0:2].astype(BF16))
+        halves = cut_thin(
+            [[added(parts), out_sum]], ahead, [(0, qkv_rows, packed), (1, out_rows, keep)], [last]
+        )
     else:
-        qkv_halves = cut_heads(parts, norm_vec, ahead, qkv_rows)
-    heads_sum = Halving(qkv_halves, dp_steps)
-    previous, seg_other = heads_sum, Held(swap(seg_mine.kept, 2))
-    sums = (down, up, heads_sum)
-    turns = 0
-    while any(part.steps for part in sums):
-        for part in sums:
-            if part.steps:
-                part.step(previous)
-                previous = part
-        turns += 1
-        if turns == 2:
-            seg_other.kept, previous.kept = gate(seg_other.kept, previous.kept)
-            segments_grad = spread(seg_mine.kept, seg_other.kept, mine, F32)
-    up_g, total_down, total = up.kept, down.kept, heads_sum.kept
-    down_g = total_down[0:down_rows]
-    out_g = total_down[down_rows : down_rows + out_rows]
-    ffn_vecs = total_down[down_rows + out_rows :]
-    qkv_g = total[0:qkv_rows]
-    norm_vecs = total[qkv_rows : qkv_rows + 4].reshape(2, 2 * cols)
-    norm_vecs = norm_vecs + swap(norm_vecs, 1)
-    norm_vecs = norm_vecs + swap(norm_vecs, 2)
+        halves = cut_heads(parts, norm_vec, (out_own, out_near, out_far), ahead, qkv_rows, out_rows)
+    heads_sum = Halving(halves, [(across, b) for b in up_bits])
+    down.step(heads_sum)
+    block_out, down.kept = gate(block_out, down.kept)
+    up.step(down)
+    heads_sum.step(up)
+    while len(heads_sum.steps) > 1:
+        heads_sum.step()
+    seg_other.kept, heads_sum.kept, heads_sum.sent = gate(
+        seg_other.kept, heads_sum.kept, heads_sum.sent
+    )
+    while up.steps:
+        up.step(seg_other)
+        down.step(up)
+    up_g, down_g = up.kept, down.kept
+    got = across(heads_sum.sent, heads_sum.steps[0][1])
+    got, up_g, down_g = gate(got, up_g, down_g)
+    if thin:
+        total = heads_sum.kept[0].astype(F32) + got[0].astype(F32)
+        high = 3 * qkv_rows // 4
+        qkv_g = unpacked(total[:high])
+        out_g, vecs = total[high : high + out_rows], total[high + out_rows :]
+    else:
+        qkv_g, out_g, vecs = end_heads(heads_sum.kept, got, qkv_rows, out_rows)
+    near_vecs = vecs + swap(vecs, 1)
+    near_vecs, seg_mine.kept = gate(near_vecs, seg_mine.kept)
+    segments_grad = spread(seg_mine.kept, seg_other.kept, mine, F32)
+    far_vecs, segments_grad = gate(swap(near_vecs, 2), segments_grad)
+    norm_vecs = near_vecs + far_vecs
 
     share = norm_gain.shape[0]
+    assert cols % share == 0
     assert up_bias.shape[0] == share
     norm_gain_g, norm_shift_g, bias_g, ffn_gain_g, ffn_shift_g = own_shares(
-        norm_vecs, ffn_vecs, here, share
+        norm_vecs, vecs, here, share
     )
     return (
         block_out,
         segments_grad,
         norm_gain_g,
         norm_shift_g,
-        qkv_g.reshape(qkv_weight.shape),
+        qkv_g,
         out_g,
         ffn_gain_g,
         ffn_shift_g,

time: 177 us -> 156 us (0.88)
  waiting for transfers between devices: 50.5 us -> 38.5 us
  local copies, waits for them, and re-layouts: 8.93 us -> 5.76 us
  Pallas kernels: 69.4 us -> 66.7 us
  starting transfers between devices: 42.7 us -> 40.8 us
    ppermute x24 -> x25, waiting for transfers between devices: 17.9 us -> 8.6 us  [swap(): lax.ppermute(value, 'tensor', [(t, t ^ bit) for t in range(lax.axis_size(...]
    another operation x15 -> x3, local copies, waits for them, and re-layouts: 3.89 us -> 0.76 us  [vector_rows(): jnp.stack(vectors + (jnp.zeros_like(vectors[0]),) * (8 - len(vectors)))]
    ppermute x19, waiting for transfers between devices: 32.6 us -> 29.9 us  [across(): lax.ppermute(value, 'dp', [(i, i ^ bit) for i in range(lax.axis_size('dp'...]
    pallas_call x2, Pallas kernels: 6.93 us -> 4.98 us  [spread(): pl.pallas_call(kernel, grid_spec=pltpu.PrefetchScalarGridSpec(num_scalar_...]
    ppermute x24 -> x25, starting transfers between devices: 14.9 us -> 13.2 us  [swap(): lax.ppermute(value, 'tensor', [(t, t ^ bit) for t in range(lax.axis_size(...]
    pallas_call x22 -> x23, Pallas kernels: 62.5 us -> 61.7 us  [call(): pl.pallas_call(kernel, grid=(1,), in_specs=inner, out_specs=[pl.BlockSpec...]
  transfers between devices with their start and end apart: 43 -> 44, of which waited for: 16 -> 19; matrix products, arithmetic and copies ran while one was open for 5% -> 4% of each run, Pallas kernels for 29% -> 32%
where the time goes in v3:
time: 156 us
  Pallas kernels  66.7 us (43%)
  starting transfers between devices  40.8 us (26%)
  waiting for transfers between devices  38.5 us (25%)
  local copies, waits for them, and re-layouts  5.76 us (4%)
  other arithmetic  3.08 us (2%)
    pallas_call x23, Pallas kernels, call(): pl.pallas_call(kernel, grid=(1,), in_specs=inner, out_specs=[pl.BlockSpec...  61.7 us
    ppermute x19, waiting for transfers between devices, across(): lax.ppermute(value, 'dp', [(i, i ^ bit) for i in range(lax.axis_size('dp'...  29.9 us
    ppermute x19, starting transfers between devices, across(): lax.ppermute(value, 'dp', [(i, i ^ bit) for i in range(lax.axis_size('dp'...  27.6 us
    ppermute x25, starting transfers between devices, swap(): lax.ppermute(value, 'tensor', [(t, t ^ bit) for t in range(lax.axis_size(...  13.2 us
    ppermute x25, waiting for transfers between devices, swap(): lax.ppermute(value, 'tensor', [(t, t ^ bit) for t in range(lax.axis_size(...  8.6 us
    pallas_call x2, Pallas kernels, spread(): pl.pallas_call(kernel, grid_spec=pltpu.PrefetchScalarGridSpec(num_scalar_...  4.98 us
  transfers between devices with their start and end apart: 44, of which 19 were waited for; matrix products, arithmetic and copies ran while one was open for 4% of the time, Pallas kernels for 32%

profile of v3, /device:TPU:0, one launch (start us, length us, event | category | flops | bytes accessed | tf_op | source)
XLA Modules:
  0.0 156.0 jit_solution(3813598503102015799)
XLA Ops:
  2.5 4.1 %collective-permute-start = (bf16[1,80,384]{2,1,0:T(8,128)(2,1)S(1)}, bf16[1,80,384]{2,1,0:T(8,128)(2,1)S(1)}, u32[]{:S(2)}, u32[]{:S(2)}) collective-permute-start(bf16[1,80,384]{2,1,0:T(8,128)(2,1)S(1)} %maximum_bitcast_fusion.1), channel_id=1, source_target_pairs={{0,16},{4,20},{8,24},{12,28},{16,0},{20,4},{24,8},{28,12},{1,17},{... | collective-permute-start | bytes 184328 | tf_op jit(solution)/shard_map/ppermute | solution.py:55
  6.8 2.9 %collective-permute-start.7 = (bf16[1,64,512]{2,1,0:T(8,128)(2,1)S(1)}, bf16[1,64,512]{2,1,0:T(8,128)(2,1)S(1)}, u32[]{:S(2)}, u32[]{:S(2)}) collective-permute-start(bf16[1,64,512]{2,1,0:T(8,128)(2,1)S(1)} %bitcast.30), channel_id=1, source_target_pairs={{0,16},{4,20},{8,24},{12,28},{16,0},{20,4},{24,8},{28,12},{1,17},{... | collective-permute-start | bytes 196616 | tf_op jit(solution)/shard_map/ppermute | solution.py:55
  10.6 3.4 %collective-permute-start.1 = (bf16[2,80,384]{2,1,0:T(8,128)(2,1)S(1)}, bf16[2,80,384]{2,1,0:T(8,128)(2,1)S(1)}, u32[]{:S(2)}, u32[]{:S(2)}) collective-permute-start(bf16[2,80,384]{2,1,0:T(8,128)(2,1)S(1)} %pad_maximum_fusion.5), channel_id=1, source_target_pairs={{0,8},{4,12},{8,0},{12,4},{16,24},{20,28},{24,16},{28,20},{1,9},{5... | collective-permute-start | bytes 368648 | tf_op jit(solution)/shard_map/ppermute | solution.py:55
  14.0 2.6 %collective-permute-done.7 = bf16[1,64,512]{2,1,0:T(8,128)(2,1)S(1)} collective-permute-done((bf16[1,64,512]{2,1,0:T(8,128)(2,1)S(1)}, bf16[1,64,512]{2,1,0:T(8,128)(2,1)S(1)}, u32[]{:S(2)}, u32[]{:S(2)}) %collective-permute-start.7) | collective-permute-done | bytes 65568 | tf_op jit(solution)/shard_map/ppermute | solution.py:55
  30.6 4.3 %attend_forward.4 = (bf16[384,768]{1,0:T(8,128)(2,1)S(1)}, bf16[128,768]{1,0:T(8,128)(2,1)S(1)}, bf16[704,128]{1,0:T(8,128)(2,1)S(1)}, f32[8,768]{1,0:T(8,128)S(1)}) custom-call(s32[1]{0:T(128)} %dynamic_slice.15.live_ref, bf16[512,768]{1,0:T(8,128)(2,1)S(1)} %get-tuple-element.137.xt_ref, bf16[528,384]{1,0:T(8,128)(2,1)S(1)} %get-tuple-element.136.w_ref, ...), custom_call_target="tpu_custom_call" | custom-call | flops 4400000000 | bytes 1982464 | tf_op jit(solution)/shard_map/attend_forward/pallas_call | solution.py:34
  36.1 3.7 %collective-permute-done.6.refs_1_ = bf16[4,80,512]{2,1,0:T(8,128)(2,1)S(1)} collective-permute-done((bf16[4,80,512]{2,1,0:T(8,128)(2,1)S(1)}, bf16[4,80,512]{2,1,0:T(8,128)(2,1)S(1)}, u32[]{:S(2)}, u32[]{:S(2)}) %collective-permute-start.6) | collective-permute-done | bytes 327712 | tf_op jit(solution)/shard_map/ppermute | solution.py:55
  43.0 4.3 %attend_forward.5 = (bf16[384,768]{1,0:T(8,128)(2,1)S(1)}, bf16[128,768]{1,0:T(8,128)(2,1)S(1)}, bf16[704,128]{1,0:T(8,128)(2,1)S(1)}, f32[8,768]{1,0:T(8,128)S(1)}) custom-call(s32[1]{0:T(128)} %dynamic_slice.15.live_ref, bf16[512,768]{1,0:T(8,128)(2,1)S(1)} %get-tuple-element.137.xt_ref, bf16[528,384]{1,0:T(8,128)(2,1)S(1)} %collective-permute-done.3.w_ref, ...), custom_call_target="tpu_custom_call" | custom-call | flops 4400000000 | bytes 1982464 | tf_op jit(solution)/shard_map/attend_forward/pallas_call | solution.py:34
  48.5 4.3 %attend_forward.6 = (bf16[384,768]{1,0:T(8,128)(2,1)S(1)}, bf16[128,768]{1,0:T(8,128)(2,1)S(1)}, bf16[704,128]{1,0:T(8,128)(2,1)S(1)}, f32[8,768]{1,0:T(8,128)S(1)}) custom-call(s32[1]{0:T(128)} %dynamic_slice.15.live_ref, bf16[512,768]{1,0:T(8,128)(2,1)S(1)} %get-tuple-element.137.xt_ref, bf16[528,384]{1,0:T(8,128)(2,1)S(1)} %collective-permute-done.10.w_ref, ...), custom_call_target="tpu_custom_call" | custom-call | flops 4400000000 | bytes 1982464 | tf_op jit(solution)/shard_map/attend_forward/pallas_call | solution.py:34
  52.8 4.3 %attend_forward.7 = (bf16[384,768]{1,0:T(8,128)(2,1)S(1)}, bf16[128,768]{1,0:T(8,128)(2,1)S(1)}, bf16[704,128]{1,0:T(8,128)(2,1)S(1)}, f32[8,768]{1,0:T(8,128)S(1)}) custom-call(s32[1]{0:T(128)} %dynamic_slice.15.live_ref, bf16[512,768]{1,0:T(8,128)(2,1)S(1)} %get-tuple-element.137.xt_ref, bf16[528,384]{1,0:T(8,128)(2,1)S(1)} %collective-permute-done.11.w_ref, ...), custom_call_target="tpu_custom_call" | custom-call | flops 4400000000 | bytes 1982464 | tf_op jit(solution)/shard_map/attend_forward/pallas_call | solution.py:34
  62.2 3.1 %feed_forward.4 = (f32[704,512]{1,0:T(8,128)S(1)}, f32[704,512]{1,0:T(8,128)S(1)}, bf16[1040,512]{1,0:T(8,128)(2,1)S(1)}) custom-call(bf16[704,512]{1,0:T(8,128)(2,1)S(1)} %get-tuple-element.159.x_ref, bf16[704,512]{1,0:T(8,128)(2,1)S(1)} %dynamic-slice_bitcast_fusion.cot_ref, bf16[1168,512]{1,0:T(8,128)(2,1)S(1)} %collective-permute-done.17.refs_7_.ud_ref), custom_call_target="tpu_custom_call" | custom-call | flops 3300000000 | bytes 7897088 | tf_op jit(solution)/shard_map/feed_forward/pallas_call | solution.py:34
  65.3 3.1 %feed_forward.5 = (f32[704,512]{1,0:T(8,128)S(1)}, f32[704,512]{1,0:T(8,128)S(1)}, bf16[1040,512]{1,0:T(8,128)(2,1)S(1)}) custom-call(bf16[704,512]{1,0:T(8,128)(2,1)S(1)} %get-tuple-element.159.x_ref, bf16[704,512]{1,0:T(8,128)(2,1)S(1)} %dynamic-slice_bitcast_fusion.cot_ref, bf16[1168,512]{1,0:T(8,128)(2,1)S(1)} %lay_out.3.refs_6_.ud_ref, ...), custom_call_target="tpu_custom_call" | custom-call | flops 3300000000 | bytes 7897088 | tf_op jit(solution)/shard_map/feed_forward/pallas_call | solution.py:34
  68.5 3.3 %feed_forward.6 = (f32[704,512]{1,0:T(8,128)S(1)}, f32[704,512]{1,0:T(8,128)S(1)}, bf16[1040,512]{1,0:T(8,128)(2,1)S(1)}) custom-call(bf16[704,512]{1,0:T(8,128)(2,1)S(1)} %get-tuple-element.159.x_ref, bf16[704,512]{1,0:T(8,128)(2,1)S(1)} %dynamic-slice_bitcast_fusion.cot_ref, bf16[1168,512]{1,0:T(8,128)(2,1)S(1)} %collective-permute-done.16.refs_5_.ud_ref, ...), custom_call_target="tpu_custom_call" | custom-call | flops 3300000000 | bytes 7897088 | tf_op jit(solution)/shard_map/feed_forward/pallas_call | solution.py:34
  72.4 3.1 %feed_forward.7 = (f32[704,512]{1,0:T(8,128)S(1)}, f32[704,512]{1,0:T(8,128)S(1)}, bf16[1040,512]{1,0:T(8,128)(2,1)S(1)}) custom-call(bf16[704,512]{1,0:T(8,128)(2,1)S(1)} %get-tuple-element.159.x_ref, bf16[704,512]{1,0:T(8,128)(2,1)S(1)} %dynamic-slice_bitcast_fusion.cot_ref, bf16[1168,512]{1,0:T(8,128)(2,1)S(1)} %lay_out.2.refs_4_.ud_ref, ...), custom_call_target="tpu_custom_call" | custom-call | flops 3300000000 | bytes 7897088 | tf_op jit(solution)/shard_map/feed_forward/pallas_call | solution.py:34
  77.8 2.9 %turn_back.1 = (bf16[704,512]{1,0:T(8,128)(2,1)S(1)}, f32[704,512]{1,0:T(8,128)S(1)}, bf16[144,512]{1,0:T(8,128)(2,1)S(1)}, bf16[144,512]{1,0:T(8,128)(2,1)S(1)}...) custom-call(f32[704,512]{1,0:T(8,128)S(1)} %get-tuple-element.174.re, ...), custom_call_target="tpu_custom_call" | custom-call | flops 550000000 | bytes 1500000 | tf_op jit(solution)/shard_map/turn_back/pallas_call | solution.py:34
  82.4 4.6 %attend_backward.4 = (f32[512,768]{1,0:T(8,128)S(1)}, bf16[512,384]{1,0:T(8,128)(2,1)S(1)}) custom-call(s32[1]{0:T(128)} %dynamic_slice.15.live_ref, bf16[512,768]{1,0:T(8,128)(2,1)S(1)} %get-tuple-element.137.xt_ref, bf16[528,384]{1,0:T(8,128)(2,1)S(1)} %collective-permute-done.11.w_ref, f32[32,768]{1,0:T(8,128)S(1)} %get-tuple-element.298.cos_ref, ...), custom_call_target="tpu_custom_call" | custom-call | flops 1100000000 | bytes 3000000 | tf_op jit(solution)/shard_map/attend_backward/pallas_call | solution.py:34
  87.5 7.6 %collective-permute-done.24 = bf16[8,64,512]{2,1,0:T(8,128)(2,1)S(1)} collective-permute-done((bf16[8,64,512]{2,1,0:T(8,128)(2,1)S(1)}, bf16[8,64,512]{2,1,0:T(8,128)(2,1)S(1)}, u32[]{:S(2)}, u32[]{:S(2)}) %collective-permute-start.24) | collective-permute-done | bytes 524320 | tf_op jit(solution)/shard_map/ppermute | solution.py:55
  96.7 3.1 %collective-permute-start.29 = (bf16[4,64,512]{2,1,0:T(8,128)(2,1)S(1)}, bf16[4,64,512]{2,1,0:T(8,128)(2,1)S(1)}, u32[]{:S(2)}, u32[]{:S(2)}) collective-permute-start(bf16[4,64,512]{2,1,0:T(8,128)(2,1)S(1)} %get-tuple-element.211), channel_id=1, source_target_pairs={{0,16},{4,20},{8,24},{12,28},{16,0},{20,4},{24,8},{28,12},{1,17},{... | collective-permute-start | bytes 786440 | tf_op jit(solution)/shard_map/ppermute | solution.py:55
  99.8 4.6 %attend_backward.5 = (f32[512,768]{1,0:T(8,128)S(1)}, bf16[512,384]{1,0:T(8,128)(2,1)S(1)}) custom-call(s32[1]{0:T(128)} %dynamic_slice.15.live_ref, bf16[512,768]{1,0:T(8,128)(2,1)S(1)} %get-tuple-element.137.xt_ref, bf16[528,384]{1,0:T(8,128)(2,1)S(1)} %collective-permute-done.10.w_ref, f32[32,768]{1,0:T(8,128)S(1)} %get-tuple-element.298.cos_ref, ...), custom_call_target="tpu_custom_call" | custom-call | flops 1100000000 | bytes 3000000 | tf_op jit(solution)/shard_map/attend_backward/pallas_call | solution.py:34
  105.5 4.8 %attend_backward.6 = (f32[512,768]{1,0:T(8,128)S(1)}, bf16[512,384]{1,0:T(8,128)(2,1)S(1)}) custom-call(s32[1]{0:T(128)} %dynamic_slice.15.live_ref, bf16[512,768]{1,0:T(8,128)(2,1)S(1)} %get-tuple-element.137.xt_ref, bf16[528,384]{1,0:T(8,128)(2,1)S(1)} %collective-permute-done.3.w_ref, f32[32,768]{1,0:T(8,128)S(1)} %get-tuple-element.298.cos_ref, ...), custom_call_target="tpu_custom_call" | custom-call | flops 1100000000 | bytes 3000000 | tf_op jit(solution)/shard_map/attend_backward/pallas_call | solution.py:34
  110.4 4.6 %attend_backward.7 = (f32[512,768]{1,0:T(8,128)S(1)}, bf16[512,384]{1,0:T(8,128)(2,1)S(1)}) custom-call(s32[1]{0:T(128)} %dynamic_slice.15.live_ref, bf16[512,768]{1,0:T(8,128)(2,1)S(1)} %get-tuple-element.137.xt_ref, bf16[528,384]{1,0:T(8,128)(2,1)S(1)} %get-tuple-element.136.w_ref, f32[32,768]{1,0:T(8,128)S(1)} %get-tuple-element.298.cos_ref, ...), custom_call_target="tpu_custom_call" | custom-call | flops 1100000000 | bytes 3000000 | tf_op jit(solution)/shard_map/attend_backward/pallas_call | solution.py:34
  125.8 3.2 %collective-permute-done.35 = bf16[2,64,512]{2,1,0:T(8,128)(2,1)S(1)} collective-permute-done((bf16[2,64,512]{2,1,0:T(8,128)(2,1)S(1)}, bf16[2,64,512]{2,1,0:T(8,128)(2,1)S(1)}, u32[]{:S(2)}, u32[]{:S(2)}) %collective-permute-start.35) | collective-permute-done | bytes 131104 | tf_op jit(solution)/shard_map/ppermute | solution.py:55
  136.4 2.8 %collective-permute-done.33.refs_2_ = bf16[704,512]{1,0:T(8,128)(2,1)S(1)} collective-permute-done((bf16[704,512]{1,0:T(8,128)(2,1)S(1)}, bf16[704,512]{1,0:T(8,128)(2,1)S(1)}, u32[]{:S(2)}, u32[]{:S(2)}) %collective-permute-start.33) | collective-permute-done | bytes 720928 | tf_op jit(solution)/shard_map/ppermute | solution.py:75
  142.1 5.2 %collective-permute-done.37.got_ref = bf16[1,80,512]{2,1,0:T(8,128)(2,1)S(1)} collective-permute-done((bf16[1,80,512]{2,1,0:T(8,128)(2,1)S(1)}, bf16[1,80,512]{2,1,0:T(8,128)(2,1)S(1)}, u32[]{:S(2)}, u32[]{:S(2)}) %collective-permute-start.37) | collective-permute-done | bytes 81952 | tf_op jit(solution)/shard_map/ppermute | solution.py:55
  151.3 2.9 %spread.3 = f32[4,704,512]{2,1,0:T(8,128)} custom-call(s32[1]{0:T(128)} %bitcast.index_ref, bf16[704,512]{1,0:T(8,128)(2,1)S(1)} %get-tuple-element.246.refs_0_, bf16[704,512]{1,0:T(8,128)(2,1)S(1)} %collective-permute-done.42.refs_1_, bf16[704,512]{1,0:T(8,128)(2,1)S(1)} %collective-permute-done.33.refs_2_, bf16[704,512]{1,0:T(8,128)(2,1)S(1)} %collective-permute-done.43.refs_3_), custom_call_target="tpu_custom_call" | custom-call | tf_op jit(solution)/shard_map/spread/pallas_call | solution.py:682
  (141 shorter events, 61.8 us)
Async XLA Ops:
  6.7 10.4 %collective-permute-start.4 = (bf16[1,80,512]{2,1,0:T(8,128)(2,1)S(1)}, bf16[1,80,512]{2,1,0:T(8,128)(2,1)S(1)}, u32[]{:S(2)}, u32[]{:S(2)}) collective-permute-start(bf16[1,80,512]{2,1,0:T(8,128)(2,1)S(1)} %maximum_bitcast_fusion), channel_id=1, source_target_pairs={{0,16},{4,20},{8,24},{12,28},{16,0},{20,4},{24,8},{28,12},{1,17},{... | collective-permute-start | bytes 245768 | tf_op jit(solution)/shard_map/ppermute | solution.py:55
  6.8 9.9 %collective-permute-start.7 = (bf16[1,64,512]{2,1,0:T(8,128)(2,1)S(1)}, bf16[1,64,512]{2,1,0:T(8,128)(2,1)S(1)}, u32[]{:S(2)}, u32[]{:S(2)}) collective-permute-start(bf16[1,64,512]{2,1,0:T(8,128)(2,1)S(1)} %bitcast.30), channel_id=1, source_target_pairs={{0,16},{4,20},{8,24},{12,28},{16,0},{20,4},{24,8},{28,12},{1,17},{... | collective-permute-start | bytes 196616 | tf_op jit(solution)/shard_map/ppermute | solution.py:55
  17.1 9.3 %collective-permute-start.5 = (bf16[2,80,512]{2,1,0:T(8,128)(2,1)S(1)}, bf16[2,80,512]{2,1,0:T(8,128)(2,1)S(1)}, u32[]{:S(2)}, u32[]{:S(2)}) collective-permute-start(bf16[2,80,512]{2,1,0:T(8,128)(2,1)S(1)} %pad_maximum_fusion.3), channel_id=1, source_target_pairs={{0,8},{4,12},{8,0},{12,4},{16,24},{20,28},{24,16},{28,20},{1,9},{5... | collective-permute-start | bytes 491528 | tf_op jit(solution)/shard_map/ppermute | solution.py:55
  19.2 9.5 %collective-permute-start.2 = (bf16[4,80,384]{2,1,0:T(8,128)(2,1)S(1)}, bf16[4,80,384]{2,1,0:T(8,128)(2,1)S(1)}, u32[]{:S(2)}, u32[]{:S(2)}) collective-permute-start(bf16[4,80,384]{2,1,0:T(8,128)(2,1)S(1)} %pad_maximum_fusion.2.refs_0_), channel_id=1, source_target_pairs={{0,4},{4,0},{8,12},{12,8},{16,20},{20,16},{24,28},{28,24},{1,5},{5... | collective-permute-start | bytes 737288 | tf_op jit(solution)/shard_map/ppermute | solution.py:55
  23.2 24.1 %collective-permute-start.9 = (bf16[4,64,512]{2,1,0:T(8,128)(2,1)S(1)}, bf16[4,64,512]{2,1,0:T(8,128)(2,1)S(1)}, u32[]{:S(2)}, u32[]{:S(2)}) collective-permute-start(bf16[4,64,512]{2,1,0:T(8,128)(2,1)S(1)} %pad_maximum_fusion.1.refs_2_), channel_id=1, source_target_pairs={{0,4},{4,0},{8,12},{12,8},{16,20},{20,16},{24,28},{28,24},{1,5},{5... | collective-permute-start | bytes 786440 | tf_op jit(solution)/shard_map/ppermute | solution.py:55
  24.9 10.0 %collective-permute-start.14 = (bf16[4,64,512]{2,1,0:T(8,128)(2,1)S(1)}, bf16[4,64,512]{2,1,0:T(8,128)(2,1)S(1)}, u32[]{:S(2)}, u32[]{:S(2)}) collective-permute-start(bf16[4,64,512]{2,1,0:T(8,128)(2,1)S(1)} %pad_maximum_fusion.1.refs_2_), channel_id=1, source_target_pairs={{0,2},{1,3},{2,0},{3,1},{4,6},{5,7},{6,4},{7,5},{8,10},{9,11},{10,... | collective-permute-start | bytes 786440 | tf_op jit(solution)/shard_map/ppermute | solution.py:75
  26.5 13.3 %collective-permute-start.6 = (bf16[4,80,512]{2,1,0:T(8,128)(2,1)S(1)}, bf16[4,80,512]{2,1,0:T(8,128)(2,1)S(1)}, u32[]{:S(2)}, u32[]{:S(2)}) collective-permute-start(bf16[4,80,512]{2,1,0:T(8,128)(2,1)S(1)} %pad_maximum_fusion.refs_0_), channel_id=1, source_target_pairs={{0,4},{4,0},{8,12},{12,8},{16,20},{20,16},{24,28},{28,24},{1,5},{5... | collective-permute-start | bytes 983048 | tf_op jit(solution)/shard_map/ppermute | solution.py:55
  27.2 29.9 %collective-permute-start.12 = (bf16[4,80,512]{2,1,0:T(8,128)(2,1)S(1)}, bf16[4,80,512]{2,1,0:T(8,128)(2,1)S(1)}, u32[]{:S(2)}, u32[]{:S(2)}) collective-permute-start(bf16[4,80,512]{2,1,0:T(8,128)(2,1)S(1)} %pad_maximum_fusion.refs_0_), channel_id=1, source_target_pairs={{0,2},{1,3},{2,0},{3,1},{4,6},{5,7},{6,4},{7,5},{8,10},{9,11},{10,... | collective-permute-start | bytes 983048 | tf_op jit(solution)/shard_map/ppermute | solution.py:75
  30.5 10.9 %collective-permute-start.3 = (bf16[528,384]{1,0:T(8,128)(2,1)S(1)}, bf16[528,384]{1,0:T(8,128)(2,1)S(1)}, u32[]{:S(2)}, u32[]{:S(2)}) collective-permute-start(bf16[528,384]{1,0:T(8,128)(2,1)S(1)} %get-tuple-element.136.w_ref), channel_id=1, source_target_pairs={{0,1},{1,0},{2,3},{3,2},{4,5},{5,4},{6,7},{7,6},{8,9},{9,8},{10,11... | collective-permute-start | bytes 1216520 | tf_op jit(solution)/shard_map/ppermute | solution.py:75
  34.9 13.1 %collective-permute-start.10 = (bf16[528,384]{1,0:T(8,128)(2,1)S(1)}, bf16[528,384]{1,0:T(8,128)(2,1)S(1)}, u32[]{:S(2)}, u32[]{:S(2)}) collective-permute-start(bf16[528,384]{1,0:T(8,128)(2,1)S(1)} %get-tuple-element.136.w_ref), channel_id=1, source_target_pairs={{0,2},{1,3},{2,0},{3,1},{4,6},{5,7},{6,4},{7,5},{8,10},{9,11},{10,... | collective-permute-start | bytes 1216520 | tf_op jit(solution)/shard_map/ppermute | solution.py:75
  39.8 17.4 %collective-permute-start.15 = (bf16[4,64,512]{2,1,0:T(8,128)(2,1)S(1)}, bf16[4,64,512]{2,1,0:T(8,128)(2,1)S(1)}, u32[]{:S(2)}, u32[]{:S(2)}) collective-permute-start(bf16[4,64,512]{2,1,0:T(8,128)(2,1)S(1)} %collective-permute-done.14.refs_2_), channel_id=1, source_target_pairs={{0,4},{4,0},{8,12},{12,8},{16,20},{20,16},{24,28},{28,24},{1,5},{5... | collective-permute-start | bytes 786440 | tf_op jit(solution)/shard_map/ppermute | solution.py:55
  41.5 15.7 %collective-permute-start.13 = (bf16[4,80,512]{2,1,0:T(8,128)(2,1)S(1)}, bf16[4,80,512]{2,1,0:T(8,128)(2,1)S(1)}, u32[]{:S(2)}, u32[]{:S(2)}) collective-permute-start(bf16[4,80,512]{2,1,0:T(8,128)(2,1)S(1)} %collective-permute-done.6.refs_1_), channel_id=1, source_target_pairs={{0,2},{1,3},{2,0},{3,1},{4,6},{5,7},{6,4},{7,5},{8,10},{9,11},{10,... | collective-permute-start | bytes 983048 | tf_op jit(solution)/shard_map/ppermute | solution.py:75
  47.9 11.2 %collective-permute-start.16 = (bf16[1168,512]{1,0:T(8,128)(2,1)S(1)}, bf16[1168,512]{1,0:T(8,128)(2,1)S(1)}, u32[]{:S(2)}, u32[]{:S(2)}) collective-permute-start(bf16[1168,512]{1,0:T(8,128)(2,1)S(1)} %lay_out.2.refs_4_.ud_ref), channel_id=1, source_target_pairs={{0,1},{1,0},{2,3},{3,2},{4,5},{5,4},{6,7},{7,6},{8,9},{9,8},{10,11... | collective-permute-start | bytes 3588104 | tf_op jit(solution)/shard_map/ppermute | solution.py:75
  80.8 14.2 %collective-permute-start.24 = (bf16[8,64,512]{2,1,0:T(8,128)(2,1)S(1)}, bf16[8,64,512]{2,1,0:T(8,128)(2,1)S(1)}, u32[]{:S(2)}, u32[]{:S(2)}) collective-permute-start(bf16[8,64,512]{2,1,0:T(8,128)(2,1)S(1)} %get-tuple-element.194), channel_id=1, source_target_pairs={{0,8},{4,12},{8,0},{12,4},{16,24},{20,28},{24,16},{28,20},{1,9},{5... | collective-permute-start | bytes 1572872 | tf_op jit(solution)/shard_map/ppermute | solution.py:55
  80.8 34.1 %collective-permute-start.21 = (bf16[704,512]{1,0:T(8,128)(2,1)S(1)}, bf16[704,512]{1,0:T(8,128)(2,1)S(1)}, u32[]{:S(2)}, u32[]{:S(2)}) collective-permute-start(bf16[704,512]{1,0:T(8,128)(2,1)S(1)} %get-tuple-element.181.refs_0_), channel_id=1, source_target_pairs={{0,2},{1,3},{2,0},{3,1},{4,6},{5,7},{6,4},{7,5},{8,10},{9,11},{10,... | collective-permute-start | bytes 2162696 | tf_op jit(solution)/shard_map/ppermute | solution.py:75
  82.2 41.5 %collective-permute-start.20 = (bf16[704,512]{1,0:T(8,128)(2,1)S(1)}, bf16[704,512]{1,0:T(8,128)(2,1)S(1)}, u32[]{:S(2)}, u32[]{:S(2)}) collective-permute-start(bf16[704,512]{1,0:T(8,128)(2,1)S(1)} %get-tuple-element.181.refs_0_), channel_id=1, source_target_pairs={{0,1},{1,0},{2,3},{3,2},{4,5},{5,4},{6,7},{7,6},{8,9},{9,8},{10,11... | collective-permute-start | bytes 2162696 | tf_op jit(solution)/shard_map/ppermute | solution.py:75
  82.2 14.3 %collective-permute-start.23 = (bf16[8,64,512]{2,1,0:T(8,128)(2,1)S(1)}, bf16[8,64,512]{2,1,0:T(8,128)(2,1)S(1)}, u32[]{:S(2)}, u32[]{:S(2)}) collective-permute-start(bf16[8,64,512]{2,1,0:T(8,128)(2,1)S(1)} %get-tuple-element.192), channel_id=1, source_target_pairs={{0,4},{4,0},{8,12},{12,8},{16,20},{20,16},{24,28},{28,24},{1,5},{5... | collective-permute-start | bytes 1572872 | tf_op jit(solution)/shard_map/ppermute | solution.py:55
  87.1 17.3 %collective-permute-start.25 = (bf16[512,384]{1,0:T(8,128)(2,1)S(1)}, bf16[512,384]{1,0:T(8,128)(2,1)S(1)}, u32[]{:S(2)}, u32[]{:S(2)}) collective-permute-start(bf16[512,384]{1,0:T(8,128)(2,1)S(1)} %get-tuple-element.201), channel_id=1, source_target_pairs={{0,1},{1,0},{2,3},{3,2},{4,5},{5,4},{6,7},{7,6},{8,9},{9,8},{10,11... | collective-permute-start | bytes 1179656 | tf_op jit(solution)/shard_map/ppermute | solution.py:75
  95.0 10.3 %collective-permute-start.27 = (bf16[144,512]{1,0:T(8,128)(2,1)S(1)}, bf16[144,512]{1,0:T(8,128)(2,1)S(1)}, u32[]{:S(2)}, u32[]{:S(2)}) collective-permute-start(bf16[144,512]{1,0:T(8,128)(2,1)S(1)} %add_convert_fusion.7), channel_id=1, source_target_pairs={{0,2},{1,3},{2,0},{3,1},{4,6},{5,7},{6,4},{7,5},{8,10},{9,11},{10,... | collective-permute-start | bytes 442376 | tf_op jit(solution)/shard_map/ppermute | solution.py:75
  96.7 18.4 %collective-permute-start.29 = (bf16[4,64,512]{2,1,0:T(8,128)(2,1)S(1)}, bf16[4,64,512]{2,1,0:T(8,128)(2,1)S(1)}, u32[]{:S(2)}, u32[]{:S(2)}) collective-permute-start(bf16[4,64,512]{2,1,0:T(8,128)(2,1)S(1)} %get-tuple-element.211), channel_id=1, source_target_pairs={{0,16},{4,20},{8,24},{12,28},{16,0},{20,4},{24,8},{28,12},{1,17},{... | collective-permute-start | bytes 786440 | tf_op jit(solution)/shard_map/ppermute | solution.py:55
  104.4 12.5 %collective-permute-start.28 = (bf16[4,64,512]{2,1,0:T(8,128)(2,1)S(1)}, bf16[4,64,512]{2,1,0:T(8,128)(2,1)S(1)}, u32[]{:S(2)}, u32[]{:S(2)}) collective-permute-start(bf16[4,64,512]{2,1,0:T(8,128)(2,1)S(1)} %get-tuple-element.209), channel_id=1, source_target_pairs={{0,8},{4,12},{8,0},{12,4},{16,24},{20,28},{24,16},{28,20},{1,9},{5... | collective-permute-start | bytes 786440 | tf_op jit(solution)/shard_map/ppermute | solution.py:55
  105.3 14.8 %collective-permute-start.32 = (bf16[512,384]{1,0:T(8,128)(2,1)S(1)}, bf16[512,384]{1,0:T(8,128)(2,1)S(1)}, u32[]{:S(2)}, u32[]{:S(2)}) collective-permute-start(bf16[512,384]{1,0:T(8,128)(2,1)S(1)} %add_convert_fusion), channel_id=1, source_target_pairs={{0,2},{1,3},{2,0},{3,1},{4,6},{5,7},{6,4},{7,5},{8,10},{9,11},{10,... | collective-permute-start | bytes 1179656 | tf_op jit(solution)/shard_map/ppermute | solution.py:75
  120.1 19.1 %collective-permute-start.33 = (bf16[704,512]{1,0:T(8,128)(2,1)S(1)}, bf16[704,512]{1,0:T(8,128)(2,1)S(1)}, u32[]{:S(2)}, u32[]{:S(2)}) collective-permute-start(bf16[704,512]{1,0:T(8,128)(2,1)S(1)} %get-tuple-element.246.refs_0_), channel_id=1, source_target_pairs={{0,2},{1,3},{2,0},{3,1},{4,6},{5,7},{6,4},{7,5},{8,10},{9,11},{10,... | collective-permute-start | bytes 2162696 | tf_op jit(solution)/shard_map/ppermute | solution.py:75
  132.3 9.1 %collective-permute-start.38 = (bf16[1,64,512]{2,1,0:T(8,128)(2,1)S(1)}, bf16[1,64,512]{2,1,0:T(8,128)(2,1)S(1)}, u32[]{:S(2)}, u32[]{:S(2)}) collective-permute-start(bf16[1,64,512]{2,1,0:T(8,128)(2,1)S(1)} %get-tuple-element.295), channel_id=1, source_target_pairs={{0,2},{1,3},{2,0},{3,1},{4,6},{5,7},{6,4},{7,5},{8,10},{9,11},{10,... | collective-permute-start | bytes 196616 | tf_op jit(solution)/shard_map/ppermute | solution.py:75
  (28 other events, 164.2 us)

commit v4 on v3

--- a/solution.py
+++ b/solution.py
@@ -94,7 +94,7 @@
         got, *kept = gate(move(self.sent, bit), *(e.kept for e in earlier))
         for e, k in zip(earlier, kept):
             e.kept = k
-        if self.steps:
+        if self.kept.shape[0] > 1:
             half = self.kept.shape[0] // 2
             parts = [slice(None, half), slice(half, None)]
             self.kept, self.sent = (
@@ -448,6 +448,20 @@
     )
 
 
+def end_ffn(up_kept, down_kept, got):
+    def kernel(up_ref, down_ref, got_ref, up_out, down_out):
+        up_out[...] = up_ref[0].astype(F32) + got_ref[0].astype(F32)
+        down_out[...] = down_ref[0].astype(F32) + got_ref[1].astype(F32)
+
+    return call(
+        kernel,
+        (up_kept, down_kept, got),
+        [(up_kept.shape[1:], F32), (down_kept.shape[1:], F32)],
+        name="end_ffn",
+        us=0.3,
+    )
+
+
 def cut_ffn(grads, up_order, down_order, rows):
     height, width = grads[0].shape
     count = up_order.shape[0]
@@ -689,6 +703,7 @@
         ),
         out_shape=jax.ShapeDtypeStruct((len(parts), rows, width), dtype),
         compiler_params=pltpu.CompilerParams(vmem_limit_bytes=24 * 1024 * 1024),
+        cost_estimate=pl.CostEstimate(flops=1000, bytes_accessed=1000, transcendentals=0),
         name="spread",
     )(jnp.reshape(tensor_index, (1,)).astype(jnp.int32), *parts)
 
@@ -855,8 +870,8 @@
     else:
         up_halves, down_halves = cut_ffn(ups, ahead, down_ahead, up_rows)
     res, up_halves, down_halves = lax.optimization_barrier((res, up_halves, down_halves))
-    up = Halving(up_halves, [(across, b) for b in up_bits] + [(swap, 2)])
-    down = Halving(down_halves, [(across, b) for b in down_bits] + [(swap, 2)])
+    up = Halving(up_halves, [(across, b) for b in up_bits])
+    down = Halving(down_halves, [(across, b) for b in down_bits])
     turned = turn_back(
         res, *acc, cot, vec, [h[1] for h in heads], wides, ffn_grads, padded
     )
@@ -908,17 +923,16 @@
     block_out, down.kept = gate(block_out, down.kept)
     up.step(down)
     heads_sum.step(up)
+    both = swap(jnp.concatenate([up.sent, down.sent]), 2)
     while len(heads_sum.steps) > 1:
         heads_sum.step()
     seg_other.kept, heads_sum.kept, heads_sum.sent = gate(
         seg_other.kept, heads_sum.kept, heads_sum.sent
     )
-    while up.steps:
-        up.step(seg_other)
-        down.step(up)
-    up_g, down_g = up.kept, down.kept
     got = across(heads_sum.sent, heads_sum.steps[0][1])
-    got, up_g, down_g = gate(got, up_g, down_g)
+    segments_grad = spread(seg_mine.kept, seg_other.kept, mine, F32)
+    got, segments_grad = gate(got, segments_grad)
+    up_g, down_g = end_ffn(up.kept, down.kept, both)
     if thin:
         total = heads_sum.kept[0].astype(F32) + got[0].astype(F32)
         high = 3 * qkv_rows // 4
@@ -927,9 +941,7 @@
     else:
         qkv_g, out_g, vecs = end_heads(heads_sum.kept, got, qkv_rows, out_rows)
     near_vecs = vecs + swap(vecs, 1)
-    near_vecs, seg_mine.kept = gate(near_vecs, seg_mine.kept)
-    segments_grad = spread(seg_mine.kept, seg_other.kept, mine, F32)
-    far_vecs, segments_grad = gate(swap(near_vecs, 2), segments_grad)
+    far_vecs, up_g, down_g = gate(swap(near_vecs, 2), up_g, down_g)
     norm_vecs = near_vecs + far_vecs
 
     share = norm_gain.shape[0]

time: 156 us -> 153 us (0.981)
  waiting for transfers between devices: 38.5 us -> 35 us
    ppermute x25 -> x24, waiting for transfers between devices: 8.6 us -> 6.74 us  [swap(): lax.ppermute(value, 'tensor', [(t, t ^ bit) for t in range(lax.axis_size(...]
    ppermute x19, waiting for transfers between devices: 29.9 us -> 28.3 us  [across(): lax.ppermute(value, 'dp', [(i, i ^ bit) for i in range(lax.axis_size('dp'...]
    pallas_call x23 -> x24, Pallas kernels: 61.7 us -> 62.4 us  [call(): pl.pallas_call(kernel, grid=(1,), in_specs=inner, out_specs=[pl.BlockSpec...]
    ppermute x25 -> x24, starting transfers between devices: 13.2 us -> 12.9 us  [swap(): lax.ppermute(value, 'tensor', [(t, t ^ bit) for t in range(lax.axis_size(...]
  transfers between devices with their start and end apart: 44 -> 43, of which waited for: 19 -> 17; matrix products, arithmetic and copies ran while one was open for 4% -> 3% of each run, Pallas kernels for 32% -> 34%
where the time goes in v4:
time: 153 us
  Pallas kernels  67.4 us (44%)
  starting transfers between devices  41.5 us (27%)
  waiting for transfers between devices  35 us (23%)
  local copies, waits for them, and re-layouts  5.76 us (4%)
  other arithmetic  1.75 us (1%)
    pallas_call x24, Pallas kernels, call(): pl.pallas_call(kernel, grid=(1,), in_specs=inner, out_specs=[pl.BlockSpec...  62.4 us
    ppermute x19, starting transfers between devices, across(): lax.ppermute(value, 'dp', [(i, i ^ bit) for i in range(lax.axis_size('dp'...  28.6 us
    ppermute x19, waiting for transfers between devices, across(): lax.ppermute(value, 'dp', [(i, i ^ bit) for i in range(lax.axis_size('dp'...  28.3 us
    ppermute x24, starting transfers between devices, swap(): lax.ppermute(value, 'tensor', [(t, t ^ bit) for t in range(lax.axis_size(...  12.9 us
    ppermute x24, waiting for transfers between devices, swap(): lax.ppermute(value, 'tensor', [(t, t ^ bit) for t in range(lax.axis_size(...  6.74 us
    pallas_call x2, Pallas kernels, spread(): pl.pallas_call(kernel, grid_spec=pltpu.PrefetchScalarGridSpec(num_scalar_...  4.98 us
  transfers between devices with their start and end apart: 43, of which 17 were waited for; matrix products, arithmetic and copies ran while one was open for 3% of the time, Pallas kernels for 34%

profile of v4, /device:TPU:0, one launch (start us, length us, event | category | flops | bytes accessed | tf_op | source)
XLA Modules:
  0.0 152.6 jit_solution(11415263924815009829)
XLA Ops:
  2.5 4.1 %collective-permute-start = (bf16[1,80,384]{2,1,0:T(8,128)(2,1)S(1)}, bf16[1,80,384]{2,1,0:T(8,128)(2,1)S(1)}, u32[]{:S(2)}, u32[]{:S(2)}) collective-permute-start(bf16[1,80,384]{2,1,0:T(8,128)(2,1)S(1)} %maximum_bitcast_fusion.1), channel_id=1, source_target_pairs={{0,16},{4,20},{8,24},{12,28},{16,0},{20,4},{24,8},{28,12},{1,17},{... | collective-permute-start | bytes 184328 | tf_op jit(solution)/shard_map/ppermute | solution.py:55
  6.8 2.9 %collective-permute-start.7 = (bf16[1,64,512]{2,1,0:T(8,128)(2,1)S(1)}, bf16[1,64,512]{2,1,0:T(8,128)(2,1)S(1)}, u32[]{:S(2)}, u32[]{:S(2)}) collective-permute-start(bf16[1,64,512]{2,1,0:T(8,128)(2,1)S(1)} %bitcast.26), channel_id=1, source_target_pairs={{0,16},{4,20},{8,24},{12,28},{16,0},{20,4},{24,8},{28,12},{1,17},{... | collective-permute-start | bytes 196616 | tf_op jit(solution)/shard_map/ppermute | solution.py:55
  10.6 3.4 %collective-permute-start.1 = (bf16[2,80,384]{2,1,0:T(8,128)(2,1)S(1)}, bf16[2,80,384]{2,1,0:T(8,128)(2,1)S(1)}, u32[]{:S(2)}, u32[]{:S(2)}) collective-permute-start(bf16[2,80,384]{2,1,0:T(8,128)(2,1)S(1)} %pad_maximum_fusion.6), channel_id=1, source_target_pairs={{0,8},{4,12},{8,0},{12,4},{16,24},{20,28},{24,16},{28,20},{1,9},{5... | collective-permute-start | bytes 368648 | tf_op jit(solution)/shard_map/ppermute | solution.py:55
  14.0 2.6 %collective-permute-done.7 = bf16[1,64,512]{2,1,0:T(8,128)(2,1)S(1)} collective-permute-done((bf16[1,64,512]{2,1,0:T(8,128)(2,1)S(1)}, bf16[1,64,512]{2,1,0:T(8,128)(2,1)S(1)}, u32[]{:S(2)}, u32[]{:S(2)}) %collective-permute-start.7) | collective-permute-done | bytes 65568 | tf_op jit(solution)/shard_map/ppermute | solution.py:55
  30.6 4.3 %attend_forward.4 = (bf16[384,768]{1,0:T(8,128)(2,1)S(1)}, bf16[128,768]{1,0:T(8,128)(2,1)S(1)}, bf16[704,128]{1,0:T(8,128)(2,1)S(1)}, f32[8,768]{1,0:T(8,128)S(1)}) custom-call(s32[1]{0:T(128)} %dynamic_slice.15.live_ref, bf16[512,768]{1,0:T(8,128)(2,1)S(1)} %get-tuple-element.133.xt_ref, bf16[528,384]{1,0:T(8,128)(2,1)S(1)} %get-tuple-element.132.w_ref, ...), custom_call_target="tpu_custom_call" | custom-call | flops 4400000000 | bytes 1982464 | tf_op jit(solution)/shard_map/attend_forward/pallas_call | solution.py:34
  36.1 3.7 %collective-permute-done.6.refs_1_ = bf16[4,80,512]{2,1,0:T(8,128)(2,1)S(1)} collective-permute-done((bf16[4,80,512]{2,1,0:T(8,128)(2,1)S(1)}, bf16[4,80,512]{2,1,0:T(8,128)(2,1)S(1)}, u32[]{:S(2)}, u32[]{:S(2)}) %collective-permute-start.6) | collective-permute-done | bytes 327712 | tf_op jit(solution)/shard_map/ppermute | solution.py:55
  43.0 4.3 %attend_forward.5 = (bf16[384,768]{1,0:T(8,128)(2,1)S(1)}, bf16[128,768]{1,0:T(8,128)(2,1)S(1)}, bf16[704,128]{1,0:T(8,128)(2,1)S(1)}, f32[8,768]{1,0:T(8,128)S(1)}) custom-call(s32[1]{0:T(128)} %dynamic_slice.15.live_ref, bf16[512,768]{1,0:T(8,128)(2,1)S(1)} %get-tuple-element.133.xt_ref, bf16[528,384]{1,0:T(8,128)(2,1)S(1)} %collective-permute-done.3.w_ref, ...), custom_call_target="tpu_custom_call" | custom-call | flops 4400000000 | bytes 1982464 | tf_op jit(solution)/shard_map/attend_forward/pallas_call | solution.py:34
  48.5 4.3 %attend_forward.6 = (bf16[384,768]{1,0:T(8,128)(2,1)S(1)}, bf16[128,768]{1,0:T(8,128)(2,1)S(1)}, bf16[704,128]{1,0:T(8,128)(2,1)S(1)}, f32[8,768]{1,0:T(8,128)S(1)}) custom-call(s32[1]{0:T(128)} %dynamic_slice.15.live_ref, bf16[512,768]{1,0:T(8,128)(2,1)S(1)} %get-tuple-element.133.xt_ref, bf16[528,384]{1,0:T(8,128)(2,1)S(1)} %collective-permute-done.10.w_ref, ...), custom_call_target="tpu_custom_call" | custom-call | flops 4400000000 | bytes 1982464 | tf_op jit(solution)/shard_map/attend_forward/pallas_call | solution.py:34
  52.8 4.3 %attend_forward.7 = (bf16[384,768]{1,0:T(8,128)(2,1)S(1)}, bf16[128,768]{1,0:T(8,128)(2,1)S(1)}, bf16[704,128]{1,0:T(8,128)(2,1)S(1)}, f32[8,768]{1,0:T(8,128)S(1)}) custom-call(s32[1]{0:T(128)} %dynamic_slice.15.live_ref, bf16[512,768]{1,0:T(8,128)(2,1)S(1)} %get-tuple-element.133.xt_ref, bf16[528,384]{1,0:T(8,128)(2,1)S(1)} %collective-permute-done.11.w_ref, ...), custom_call_target="tpu_custom_call" | custom-call | flops 4400000000 | bytes 1982464 | tf_op jit(solution)/shard_map/attend_forward/pallas_call | solution.py:34
  62.2 3.1 %feed_forward.4 = (f32[704,512]{1,0:T(8,128)S(1)}, f32[704,512]{1,0:T(8,128)S(1)}, bf16[1040,512]{1,0:T(8,128)(2,1)S(1)}) custom-call(bf16[704,512]{1,0:T(8,128)(2,1)S(1)} %get-tuple-element.155.x_ref, bf16[704,512]{1,0:T(8,128)(2,1)S(1)} %dynamic-slice_bitcast_fusion.cot_ref, bf16[1168,512]{1,0:T(8,128)(2,1)S(1)} %collective-permute-done.17.refs_7_.ud_ref), custom_call_target="tpu_custom_call" | custom-call | flops 3300000000 | bytes 7897088 | tf_op jit(solution)/shard_map/feed_forward/pallas_call | solution.py:34
  65.3 3.1 %feed_forward.5 = (f32[704,512]{1,0:T(8,128)S(1)}, f32[704,512]{1,0:T(8,128)S(1)}, bf16[1040,512]{1,0:T(8,128)(2,1)S(1)}) custom-call(bf16[704,512]{1,0:T(8,128)(2,1)S(1)} %get-tuple-element.155.x_ref, bf16[704,512]{1,0:T(8,128)(2,1)S(1)} %dynamic-slice_bitcast_fusion.cot_ref, bf16[1168,512]{1,0:T(8,128)(2,1)S(1)} %lay_out.3.refs_6_.ud_ref, ...), custom_call_target="tpu_custom_call" | custom-call | flops 3300000000 | bytes 7897088 | tf_op jit(solution)/shard_map/feed_forward/pallas_call | solution.py:34
  68.5 3.3 %feed_forward.6 = (f32[704,512]{1,0:T(8,128)S(1)}, f32[704,512]{1,0:T(8,128)S(1)}, bf16[1040,512]{1,0:T(8,128)(2,1)S(1)}) custom-call(bf16[704,512]{1,0:T(8,128)(2,1)S(1)} %get-tuple-element.155.x_ref, bf16[704,512]{1,0:T(8,128)(2,1)S(1)} %dynamic-slice_bitcast_fusion.cot_ref, bf16[1168,512]{1,0:T(8,128)(2,1)S(1)} %collective-permute-done.16.refs_5_.ud_ref, ...), custom_call_target="tpu_custom_call" | custom-call | flops 3300000000 | bytes 7897088 | tf_op jit(solution)/shard_map/feed_forward/pallas_call | solution.py:34
  72.4 3.1 %feed_forward.7 = (f32[704,512]{1,0:T(8,128)S(1)}, f32[704,512]{1,0:T(8,128)S(1)}, bf16[1040,512]{1,0:T(8,128)(2,1)S(1)}) custom-call(bf16[704,512]{1,0:T(8,128)(2,1)S(1)} %get-tuple-element.155.x_ref, bf16[704,512]{1,0:T(8,128)(2,1)S(1)} %dynamic-slice_bitcast_fusion.cot_ref, bf16[1168,512]{1,0:T(8,128)(2,1)S(1)} %lay_out.2.refs_4_.ud_ref, ...), custom_call_target="tpu_custom_call" | custom-call | flops 3300000000 | bytes 7897088 | tf_op jit(solution)/shard_map/feed_forward/pallas_call | solution.py:34
  77.8 2.9 %turn_back.1 = (bf16[704,512]{1,0:T(8,128)(2,1)S(1)}, f32[704,512]{1,0:T(8,128)S(1)}, bf16[144,512]{1,0:T(8,128)(2,1)S(1)}, bf16[144,512]{1,0:T(8,128)(2,1)S(1)}...) custom-call(f32[704,512]{1,0:T(8,128)S(1)} %get-tuple-element.170.re, ...), custom_call_target="tpu_custom_call" | custom-call | flops 550000000 | bytes 1500000 | tf_op jit(solution)/shard_map/turn_back/pallas_call | solution.py:34
  82.4 4.6 %attend_backward.4 = (f32[512,768]{1,0:T(8,128)S(1)}, bf16[512,384]{1,0:T(8,128)(2,1)S(1)}) custom-call(s32[1]{0:T(128)} %dynamic_slice.15.live_ref, bf16[512,768]{1,0:T(8,128)(2,1)S(1)} %get-tuple-element.133.xt_ref, bf16[528,384]{1,0:T(8,128)(2,1)S(1)} %collective-permute-done.11.w_ref, f32[32,768]{1,0:T(8,128)S(1)} %get-tuple-element.290.cos_ref, ...), custom_call_target="tpu_custom_call" | custom-call | flops 1100000000 | bytes 3000000 | tf_op jit(solution)/shard_map/attend_backward/pallas_call | solution.py:34
  87.5 7.6 %collective-permute-done.24 = bf16[8,64,512]{2,1,0:T(8,128)(2,1)S(1)} collective-permute-done((bf16[8,64,512]{2,1,0:T(8,128)(2,1)S(1)}, bf16[8,64,512]{2,1,0:T(8,128)(2,1)S(1)}, u32[]{:S(2)}, u32[]{:S(2)}) %collective-permute-start.24) | collective-permute-done | bytes 524320 | tf_op jit(solution)/shard_map/ppermute | solution.py:55
  96.7 3.1 %collective-permute-start.29 = (bf16[4,64,512]{2,1,0:T(8,128)(2,1)S(1)}, bf16[4,64,512]{2,1,0:T(8,128)(2,1)S(1)}, u32[]{:S(2)}, u32[]{:S(2)}) collective-permute-start(bf16[4,64,512]{2,1,0:T(8,128)(2,1)S(1)} %get-tuple-element.207), channel_id=1, source_target_pairs={{0,16},{4,20},{8,24},{12,28},{16,0},{20,4},{24,8},{28,12},{1,17},{... | collective-permute-start | bytes 786440 | tf_op jit(solution)/shard_map/ppermute | solution.py:55
  99.8 4.6 %attend_backward.5 = (f32[512,768]{1,0:T(8,128)S(1)}, bf16[512,384]{1,0:T(8,128)(2,1)S(1)}) custom-call(s32[1]{0:T(128)} %dynamic_slice.15.live_ref, bf16[512,768]{1,0:T(8,128)(2,1)S(1)} %get-tuple-element.133.xt_ref, bf16[528,384]{1,0:T(8,128)(2,1)S(1)} %collective-permute-done.10.w_ref, f32[32,768]{1,0:T(8,128)S(1)} %get-tuple-element.290.cos_ref, ...), custom_call_target="tpu_custom_call" | custom-call | flops 1100000000 | bytes 3000000 | tf_op jit(solution)/shard_map/attend_backward/pallas_call | solution.py:34
  105.5 4.8 %attend_backward.6 = (f32[512,768]{1,0:T(8,128)S(1)}, bf16[512,384]{1,0:T(8,128)(2,1)S(1)}) custom-call(s32[1]{0:T(128)} %dynamic_slice.15.live_ref, bf16[512,768]{1,0:T(8,128)(2,1)S(1)} %get-tuple-element.133.xt_ref, bf16[528,384]{1,0:T(8,128)(2,1)S(1)} %collective-permute-done.3.w_ref, f32[32,768]{1,0:T(8,128)S(1)} %get-tuple-element.290.cos_ref, ...), custom_call_target="tpu_custom_call" | custom-call | flops 1100000000 | bytes 3000000 | tf_op jit(solution)/shard_map/attend_backward/pallas_call | solution.py:34
  110.4 4.6 %attend_backward.7 = (f32[512,768]{1,0:T(8,128)S(1)}, bf16[512,384]{1,0:T(8,128)(2,1)S(1)}) custom-call(s32[1]{0:T(128)} %dynamic_slice.15.live_ref, bf16[512,768]{1,0:T(8,128)(2,1)S(1)} %get-tuple-element.133.xt_ref, bf16[528,384]{1,0:T(8,128)(2,1)S(1)} %get-tuple-element.132.w_ref, f32[32,768]{1,0:T(8,128)S(1)} %get-tuple-element.290.cos_ref, ...), custom_call_target="tpu_custom_call" | custom-call | flops 1100000000 | bytes 3000000 | tf_op jit(solution)/shard_map/attend_backward/pallas_call | solution.py:34
  123.7 2.1 %spread.2 = bf16[4,704,512]{2,1,0:T(8,128)(2,1)} custom-call(s32[1]{0:T(128)} %bitcast.index_ref, bf16[704,512]{1,0:T(8,128)(2,1)S(1)} %get-tuple-element.177.refs_0_, bf16[704,512]{1,0:T(8,128)(2,1)S(1)} %collective-permute-done.20.refs_1_, bf16[704,512]{1,0:T(8,128)(2,1)S(1)} %collective-permute-done.21.refs_2_, ...), custom_call_target="tpu_custom_call" | custom-call | flops 1000 | bytes 1000 | tf_op jit(solution)/shard_map/spread/pallas_call | solution.py:696
  125.8 3.2 %collective-permute-done.35 = bf16[2,64,512]{2,1,0:T(8,128)(2,1)S(1)} collective-permute-done((bf16[2,64,512]{2,1,0:T(8,128)(2,1)S(1)}, bf16[2,64,512]{2,1,0:T(8,128)(2,1)S(1)}, u32[]{:S(2)}, u32[]{:S(2)}) %collective-permute-start.35) | collective-permute-done | bytes 131104 | tf_op jit(solution)/shard_map/ppermute | solution.py:55
  132.3 4.1 %collective-permute-done.36 = bf16[2,80,512]{2,1,0:T(8,128)(2,1)S(1)} collective-permute-done((bf16[2,80,512]{2,1,0:T(8,128)(2,1)S(1)}, bf16[2,80,512]{2,1,0:T(8,128)(2,1)S(1)}, u32[]{:S(2)}, u32[]{:S(2)}) %collective-permute-start.36) | collective-permute-done | bytes 163872 | tf_op jit(solution)/shard_map/ppermute | solution.py:55
  140.7 2.9 %spread.3 = f32[4,704,512]{2,1,0:T(8,128)} custom-call(s32[1]{0:T(128)} %bitcast.index_ref, bf16[704,512]{1,0:T(8,128)(2,1)S(1)} %get-tuple-element.231.refs_0_, bf16[704,512]{1,0:T(8,128)(2,1)S(1)} %collective-permute-done.38.refs_1_, bf16[704,512]{1,0:T(8,128)(2,1)S(1)} %collective-permute-done.33.refs_2_, bf16[704,512]{1,0:T(8,128)(2,1)S(1)} %collective-permute-done.39.refs_3_), custom_call_target="tpu_custom_call" | custom-call | flops 1000 | bytes 1000 | tf_op jit(solution)/shard_map/spread/pallas_call | solution.py:696
  (139 shorter events, 60.2 us)
Async XLA Ops:
  6.7 10.4 %collective-permute-start.4 = (bf16[1,80,512]{2,1,0:T(8,128)(2,1)S(1)}, bf16[1,80,512]{2,1,0:T(8,128)(2,1)S(1)}, u32[]{:S(2)}, u32[]{:S(2)}) collective-permute-start(bf16[1,80,512]{2,1,0:T(8,128)(2,1)S(1)} %maximum_bitcast_fusion), channel_id=1, source_target_pairs={{0,16},{4,20},{8,24},{12,28},{16,0},{20,4},{24,8},{28,12},{1,17},{... | collective-permute-start | bytes 245768 | tf_op jit(solution)/shard_map/ppermute | solution.py:55
  6.8 9.9 %collective-permute-start.7 = (bf16[1,64,512]{2,1,0:T(8,128)(2,1)S(1)}, bf16[1,64,512]{2,1,0:T(8,128)(2,1)S(1)}, u32[]{:S(2)}, u32[]{:S(2)}) collective-permute-start(bf16[1,64,512]{2,1,0:T(8,128)(2,1)S(1)} %bitcast.26), channel_id=1, source_target_pairs={{0,16},{4,20},{8,24},{12,28},{16,0},{20,4},{24,8},{28,12},{1,17},{... | collective-permute-start | bytes 196616 | tf_op jit(solution)/shard_map/ppermute | solution.py:55
  17.1 9.3 %collective-permute-start.5 = (bf16[2,80,512]{2,1,0:T(8,128)(2,1)S(1)}, bf16[2,80,512]{2,1,0:T(8,128)(2,1)S(1)}, u32[]{:S(2)}, u32[]{:S(2)}) collective-permute-start(bf16[2,80,512]{2,1,0:T(8,128)(2,1)S(1)} %pad_maximum_fusion.3), channel_id=1, source_target_pairs={{0,8},{4,12},{8,0},{12,4},{16,24},{20,28},{24,16},{28,20},{1,9},{5... | collective-permute-start | bytes 491528 | tf_op jit(solution)/shard_map/ppermute | solution.py:55
  19.2 9.5 %collective-permute-start.2 = (bf16[4,80,384]{2,1,0:T(8,128)(2,1)S(1)}, bf16[4,80,384]{2,1,0:T(8,128)(2,1)S(1)}, u32[]{:S(2)}, u32[]{:S(2)}) collective-permute-start(bf16[4,80,384]{2,1,0:T(8,128)(2,1)S(1)} %pad_maximum_fusion.2.refs_0_), channel_id=1, source_target_pairs={{0,4},{4,0},{8,12},{12,8},{16,20},{20,16},{24,28},{28,24},{1,5},{5... | collective-permute-start | bytes 737288 | tf_op jit(solution)/shard_map/ppermute | solution.py:55
  23.2 24.1 %collective-permute-start.9 = (bf16[4,64,512]{2,1,0:T(8,128)(2,1)S(1)}, bf16[4,64,512]{2,1,0:T(8,128)(2,1)S(1)}, u32[]{:S(2)}, u32[]{:S(2)}) collective-permute-start(bf16[4,64,512]{2,1,0:T(8,128)(2,1)S(1)} %pad_maximum_fusion.1.refs_2_), channel_id=1, source_target_pairs={{0,4},{4,0},{8,12},{12,8},{16,20},{20,16},{24,28},{28,24},{1,5},{5... | collective-permute-start | bytes 786440 | tf_op jit(solution)/shard_map/ppermute | solution.py:55
  24.9 10.0 %collective-permute-start.14 = (bf16[4,64,512]{2,1,0:T(8,128)(2,1)S(1)}, bf16[4,64,512]{2,1,0:T(8,128)(2,1)S(1)}, u32[]{:S(2)}, u32[]{:S(2)}) collective-permute-start(bf16[4,64,512]{2,1,0:T(8,128)(2,1)S(1)} %pad_maximum_fusion.1.refs_2_), channel_id=1, source_target_pairs={{0,2},{1,3},{2,0},{3,1},{4,6},{5,7},{6,4},{7,5},{8,10},{9,11},{10,... | collective-permute-start | bytes 786440 | tf_op jit(solution)/shard_map/ppermute | solution.py:75
  26.5 13.3 %collective-permute-start.6 = (bf16[4,80,512]{2,1,0:T(8,128)(2,1)S(1)}, bf16[4,80,512]{2,1,0:T(8,128)(2,1)S(1)}, u32[]{:S(2)}, u32[]{:S(2)}) collective-permute-start(bf16[4,80,512]{2,1,0:T(8,128)(2,1)S(1)} %pad_maximum_fusion.refs_0_), channel_id=1, source_target_pairs={{0,4},{4,0},{8,12},{12,8},{16,20},{20,16},{24,28},{28,24},{1,5},{5... | collective-permute-start | bytes 983048 | tf_op jit(solution)/shard_map/ppermute | solution.py:55
  27.2 29.9 %collective-permute-start.12 = (bf16[4,80,512]{2,1,0:T(8,128)(2,1)S(1)}, bf16[4,80,512]{2,1,0:T(8,128)(2,1)S(1)}, u32[]{:S(2)}, u32[]{:S(2)}) collective-permute-start(bf16[4,80,512]{2,1,0:T(8,128)(2,1)S(1)} %pad_maximum_fusion.refs_0_), channel_id=1, source_target_pairs={{0,2},{1,3},{2,0},{3,1},{4,6},{5,7},{6,4},{7,5},{8,10},{9,11},{10,... | collective-permute-start | bytes 983048 | tf_op jit(solution)/shard_map/ppermute | solution.py:75
  30.5 10.9 %collective-permute-start.3 = (bf16[528,384]{1,0:T(8,128)(2,1)S(1)}, bf16[528,384]{1,0:T(8,128)(2,1)S(1)}, u32[]{:S(2)}, u32[]{:S(2)}) collective-permute-start(bf16[528,384]{1,0:T(8,128)(2,1)S(1)} %get-tuple-element.132.w_ref), channel_id=1, source_target_pairs={{0,1},{1,0},{2,3},{3,2},{4,5},{5,4},{6,7},{7,6},{8,9},{9,8},{10,11... | collective-permute-start | bytes 1216520 | tf_op jit(solution)/shard_map/ppermute | solution.py:75
  34.9 13.1 %collective-permute-start.10 = (bf16[528,384]{1,0:T(8,128)(2,1)S(1)}, bf16[528,384]{1,0:T(8,128)(2,1)S(1)}, u32[]{:S(2)}, u32[]{:S(2)}) collective-permute-start(bf16[528,384]{1,0:T(8,128)(2,1)S(1)} %get-tuple-element.132.w_ref), channel_id=1, source_target_pairs={{0,2},{1,3},{2,0},{3,1},{4,6},{5,7},{6,4},{7,5},{8,10},{9,11},{10,... | collective-permute-start | bytes 1216520 | tf_op jit(solution)/shard_map/ppermute | solution.py:75
  39.8 17.4 %collective-permute-start.15 = (bf16[4,64,512]{2,1,0:T(8,128)(2,1)S(1)}, bf16[4,64,512]{2,1,0:T(8,128)(2,1)S(1)}, u32[]{:S(2)}, u32[]{:S(2)}) collective-permute-start(bf16[4,64,512]{2,1,0:T(8,128)(2,1)S(1)} %collective-permute-done.14.refs_2_), channel_id=1, source_target_pairs={{0,4},{4,0},{8,12},{12,8},{16,20},{20,16},{24,28},{28,24},{1,5},{5... | collective-permute-start | bytes 786440 | tf_op jit(solution)/shard_map/ppermute | solution.py:55
  41.5 15.7 %collective-permute-start.13 = (bf16[4,80,512]{2,1,0:T(8,128)(2,1)S(1)}, bf16[4,80,512]{2,1,0:T(8,128)(2,1)S(1)}, u32[]{:S(2)}, u32[]{:S(2)}) collective-permute-start(bf16[4,80,512]{2,1,0:T(8,128)(2,1)S(1)} %collective-permute-done.6.refs_1_), channel_id=1, source_target_pairs={{0,2},{1,3},{2,0},{3,1},{4,6},{5,7},{6,4},{7,5},{8,10},{9,11},{10,... | collective-permute-start | bytes 983048 | tf_op jit(solution)/shard_map/ppermute | solution.py:75
  47.9 11.2 %collective-permute-start.16 = (bf16[1168,512]{1,0:T(8,128)(2,1)S(1)}, bf16[1168,512]{1,0:T(8,128)(2,1)S(1)}, u32[]{:S(2)}, u32[]{:S(2)}) collective-permute-start(bf16[1168,512]{1,0:T(8,128)(2,1)S(1)} %lay_out.2.refs_4_.ud_ref), channel_id=1, source_target_pairs={{0,1},{1,0},{2,3},{3,2},{4,5},{5,4},{6,7},{7,6},{8,9},{9,8},{10,11... | collective-permute-start | bytes 3588104 | tf_op jit(solution)/shard_map/ppermute | solution.py:75
  80.8 14.2 %collective-permute-start.24 = (bf16[8,64,512]{2,1,0:T(8,128)(2,1)S(1)}, bf16[8,64,512]{2,1,0:T(8,128)(2,1)S(1)}, u32[]{:S(2)}, u32[]{:S(2)}) collective-permute-start(bf16[8,64,512]{2,1,0:T(8,128)(2,1)S(1)} %get-tuple-element.190), channel_id=1, source_target_pairs={{0,8},{4,12},{8,0},{12,4},{16,24},{20,28},{24,16},{28,20},{1,9},{5... | collective-permute-start | bytes 1572872 | tf_op jit(solution)/shard_map/ppermute | solution.py:55
  80.8 34.1 %collective-permute-start.21 = (bf16[704,512]{1,0:T(8,128)(2,1)S(1)}, bf16[704,512]{1,0:T(8,128)(2,1)S(1)}, u32[]{:S(2)}, u32[]{:S(2)}) collective-permute-start(bf16[704,512]{1,0:T(8,128)(2,1)S(1)} %get-tuple-element.177.refs_0_), channel_id=1, source_target_pairs={{0,2},{1,3},{2,0},{3,1},{4,6},{5,7},{6,4},{7,5},{8,10},{9,11},{10,... | collective-permute-start | bytes 2162696 | tf_op jit(solution)/shard_map/ppermute | solution.py:75
  82.2 41.5 %collective-permute-start.20 = (bf16[704,512]{1,0:T(8,128)(2,1)S(1)}, bf16[704,512]{1,0:T(8,128)(2,1)S(1)}, u32[]{:S(2)}, u32[]{:S(2)}) collective-permute-start(bf16[704,512]{1,0:T(8,128)(2,1)S(1)} %get-tuple-element.177.refs_0_), channel_id=1, source_target_pairs={{0,1},{1,0},{2,3},{3,2},{4,5},{5,4},{6,7},{7,6},{8,9},{9,8},{10,11... | collective-permute-start | bytes 2162696 | tf_op jit(solution)/shard_map/ppermute | solution.py:75
  82.2 14.3 %collective-permute-start.23 = (bf16[8,64,512]{2,1,0:T(8,128)(2,1)S(1)}, bf16[8,64,512]{2,1,0:T(8,128)(2,1)S(1)}, u32[]{:S(2)}, u32[]{:S(2)}) collective-permute-start(bf16[8,64,512]{2,1,0:T(8,128)(2,1)S(1)} %get-tuple-element.188), channel_id=1, source_target_pairs={{0,4},{4,0},{8,12},{12,8},{16,20},{20,16},{24,28},{28,24},{1,5},{5... | collective-permute-start | bytes 1572872 | tf_op jit(solution)/shard_map/ppermute | solution.py:55
  87.1 17.3 %collective-permute-start.25 = (bf16[512,384]{1,0:T(8,128)(2,1)S(1)}, bf16[512,384]{1,0:T(8,128)(2,1)S(1)}, u32[]{:S(2)}, u32[]{:S(2)}) collective-permute-start(bf16[512,384]{1,0:T(8,128)(2,1)S(1)} %get-tuple-element.197), channel_id=1, source_target_pairs={{0,1},{1,0},{2,3},{3,2},{4,5},{5,4},{6,7},{7,6},{8,9},{9,8},{10,11... | collective-permute-start | bytes 1179656 | tf_op jit(solution)/shard_map/ppermute | solution.py:75
  95.0 10.3 %collective-permute-start.27 = (bf16[144,512]{1,0:T(8,128)(2,1)S(1)}, bf16[144,512]{1,0:T(8,128)(2,1)S(1)}, u32[]{:S(2)}, u32[]{:S(2)}) collective-permute-start(bf16[144,512]{1,0:T(8,128)(2,1)S(1)} %add_convert_fusion.7), channel_id=1, source_target_pairs={{0,2},{1,3},{2,0},{3,1},{4,6},{5,7},{6,4},{7,5},{8,10},{9,11},{10,... | collective-permute-start | bytes 442376 | tf_op jit(solution)/shard_map/ppermute | solution.py:75
  96.7 18.4 %collective-permute-start.29 = (bf16[4,64,512]{2,1,0:T(8,128)(2,1)S(1)}, bf16[4,64,512]{2,1,0:T(8,128)(2,1)S(1)}, u32[]{:S(2)}, u32[]{:S(2)}) collective-permute-start(bf16[4,64,512]{2,1,0:T(8,128)(2,1)S(1)} %get-tuple-element.207), channel_id=1, source_target_pairs={{0,16},{4,20},{8,24},{12,28},{16,0},{20,4},{24,8},{28,12},{1,17},{... | collective-permute-start | bytes 786440 | tf_op jit(solution)/shard_map/ppermute | solution.py:55
  104.4 12.5 %collective-permute-start.28 = (bf16[4,64,512]{2,1,0:T(8,128)(2,1)S(1)}, bf16[4,64,512]{2,1,0:T(8,128)(2,1)S(1)}, u32[]{:S(2)}, u32[]{:S(2)}) collective-permute-start(bf16[4,64,512]{2,1,0:T(8,128)(2,1)S(1)} %get-tuple-element.205), channel_id=1, source_target_pairs={{0,8},{4,12},{8,0},{12,4},{16,24},{20,28},{24,16},{28,20},{1,9},{5... | collective-permute-start | bytes 786440 | tf_op jit(solution)/shard_map/ppermute | solution.py:55
  105.3 14.8 %collective-permute-start.32 = (bf16[512,384]{1,0:T(8,128)(2,1)S(1)}, bf16[512,384]{1,0:T(8,128)(2,1)S(1)}, u32[]{:S(2)}, u32[]{:S(2)}) collective-permute-start(bf16[512,384]{1,0:T(8,128)(2,1)S(1)} %add_convert_fusion), channel_id=1, source_target_pairs={{0,2},{1,3},{2,0},{3,1},{4,6},{5,7},{6,4},{7,5},{8,10},{9,11},{10,... | collective-permute-start | bytes 1179656 | tf_op jit(solution)/shard_map/ppermute | solution.py:75
  120.1 17.8 %collective-permute-start.33 = (bf16[704,512]{1,0:T(8,128)(2,1)S(1)}, bf16[704,512]{1,0:T(8,128)(2,1)S(1)}, u32[]{:S(2)}, u32[]{:S(2)}) collective-permute-start(bf16[704,512]{1,0:T(8,128)(2,1)S(1)} %get-tuple-element.231.refs_0_), channel_id=1, source_target_pairs={{0,2},{1,3},{2,0},{3,1},{4,6},{5,7},{6,4},{7,5},{8,10},{9,11},{10,... | collective-permute-start | bytes 2162696 | tf_op jit(solution)/shard_map/ppermute | solution.py:75
  120.2 8.9 %collective-permute-start.35 = (bf16[2,64,512]{2,1,0:T(8,128)(2,1)S(1)}, bf16[2,64,512]{2,1,0:T(8,128)(2,1)S(1)}, u32[]{:S(2)}, u32[]{:S(2)}) collective-permute-start(bf16[2,64,512]{2,1,0:T(8,128)(2,1)S(1)} %get-tuple-element.226), channel_id=1, source_target_pairs={{0,16},{4,20},{8,24},{12,28},{16,0},{20,4},{24,8},{28,12},{1,17},{... | collective-permute-start | bytes 393224 | tf_op jit(solution)/shard_map/ppermute | solution.py:55
  (27 other events, 163.6 us)
